TPU v7x, 128 devices: a whole 4x4x4 slice. The times are simulated.
128 devices in a mesh: band: 16 (over y, z), grid: 8 (over x, core).
Axes of the slice: x: 4, y: 4, z: 4, core: 2. Of those that a mesh axis runs over, the one named last changes fastest.
Arguments:
- x_initial: float32 [640, 3, 256, 256], P(('band', 'grid')), may hold values from -0.1 to 1, as said below
- sp2_choices: int32 [4], replicated, may hold values from 0 to 1, as said below
- domain_blocks: int32 [384, 5], replicated, may hold values from -1 to 639, as said below
- basis_values: bfloat16 [384, 768, 1280], P(('band', 'grid')), may hold values from -0.25 to 0.25
Outputs:
- density: float32 [640, 3, 256, 256], P(('band', 'grid'))
- hamiltonian: float32 [640, 3, 256, 256], P(('band', 'grid'))
- potential: float32 [384, 768], P(('band', 'grid'))
Inputs may be any that keep to these rules, and one draw needn't show every extreme that they name: Lower block form of a symmetric matrix: each x_initial[I, 2] is symmetric, and the blocks x_initial[I, q] with I - 2 + q < 0 are zero. `domain_blocks`: domain rows are grouped by device in the order of the joined axes band then grid, 3 rows a device. A row lists 2 to 5 consecutive block numbers followed by -1 entries. All blocks of a domain are block rows of one device with the same grid index whose band index differs from the domain's device by at most 2; the domains of one device lie on different devices. Every device has a domain of 5 blocks. `sp2_choices`: not all steps apply the same polynomial.
All inputs are finite; a program needn't handle non-finite values.
Results may differ from a plain program's by a relative error of at most 0.0017.
The roundings to bfloat16 on the way count: a program that leaves them out, or rounds other values in their place, can miss the bound.
Values may be sent and summed in bfloat16 or wider, within the bound.
No kernel may reach another device: no remote copies, remote signals or barrier semaphores. Data moves between devices by JAX's collectives and lax.ppermute only.
A program may use at most 128 MiB of HBM per device.

v0:
```python
import functools

import jax
import jax.numpy as jnp
from jax import lax
from jax.experimental import pallas as pl
from jax.experimental.pallas import tpu as pltpu
from jax.sharding import PartitionSpec as P


DBLK = 5
ITERS = 4
BS = 256
TILE = 256
SLOT_MOVES = (0, 1, -1, 2, -2)
OWN_PLACE, STARTS, COUNTS, MOVES, TABLE = 0, 1, 6, 11, 16

NN = (((1,), (0,)), ((), ()))
NT = (((1,), (1,)), ((), ()))
TN = (((0,), (0,)), ((), ()))


def passed_along(x, axis, by):
    count = lax.axis_size(axis)
    pairs = [(i, i + by) for i in range(count) if 0 <= i + by < count]
    return lax.ppermute(x, axis, pairs)


def dot32(a, b, dims):
    return lax.dot_general(a, b, dims, preferred_element_type=jnp.float32)


def square_kernel(choice_ref, x_ref, narrow_ref, top_ref, bottom_ref, x_out, narrow_out, ext):
    rows = narrow_ref.shape[0]
    row = pl.program_id(0)

    @pl.when(row == 0)
    def _():
        ext[0, 2] = top_ref[0]
        ext[1, 1] = top_ref[1]
        ext[1, 2] = top_ref[2]
        ext[rows + 2, 0] = bottom_ref[0]
        ext[rows + 2, 1] = bottom_ref[1]
        ext[rows + 3, 0] = bottom_ref[2]
        for r in range(rows):
            ext[r + 2] = narrow_ref[r]

    i = row + 2

    def blk(r, q):
        return ext[r, q]

    here = [blk(i, q) for q in range(3)]
    up1, up0 = blk(i - 1, 1), blk(i - 1, 2)
    upup = blk(i - 2, 2)
    dn1, dn0 = blk(i + 1, 1), blk(i + 1, 0)
    dd = blk(i + 2, 0)
    diag = (
        dot32(here[0], here[0], NT)
        + dot32(here[1], here[1], NT)
        + dot32(here[2], here[2], NT)
        + dot32(dn1, dn1, TN)
        + dot32(dd, dd, TN)
    )
    near = (
        dot32(here[0], up1, NT)
        + dot32(here[1], up0, NN)
        + dot32(here[2], here[1], NN)
        + dot32(dn1, dn0, TN)
    )
    far = dot32(here[0], upup, NN) + dot32(here[1], up1, NN) + dot32(here[2], here[0], NN)
    twice = choice_ref[0] == 1
    for q, squared in ((0, far), (1, near), (2, diag)):
        new = jnp.where(twice, 2.0 * x_ref[0, q] - squared, squared)
        x_out[0, q] = new
        narrow_out[0, q] = new.astype(jnp.bfloat16)


def square_step(choice, x, narrow, top, bottom):
    rows = x.shape[0]
    per_row = pl.BlockSpec((1, 3, BS, BS), lambda r: (r, 0, 0, 0))
    whole = pl.BlockSpec(memory_space=pltpu.VMEM)
    return pl.pallas_call(
        square_kernel,
        grid=(rows,),
        in_specs=[pl.BlockSpec(memory_space=pltpu.SMEM), per_row, whole, whole, whole],
        out_specs=[per_row, per_row],
        out_shape=[
            pltpu.HBM(x.shape, jnp.float32),
            jax.ShapeDtypeStruct(x.shape, jnp.bfloat16),
        ],
        scratch_shapes=[pltpu.VMEM((rows + 4, 3, BS, BS), jnp.bfloat16)],
        compiler_params=pltpu.CompilerParams(vmem_limit_bytes=24 << 20),
        cost_estimate=pl.CostEstimate(
            flops=rows * 12 * 2 * BS**3, bytes_accessed=x.size * 12, transcendentals=0
        ),
        name="square_step",
    )(choice, pltpu.with_memory_space_constraint(x, pltpu.HBM), narrow, top, bottom)


def plan_kernel(moves, geometry, blocks_ref, basis_ref, *refs):
    *outs, table_ref, buf, in_sems, out_sems = refs
    rows, band_count, grid_count = geometry
    local = basis_ref.shape[0]
    band = lax.axis_index("band")
    grid = lax.axis_index("grid")
    device = band * grid_count + grid
    own_moves = []
    for d in range(local):
        first = blocks_ref[0, device * local + d]
        own_moves.append(first // (rows * grid_count) - band)

    def place_of(move):
        place = jnp.int32(0)
        for d in range(local):
            place = jnp.where(own_moves[d] == move, d, place)
        return place

    for n, move in enumerate(moves):
        pltpu.make_async_copy(basis_ref.at[place_of(move)], buf.at[n], in_sems.at[n]).start()
    table_ref[OWN_PLACE] = place_of(0)
    for slot, move in enumerate(SLOT_MOVES):
        source = band - move
        live = (source >= 0) & (source < band_count)
        source = jnp.clip(source, 0, band_count - 1) * grid_count + grid
        start = jnp.int32(0)
        count = jnp.int32(0)
        for d in range(local):
            first = blocks_ref[0, source * local + d]
            match = live & (first // rows == device)
            blocks = jnp.int32(0)
            for k in range(DBLK):
                blocks += jnp.where(blocks_ref[k, source * local + d] >= 0, 1, 0)
            start = jnp.where(match, first - device * rows, start)
            count = jnp.where(match, blocks, count)
        table_ref[STARTS + slot] = start
        table_ref[COUNTS + slot] = count
    for d in range(local):
        table_ref[MOVES + d] = own_moves[d]
    for n, move in enumerate(moves):
        pltpu.make_async_copy(basis_ref.at[place_of(move)], buf.at[n], in_sems.at[n]).wait()
        pltpu.make_async_copy(buf.at[n], outs[n], out_sems.at[n]).start()
    for n, move in enumerate(moves):
        pltpu.make_async_copy(buf.at[n], outs[n], out_sems.at[n]).wait()


def plan_step(moves, blocks, basis, rows, band_count, grid_count):
    any_space = pl.BlockSpec(memory_space=pl.ANY)
    smem = pl.BlockSpec(memory_space=pltpu.SMEM)
    one = jax.ShapeDtypeStruct(basis.shape[1:], basis.dtype)
    return pl.pallas_call(
        functools.partial(plan_kernel, moves, (rows, band_count, grid_count)),
        in_specs=[smem, pl.BlockSpec(memory_space=pltpu.HBM)],
        out_specs=[any_space] * len(moves) + [smem],
        out_shape=[one] * len(moves) + [jax.ShapeDtypeStruct((TABLE,), jnp.int32)],
        scratch_shapes=[
            pltpu.VMEM((len(moves),) + basis.shape[1:], basis.dtype),
            pltpu.SemaphoreType.DMA((len(moves),)),
            pltpu.SemaphoreType.DMA((len(moves),)),
        ],
        compiler_params=pltpu.CompilerParams(vmem_limit_bytes=16 << 20),
        name="plan_step",
    )(blocks, basis)


def pick_kernel(moves, cuts, table_ref, basis_ref, *refs):
    *outs, buf, in_sems, out_sems = refs
    local = basis_ref.shape[0]

    def place_of(move):
        place = jnp.int32(0)
        for d in range(local):
            place = jnp.where(table_ref[MOVES + d] == move, d, place)
        return place

    def load(n):
        return pltpu.make_async_copy(basis_ref.at[place_of(moves[n])], buf.at[n], in_sems.at[n])

    def stores(n):
        return [
            pltpu.make_async_copy(
                buf.at[n, pl.ds(low, high - low)],
                outs[n * len(cuts) + c],
                out_sems.at[n * len(cuts) + c],
            )
            for c, (low, high) in enumerate(cuts)
        ]

    for n in range(len(moves)):
        load(n).start()
    for n in range(len(moves)):
        load(n).wait()
        for copy in stores(n):
            copy.start()
    for n in range(len(moves)):
        for copy in stores(n):
            copy.wait()


def pick_step(moves, cuts, table, basis):
    any_space = pl.BlockSpec(memory_space=pl.ANY)
    smem = pl.BlockSpec(memory_space=pltpu.SMEM)
    width = basis.shape[2]
    outs = [jax.ShapeDtypeStruct((high - low, width), basis.dtype) for low, high in cuts]
    return pl.pallas_call(
        functools.partial(pick_kernel, moves, cuts),
        in_specs=[smem, pl.BlockSpec(memory_space=pltpu.HBM)],
        out_specs=[any_space] * (len(moves) * len(cuts)),
        out_shape=outs * len(moves),
        scratch_shapes=[
            pltpu.VMEM((len(moves),) + basis.shape[1:], basis.dtype),
            pltpu.SemaphoreType.DMA((len(moves),)),
            pltpu.SemaphoreType.DMA((len(moves) * len(cuts),)),
        ],
        compiler_params=pltpu.CompilerParams(vmem_limit_bytes=16 << 20),
        name="pick_step",
    )(table, basis)


def fill_stack(tile_ref, stack):
    rows = tile_ref.shape[0]
    for r in range(rows):
        stack[r, 0:BS] = tile_ref[r, 2]
        for gap in (1, 2):
            where = pl.ds(gap * BS, BS)
            if r + gap < rows:
                stack[r, where] = tile_ref[r + gap, 2 - gap] * 2
            else:
                stack[r, where] = jnp.zeros((BS, BS), jnp.bfloat16)


def blank_tail(phi, slot, blocks):
    for k in range(2, DBLK):

        @pl.when(k >= blocks)
        def _():
            phi[slot, :, k * BS : (k + 1) * BS] = jnp.zeros((phi.shape[1], BS), jnp.bfloat16)


def potential_of_slot(phi, slot, first, stack, pot_out, psi_at, factor):
    points = phi.shape[1]
    rows = stack.shape[0]

    @pl.loop(0, points // TILE)
    def _(step):
        here = pl.ds(pl.multiple_of(step * TILE, TILE), TILE)
        total = jnp.zeros((TILE, BS), jnp.float32)
        for j in range(DBLK):
            last = min(j + 3, DBLK)
            row = jnp.minimum(first + j, rows - 1)
            applied = dot32(phi[slot, here, j * BS : last * BS], stack[row, 0 : (last - j) * BS], NN)
            total += applied * phi[slot, here, j * BS : (j + 1) * BS].astype(jnp.float32)
        potential = jnp.tanh(jnp.sum(total, axis=1, keepdims=True))
        spread = jnp.transpose(jnp.broadcast_to(potential, (TILE, 128)))
        pot_out[slot, :, here] = spread[0:1]
        scale = factor * potential
        psi_at(here)[...] = (scale * phi[slot, here, :].astype(jnp.float32)).astype(jnp.bfloat16)


def add_blocks(ham, psi, phi, slot, first, blocks):
    for k in range(DBLK):

        @pl.when(k < blocks)
        def _():
            low = max(0, k - 2)
            piece = dot32(psi[:, k * BS : (k + 1) * BS], phi[slot, :, low * BS : (k + 1) * BS], TN)
            for j in range(low, k + 1):
                ham[first + k, 2 - (k - j)] += piece[:, (j - low) * BS : (j - low + 1) * BS]


def domain_kernel(slots, has_base, factor, table_ref, tile_ref, *refs):
    refs = list(refs)
    base_ref = refs.pop(0) if has_base else None
    basis_refs = [refs.pop(0) for _ in slots]
    ham_out, pot_out, phi, psi, stack, ham, sems, base_sem = refs

    def fetch(n):
        source = basis_refs[n]
        if len(source.shape) == 3:
            source = source.at[table_ref[OWN_PLACE]]
        return pltpu.make_async_copy(source, phi.at[n], sems.at[n])

    for n in range(len(slots)):
        fetch(n).start()
    if has_base:
        base = pltpu.make_async_copy(base_ref, ham, base_sem)
        base.start()
    else:
        ham[...] = jnp.zeros_like(ham)
    fill_stack(tile_ref, stack)
    pot_out[...] = jnp.zeros_like(pot_out)
    for n in range(len(slots)):
        fetch(n).wait()
    if has_base:
        base.wait()

    @pl.loop(0, len(slots))
    def _(n):
        first = table_ref[STARTS + slots[0] + n]
        blocks = table_ref[COUNTS + slots[0] + n]

        @pl.when(blocks > 0)
        def _():
            blank_tail(phi, n, blocks)
            potential_of_slot(phi, n, first, stack, pot_out, lambda here: psi.at[here], factor)
            add_blocks(ham, psi, phi, n, first, blocks)

    result = pltpu.make_async_copy(ham, ham_out, base_sem)
    result.start()
    result.wait()


def domain_step(slots, table, tiles, base, arrays, factor):
    rows = tiles.shape[0]
    points, width = arrays[-1].shape[-2:]
    number = len(arrays)
    has_base = base is not None
    smem = pl.BlockSpec(memory_space=pltpu.SMEM)
    vmem = pl.BlockSpec(memory_space=pltpu.VMEM)
    hbm = pl.BlockSpec(memory_space=pl.ANY)
    operands = [table, tiles] + ([base] if has_base else []) + list(arrays)
    return pl.pallas_call(
        functools.partial(domain_kernel, slots, has_base, factor),
        in_specs=[smem, vmem]
        + [pl.BlockSpec(memory_space=pltpu.HBM) if o.ndim >= 3 else hbm for o in operands[2:]],
        out_specs=[pl.BlockSpec(memory_space=pltpu.HBM), vmem],
        out_shape=[
            pltpu.HBM((rows, 3, BS, BS), jnp.float32),
            jax.ShapeDtypeStruct((number, 1, points), jnp.float32),
        ],
        scratch_shapes=[
            pltpu.VMEM((number, points, width), jnp.bfloat16),
            pltpu.VMEM((points, width), jnp.bfloat16),
            pltpu.VMEM((rows, 3 * BS, BS), jnp.bfloat16),
            pltpu.VMEM((rows, 3, BS, BS), jnp.float32),
            pltpu.SemaphoreType.DMA((number,)),
            pltpu.SemaphoreType.DMA,
        ],
        compiler_params=pltpu.CompilerParams(vmem_limit_bytes=36 << 20),
        cost_estimate=pl.CostEstimate(
            flops=number * 24 * 2 * points * BS * BS,
            bytes_accessed=number * points * width * 2 + rows * 3 * BS * BS * 6,
            transcendentals=number * points,
        ),
        name="domain_step",
    )(*operands)


def potential_kernel(slots, factor, table_ref, tile_ref, *refs):
    basis_refs = refs[: len(slots)]
    psi_out, pot_out, phi, stack = refs[len(slots) :]
    fill_stack(tile_ref, stack)
    pot_out[...] = jnp.zeros_like(pot_out)
    for n in range(len(slots)):
        phi[n] = basis_refs[n][...]

    @pl.loop(0, len(slots))
    def _(n):
        first = table_ref[STARTS + slots[0] + n]
        blocks = table_ref[COUNTS + slots[0] + n]

        @pl.when(blocks > 0)
        def _():
            blank_tail(phi, n, blocks)
            potential_of_slot(phi, n, first, stack, pot_out, lambda here: psi_out.at[n, here], factor)


def potential_step(slots, table, tiles, arrays, factor):
    rows = tiles.shape[0]
    points, width = arrays[-1].shape
    number = len(arrays)
    smem = pl.BlockSpec(memory_space=pltpu.SMEM)
    vmem = pl.BlockSpec(memory_space=pltpu.VMEM)
    hbm = pl.BlockSpec(memory_space=pl.ANY)
    return pl.pallas_call(
        functools.partial(potential_kernel, slots, factor),
        in_specs=[smem, vmem] + [vmem] * number,
        out_specs=[vmem, vmem],
        out_shape=[
            jax.ShapeDtypeStruct((number, points, width), jnp.bfloat16),
            jax.ShapeDtypeStruct((number, 1, points), jnp.float32),
        ],
        scratch_shapes=[
            pltpu.VMEM((number, points, width), jnp.bfloat16),
            pltpu.VMEM((rows, 3 * BS, BS), jnp.bfloat16),
        ],
        compiler_params=pltpu.CompilerParams(vmem_limit_bytes=16 << 20),
        cost_estimate=pl.CostEstimate(
            flops=number * 12 * 2 * points * BS * BS,
            bytes_accessed=number * points * width * 4,
            transcendentals=number * points,
        ),
        name="potential_step",
    )(table, tiles, *arrays)


def block_kernel(slots, table_ref, psi_ref, base_ref, *refs):
    basis_refs = refs[: len(slots)]
    ham_out, ham, sems = refs[len(slots) :]
    rows = ham.shape[0]

    def send(r):
        return pltpu.make_async_copy(ham.at[r], ham_out.at[r], sems.at[r])

    for r in range(rows):
        ham[r] = base_ref[r]
        for n, slot in enumerate(slots):
            k = r - table_ref[STARTS + slot]
            blocks = table_ref[COUNTS + slot]

            @pl.when((k >= 0) & (k < blocks))
            def _():
                left = psi_ref[n, :, pl.ds(pl.multiple_of(k * BS, BS), BS)]
                for gap in range(3):

                    @pl.when(k >= gap)
                    def _():
                        where = pl.ds(pl.multiple_of((k - gap) * BS, BS), BS)
                        ham[r, 2 - gap] += dot32(left, basis_refs[n][:, where], TN)

        send(r).start()
    for r in range(rows):
        send(r).wait()


def block_step(slots, table, psi, base, arrays):
    number, points, width = psi.shape
    rows = base.shape[0]
    smem = pl.BlockSpec(memory_space=pltpu.SMEM)
    vmem = pl.BlockSpec(memory_space=pltpu.VMEM)
    return pl.pallas_call(
        functools.partial(block_kernel, slots),
        in_specs=[smem, vmem, vmem] + [vmem] * number,
        out_specs=pl.BlockSpec(memory_space=pltpu.HBM),
        out_shape=pltpu.HBM(base.shape, jnp.float32),
        scratch_shapes=[
            pltpu.VMEM(base.shape, jnp.float32),
            pltpu.SemaphoreType.DMA((rows,)),
        ],
        compiler_params=pltpu.CompilerParams(vmem_limit_bytes=20 << 20),
        cost_estimate=pl.CostEstimate(
            flops=number * 12 * 2 * points * BS * BS,
            bytes_accessed=number * points * width * 4 + base.size * 8,
            transcendentals=0,
        ),
        name="block_step",
    )(table, psi, base, *arrays)


def whole_step(x_initial, sp2_choices, domain_blocks, basis_values):
    row_count = x_initial.shape[0]
    band_count = lax.axis_size("band")
    grid_count = lax.axis_size("grid")
    local_domains, points, width = basis_values.shape
    factor = width / points
    cuts = ((0, 512), (512, points))

    def orbitals(value, move):
        return passed_along(value, "band", move)

    basis_values = pltpu.with_memory_space_constraint(basis_values, pltpu.HBM)
    blocks = pltpu.with_memory_space_constraint(domain_blocks.T, pltpu.HBM)
    plus, minus, table = plan_step(
        (1, -1), blocks, basis_values, row_count, band_count, grid_count
    )
    near = [orbitals(plus, 1), orbitals(minus, -1)]
    plus_a, plus_b, minus_a, minus_b = pick_step((2, -2), cuts, table, basis_values)
    far_a = [orbitals(plus_a, 2), orbitals(minus_a, -2)]
    far_b = [orbitals(plus_b, 2), orbitals(minus_b, -2)]

    x = x_initial
    narrow = x.astype(jnp.bfloat16)
    for iteration in range(ITERS):
        upward = jnp.stack([narrow[-2, 2], narrow[-1, 1], narrow[-1, 2]])
        downward = jnp.stack([narrow[0, 0], narrow[0, 1], narrow[1, 0]])
        top = passed_along(upward, ("band", "grid"), 1)
        bottom = passed_along(downward, ("band", "grid"), -1)
        x, narrow = square_step(sp2_choices[iteration : iteration + 1], x, narrow, top, bottom)

    ham, near_pot = domain_step((0, 1, 2), table, narrow, None, [basis_values] + near, factor)
    ham, pot_a = domain_step((3, 4), table, narrow, ham, far_a, factor)
    psi_b, pot_b = potential_step((3, 4), table, narrow, far_b, factor)
    far_pot = jnp.concatenate([pot_a[:, 0], pot_b[:, 0]], axis=1)
    ham = block_step((3, 4), table, psi_b, ham, far_b)
    sent_back = [near_pot[0, 0]]
    for move, values in ((1, near_pot[1, 0]), (-1, near_pot[2, 0]), (2, far_pot[0]), (-2, far_pot[1])):
        sent_back.append(passed_along(values, "band", -move))
    own_moves = table[MOVES : MOVES + local_domains]
    own_potential = jnp.zeros((local_domains, points), jnp.float32)
    for move, values in zip(SLOT_MOVES, sent_back):
        own_potential = jnp.where((own_moves == move)[:, None], values[None, :], own_potential)
    return x, ham, own_potential


def solution(mesh):
    placed = (P(("band", "grid"), None, None, None), P(), P(), P(("band", "grid"), None, None))
    return jax.shard_map(
        whole_step,
        mesh=mesh,
        in_specs=placed,
        out_specs=(
            P(("band", "grid"), None, None, None),
            P(("band", "grid"), None, None, None),
            P(("band", "grid"), None),
        ),
        check_vma=False,
    )
```

profile of v0, /device:TPU:56, one launch (start us, length us, event | category | flops | bytes accessed | tf_op | source)
XLA Modules:
  0.0 254.0 jit_solution(17617910920551768339)
XLA Ops:
  3.1 3.7 %collective-permute-start.1 = (bf16[3,256,256]{2,1,0:T(8,128)(2,1)S(1)}, bf16[3,256,256]{2,1,0:T(8,128)(2,1)S(1)}, u32[]{:S(2)}, u32[]{:S(2)}) collective-permute-start(bf16[3,256,256]{2,1,0:T(8,128)(2,1)S(1)} %pad_maximum_fusion.1), channel_id=1, source_target_pairs={{1,0},{2,1},{3,2},{4,3},{5,4},{6,5},{7,6},{8,7},{9,8},{10,9},{11,1... | collective-permute-start | bytes 1179656 | tf_op jit(solution)/shard_map/ppermute | solution.py:26
  9.4 2.6 %collective-permute-done.1.bottom_ref = bf16[3,256,256]{2,1,0:T(8,128)(2,1)S(1)} collective-permute-done((bf16[3,256,256]{2,1,0:T(8,128)(2,1)S(1)}, bf16[3,256,256]{2,1,0:T(8,128)(2,1)S(1)}, u32[]{:S(2)}, u32[]{:S(2)}) %collective-permute-start.1) | collective-permute-done | bytes 393248 | tf_op jit(solution)/shard_map/ppermute | solution.py:26
  12.0 6.0 %collective-permute-done.top_ref = bf16[3,256,256]{2,1,0:T(8,128)(2,1)S(1)} collective-permute-done((bf16[3,256,256]{2,1,0:T(8,128)(2,1)S(1)}, bf16[3,256,256]{2,1,0:T(8,128)(2,1)S(1)}, u32[]{:S(2)}, u32[]{:S(2)}) %collective-permute-start) | collective-permute-done | bytes 393248 | tf_op jit(solution)/shard_map/ppermute | solution.py:26
  18.0 7.5 %square_step.4 = (f32[5,3,256,256]{3,2,1,0:T(8,128)}, bf16[5,3,256,256]{3,2,1,0:T(8,128)(2,1)S(1)}) custom-call(s32[1]{0:T(128)} %get-tuple-element.79.choice_ref, f32[5,3,256,256]{3,2,1,0:T(8,128)} %x_ref.1, bf16[5,3,256,256]{3,2,1,0:T(8,128)(2,1)S(1)} %convert_element_type.3.narrow_ref, bf16[3,256,256]{2,1,0:T(8,128)(2,1)S(1)} %collective-permute-done.top_ref, ...), custom_call_target="tpu_custom_call" | custom-call | flops 2013265920 | bytes 11796480 | tf_op jit(solution)/shard_map/square_step/pallas_call | solution.py:83
  30.0 2.8 %collective-permute-done.3.bottom_ref = bf16[3,256,256]{2,1,0:T(8,128)(2,1)S(1)} collective-permute-done((bf16[3,256,256]{2,1,0:T(8,128)(2,1)S(1)}, bf16[3,256,256]{2,1,0:T(8,128)(2,1)S(1)}, u32[]{:S(2)}, u32[]{:S(2)}) %collective-permute-start.3) | collective-permute-done | bytes 393248 | tf_op jit(solution)/shard_map/ppermute | solution.py:26
  32.8 6.0 %collective-permute-done.2.top_ref = bf16[3,256,256]{2,1,0:T(8,128)(2,1)S(1)} collective-permute-done((bf16[3,256,256]{2,1,0:T(8,128)(2,1)S(1)}, bf16[3,256,256]{2,1,0:T(8,128)(2,1)S(1)}, u32[]{:S(2)}, u32[]{:S(2)}) %collective-permute-start.2) | collective-permute-done | bytes 393248 | tf_op jit(solution)/shard_map/ppermute | solution.py:26
  38.8 7.5 %square_step.5 = (f32[5,3,256,256]{3,2,1,0:T(8,128)}, bf16[5,3,256,256]{3,2,1,0:T(8,128)(2,1)S(1)}) custom-call(s32[1]{0:T(128)} %get-tuple-element.82.choice_ref, f32[5,3,256,256]{3,2,1,0:T(8,128)} %get-tuple-element.24.x_ref, bf16[5,3,256,256]{3,2,1,0:T(8,128)(2,1)S(1)} %get-tuple-element.25.narrow_ref, ...), custom_call_target="tpu_custom_call" | custom-call | flops 2013265920 | bytes 11796480 | tf_op jit(solution)/shard_map/square_step/pallas_call | solution.py:83
  50.8 4.1 %plan_step.1 = (bf16[768,1280]{1,0:T(8,128)(2,1)S(1)}, bf16[768,1280]{1,0:T(8,128)(2,1)S(1)}, s32[16]{0:T(128)S(1)}) custom-call(s32[5,384]{1,0:T(8,128)} %bitcast.56, bf16[3,768,1280]{2,1,0:T(8,128)(2,1)} %refs_0_.1), custom_call_target="tpu_custom_call" | custom-call | tf_op jit(solution)/shard_map/plan_step/pallas_call | solution.py:151
  54.9 3.8 %collective-permute-start.10 = (bf16[768,1280]{1,0:T(8,128)(2,1)S(1)}, bf16[768,1280]{1,0:T(8,128)(2,1)S(1)}, u32[]{:S(2)}, u32[]{:S(2)}) collective-permute-start(bf16[768,1280]{1,0:T(8,128)(2,1)S(1)} %get-tuple-element.36), channel_id=1, source_target_pairs={{0,8},{8,16},{16,24},{24,32},{32,40},{40,48},{48,56},{56,64},{64,7... | collective-permute-start | bytes 5898248 | tf_op jit(solution)/shard_map/ppermute | solution.py:26
  58.7 8.4 %collective-permute-start.11 = (bf16[768,1280]{1,0:T(8,128)(2,1)S(1)}, bf16[768,1280]{1,0:T(8,128)(2,1)S(1)}, u32[]{:S(2)}, u32[]{:S(2)}) collective-permute-start(bf16[768,1280]{1,0:T(8,128)(2,1)S(1)} %get-tuple-element.37), channel_id=1, source_target_pairs={{8,0},{16,8},{24,16},{32,24},{40,32},{48,40},{56,48},{64,56},{72,6... | collective-permute-start | bytes 5898248 | tf_op jit(solution)/shard_map/ppermute | solution.py:26
  67.2 3.0 %pick_step.1 = (bf16[512,1280]{1,0:T(8,128)(2,1)S(1)}, bf16[256,1280]{1,0:T(8,128)(2,1)S(1)}, bf16[512,1280]{1,0:T(8,128)(2,1)S(1)}, bf16[256,1280]{1,0:T(8,128)(2,1)S(1)}) custom-call(s32[16]{0:T(128)S(1)} %get-tuple-element.31.table_ref, bf16[3,768,1280]{2,1,0:T(8,128)(2,1)} %refs_0_.1), custom_call_target="tpu_custom_call" | custom-call | tf_op jit(solution)/shard_map/pick_step/pallas_call | solution.py:205
  72.2 7.5 %square_step.6 = (f32[5,3,256,256]{3,2,1,0:T(8,128)}, bf16[5,3,256,256]{3,2,1,0:T(8,128)(2,1)S(1)}) custom-call(s32[1]{0:T(128)} %get-tuple-element.80.choice_ref, f32[5,3,256,256]{3,2,1,0:T(8,128)} %get-tuple-element.26.x_ref, bf16[5,3,256,256]{3,2,1,0:T(8,128)(2,1)S(1)} %get-tuple-element.27.narrow_ref, ...), custom_call_target="tpu_custom_call" | custom-call | flops 2013265920 | bytes 11796480 | tf_op jit(solution)/shard_map/square_step/pallas_call | solution.py:83
  79.7 7.1 %collective-permute-start.7 = (bf16[3,256,256]{2,1,0:T(8,128)(2,1)S(1)}, bf16[3,256,256]{2,1,0:T(8,128)(2,1)S(1)}, u32[]{:S(2)}, u32[]{:S(2)}) collective-permute-start(bf16[3,256,256]{2,1,0:T(8,128)(2,1)S(1)} %pad_maximum_fusion.7), channel_id=1, source_target_pairs={{1,0},{2,1},{3,2},{4,3},{5,4},{6,5},{7,6},{8,7},{9,8},{10,9},{11,1... | collective-permute-start | bytes 1179656 | tf_op jit(solution)/shard_map/ppermute | solution.py:26
  88.8 54.6 %collective-permute-done.8.refs_0_ = bf16[256,1280]{1,0:T(8,128)(2,1)S(1)} collective-permute-done((bf16[256,1280]{1,0:T(8,128)(2,1)S(1)}, bf16[256,1280]{1,0:T(8,128)(2,1)S(1)}, u32[]{:S(2)}, u32[]{:S(2)}) %collective-permute-start.8) | collective-permute-done | bytes 655392 | tf_op jit(solution)/shard_map/ppermute | solution.py:26
  145.3 5.5 %collective-permute-start.12 = (bf16[512,1280]{1,0:T(8,128)(2,1)S(1)}, bf16[512,1280]{1,0:T(8,128)(2,1)S(1)}, u32[]{:S(2)}, u32[]{:S(2)}) collective-permute-start(bf16[512,1280]{1,0:T(8,128)(2,1)S(1)} %get-tuple-element.39), channel_id=1, source_target_pairs={{0,16},{8,24},{16,32},{24,40},{32,48},{40,56},{48,64},{56,72},{64,... | collective-permute-start | bytes 3932168 | tf_op jit(solution)/shard_map/ppermute | solution.py:26
  150.8 3.0 %collective-permute-start.13 = (bf16[512,1280]{1,0:T(8,128)(2,1)S(1)}, bf16[512,1280]{1,0:T(8,128)(2,1)S(1)}, u32[]{:S(2)}, u32[]{:S(2)}) collective-permute-start(bf16[512,1280]{1,0:T(8,128)(2,1)S(1)} %get-tuple-element.40), channel_id=1, source_target_pairs={{16,0},{24,8},{32,16},{40,24},{48,32},{56,40},{64,48},{72,56},{80,... | collective-permute-start | bytes 3932168 | tf_op jit(solution)/shard_map/ppermute | solution.py:26
  153.8 7.4 %square_step.7 = (f32[5,3,256,256]{3,2,1,0:T(8,128)}, bf16[5,3,256,256]{3,2,1,0:T(8,128)(2,1)S(1)}) custom-call(s32[1]{0:T(128)} %get-tuple-element.81.choice_ref, f32[5,3,256,256]{3,2,1,0:T(8,128)} %get-tuple-element.28.x_ref, bf16[5,3,256,256]{3,2,1,0:T(8,128)(2,1)S(1)} %get-tuple-element.29.narrow_ref, ...), custom_call_target="tpu_custom_call" | custom-call | flops 2013265920 | bytes 11796480 | tf_op jit(solution)/shard_map/square_step/pallas_call | solution.py:83
  161.3 31.2 %collective-permute-done.9.refs_1_ = bf16[256,1280]{1,0:T(8,128)(2,1)S(1)} collective-permute-done((bf16[256,1280]{1,0:T(8,128)(2,1)S(1)}, bf16[256,1280]{1,0:T(8,128)(2,1)S(1)}, u32[]{:S(2)}, u32[]{:S(2)}) %collective-permute-start.9) | collective-permute-done | bytes 655392 | tf_op jit(solution)/shard_map/ppermute | solution.py:26
  194.8 7.6 %domain_step.2 = (f32[5,3,256,256]{3,2,1,0:T(8,128)}, f32[3,1,768]{2,1,0:T(1,128)S(1)}) custom-call(s32[16]{0:T(128)S(1)} %get-tuple-element.31.table_ref, bf16[5,3,256,256]{3,2,1,0:T(8,128)(2,1)S(1)} %get-tuple-element.32.tile_ref, bf16[3,768,1280]{2,1,0:T(8,128)(2,1)} %refs_0_.1, bf16[768,1280]{1,0:T(8,128)(2,1)S(1)} %collective-permute-done.10.refs_1_, ...), custom_call_target="tpu_custom_call" | custom-call | flops 7247757312 | bytes 11796480 | tf_op jit(solution)/shard_map/domain_step/pallas_call | solution.py:322
  202.3 16.6 %collective-permute-done.13.refs_2_ = bf16[512,1280]{1,0:T(8,128)(2,1)S(1)} collective-permute-done((bf16[512,1280]{1,0:T(8,128)(2,1)S(1)}, bf16[512,1280]{1,0:T(8,128)(2,1)S(1)}, u32[]{:S(2)}, u32[]{:S(2)}) %collective-permute-start.13) | collective-permute-done | bytes 1310752 | tf_op jit(solution)/shard_map/ppermute | solution.py:26
  221.1 9.3 %domain_step.3 = (f32[5,3,256,256]{3,2,1,0:T(8,128)}, f32[2,1,512]{2,1,0:T(1,128)S(1)}) custom-call(s32[16]{0:T(128)S(1)} %get-tuple-element.31.table_ref, bf16[5,3,256,256]{3,2,1,0:T(8,128)(2,1)S(1)} %get-tuple-element.32.tile_ref, f32[5,3,256,256]{3,2,1,0:T(8,128)S(1)} %copy-done.1, bf16[512,1280]{1,0:T(8,128)(2,1)S(1)} %collective-permute-done.12.refs_1_, ...), custom_call_target="tpu_custom_call" | custom-call | flops 3221225472 | bytes 8519680 | tf_op jit(solution)/shard_map/domain_step/pallas_call | solution.py:322
  232.3 6.3 %collective-permute-start.15 = (f32[768]{0:T(1024)S(1)}, f32[768]{0:T(1024)S(1)}, u32[]{:S(2)}, u32[]{:S(2)}) collective-permute-start(f32[768]{0:T(1024)S(1)} %get-tuple-element.49), channel_id=1, source_target_pairs={{16,0},{24,8},{32,16},{40,24},{48,32},{56,40},{64,48},{72,56},{80,... | collective-permute-start | bytes 9224 | tf_op jit(solution)/shard_map/ppermute | solution.py:26
  240.6 3.9 %collective-permute-start.17 = (f32[768]{0:T(1024)S(1)}, f32[768]{0:T(1024)S(1)}, u32[]{:S(2)}, u32[]{:S(2)}) collective-permute-start(f32[768]{0:T(1024)S(1)} %get-tuple-element.47), channel_id=1, source_target_pairs={{8,0},{16,8},{24,16},{32,24},{40,32},{48,40},{56,48},{64,56},{72,6... | collective-permute-start | bytes 9224 | tf_op jit(solution)/shard_map/ppermute | solution.py:26
  246.7 6.6 %block_step.1 = f32[5,3,256,256]{3,2,1,0:T(8,128)} custom-call(s32[16]{0:T(128)S(1)} %get-tuple-element.31.table_ref, bf16[2,256,1280]{2,1,0:T(8,128)(2,1)S(1)} %get-tuple-element.35.psi_ref, f32[5,3,256,256]{3,2,1,0:T(8,128)S(1)} %copy-done, bf16[256,1280]{1,0:T(8,128)(2,1)S(1)} %collective-permute-done.8.refs_0_, ...), custom_call_target="tpu_custom_call" | custom-call | flops 805306368 | bytes 10485760 | tf_op jit(solution)/shard_map/block_step/pallas_call | solution.py:431
  (48 shorter events, 31.1 us)
Async XLA Ops:
  3.0 5.8 %copy-start.2 = (s32[4]{0:T(128)S(1)}, s32[4]{0:T(128)}, u32[]{:S(2)}) copy-start(s32[4]{0:T(128)} %param.5) | copy-start | bytes 52
  3.1 8.9 %collective-permute-start.1 = (bf16[3,256,256]{2,1,0:T(8,128)(2,1)S(1)}, bf16[3,256,256]{2,1,0:T(8,128)(2,1)S(1)}, u32[]{:S(2)}, u32[]{:S(2)}) collective-permute-start(bf16[3,256,256]{2,1,0:T(8,128)(2,1)S(1)} %pad_maximum_fusion.1), channel_id=1, source_target_pairs={{1,0},{2,1},{3,2},{4,3},{5,4},{6,5},{7,6},{8,7},{9,8},{10,9},{11,1... | collective-permute-start | bytes 1179656 | tf_op jit(solution)/shard_map/ppermute | solution.py:26
  6.8 11.2 %collective-permute-start = (bf16[3,256,256]{2,1,0:T(8,128)(2,1)S(1)}, bf16[3,256,256]{2,1,0:T(8,128)(2,1)S(1)}, u32[]{:S(2)}, u32[]{:S(2)}) collective-permute-start(bf16[3,256,256]{2,1,0:T(8,128)(2,1)S(1)} %pad_maximum_fusion), channel_id=1, source_target_pairs={{0,1},{1,2},{2,3},{3,4},{4,5},{5,6},{6,7},{7,8},{8,9},{9,10},{10,1... | collective-permute-start | bytes 1179656 | tf_op jit(solution)/shard_map/ppermute | solution.py:26
  25.6 7.2 %collective-permute-start.3 = (bf16[3,256,256]{2,1,0:T(8,128)(2,1)S(1)}, bf16[3,256,256]{2,1,0:T(8,128)(2,1)S(1)}, u32[]{:S(2)}, u32[]{:S(2)}) collective-permute-start(bf16[3,256,256]{2,1,0:T(8,128)(2,1)S(1)} %pad_maximum_fusion.3), channel_id=1, source_target_pairs={{1,0},{2,1},{3,2},{4,3},{5,4},{6,5},{7,6},{8,7},{9,8},{10,9},{11,1... | collective-permute-start | bytes 1179656 | tf_op jit(solution)/shard_map/ppermute | solution.py:26
  27.6 11.2 %collective-permute-start.2 = (bf16[3,256,256]{2,1,0:T(8,128)(2,1)S(1)}, bf16[3,256,256]{2,1,0:T(8,128)(2,1)S(1)}, u32[]{:S(2)}, u32[]{:S(2)}) collective-permute-start(bf16[3,256,256]{2,1,0:T(8,128)(2,1)S(1)} %pad_maximum_fusion.2), channel_id=1, source_target_pairs={{0,1},{1,2},{2,3},{3,4},{4,5},{5,6},{6,7},{7,8},{8,9},{9,10},{10,1... | collective-permute-start | bytes 1179656 | tf_op jit(solution)/shard_map/ppermute | solution.py:26
  46.4 25.7 %collective-permute-start.5 = (bf16[3,256,256]{2,1,0:T(8,128)(2,1)S(1)}, bf16[3,256,256]{2,1,0:T(8,128)(2,1)S(1)}, u32[]{:S(2)}, u32[]{:S(2)}) collective-permute-start(bf16[3,256,256]{2,1,0:T(8,128)(2,1)S(1)} %pad_maximum_fusion.5), channel_id=1, source_target_pairs={{1,0},{2,1},{3,2},{4,3},{5,4},{6,5},{7,6},{8,7},{9,8},{10,9},{11,1... | collective-permute-start | bytes 1179656 | tf_op jit(solution)/shard_map/ppermute | solution.py:26
  48.4 23.7 %collective-permute-start.4 = (bf16[3,256,256]{2,1,0:T(8,128)(2,1)S(1)}, bf16[3,256,256]{2,1,0:T(8,128)(2,1)S(1)}, u32[]{:S(2)}, u32[]{:S(2)}) collective-permute-start(bf16[3,256,256]{2,1,0:T(8,128)(2,1)S(1)} %pad_maximum_fusion.4), channel_id=1, source_target_pairs={{0,1},{1,2},{2,3},{3,4},{4,5},{5,6},{6,7},{7,8},{8,9},{9,10},{10,1... | collective-permute-start | bytes 1179656 | tf_op jit(solution)/shard_map/ppermute | solution.py:26
  54.9 139.9 %collective-permute-start.10 = (bf16[768,1280]{1,0:T(8,128)(2,1)S(1)}, bf16[768,1280]{1,0:T(8,128)(2,1)S(1)}, u32[]{:S(2)}, u32[]{:S(2)}) collective-permute-start(bf16[768,1280]{1,0:T(8,128)(2,1)S(1)} %get-tuple-element.36), channel_id=1, source_target_pairs={{0,8},{8,16},{16,24},{24,32},{32,40},{40,48},{48,56},{56,64},{64,7... | collective-permute-start | bytes 5898248 | tf_op jit(solution)/shard_map/ppermute | solution.py:26
  58.7 136.0 %collective-permute-start.11 = (bf16[768,1280]{1,0:T(8,128)(2,1)S(1)}, bf16[768,1280]{1,0:T(8,128)(2,1)S(1)}, u32[]{:S(2)}, u32[]{:S(2)}) collective-permute-start(bf16[768,1280]{1,0:T(8,128)(2,1)S(1)} %get-tuple-element.37), channel_id=1, source_target_pairs={{8,0},{16,8},{24,16},{32,24},{40,32},{48,40},{56,48},{64,56},{72,6... | collective-permute-start | bytes 5898248 | tf_op jit(solution)/shard_map/ppermute | solution.py:26
  70.2 73.2 %collective-permute-start.8 = (bf16[256,1280]{1,0:T(8,128)(2,1)S(1)}, bf16[256,1280]{1,0:T(8,128)(2,1)S(1)}, u32[]{:S(2)}, u32[]{:S(2)}) collective-permute-start(bf16[256,1280]{1,0:T(8,128)(2,1)S(1)} %get-tuple-element.33), channel_id=1, source_target_pairs={{0,16},{8,24},{16,32},{24,40},{32,48},{40,56},{48,64},{56,72},{64,... | collective-permute-start | bytes 1966088 | tf_op jit(solution)/shard_map/ppermute | solution.py:26
  79.7 65.6 %collective-permute-start.7 = (bf16[3,256,256]{2,1,0:T(8,128)(2,1)S(1)}, bf16[3,256,256]{2,1,0:T(8,128)(2,1)S(1)}, u32[]{:S(2)}, u32[]{:S(2)}) collective-permute-start(bf16[3,256,256]{2,1,0:T(8,128)(2,1)S(1)} %pad_maximum_fusion.7), channel_id=1, source_target_pairs={{1,0},{2,1},{3,2},{4,3},{5,4},{6,5},{7,6},{8,7},{9,8},{10,9},{11,1... | collective-permute-start | bytes 1179656 | tf_op jit(solution)/shard_map/ppermute | solution.py:26
  86.9 63.9 %collective-permute-start.6 = (bf16[3,256,256]{2,1,0:T(8,128)(2,1)S(1)}, bf16[3,256,256]{2,1,0:T(8,128)(2,1)S(1)}, u32[]{:S(2)}, u32[]{:S(2)}) collective-permute-start(bf16[3,256,256]{2,1,0:T(8,128)(2,1)S(1)} %pad_maximum_fusion.6), channel_id=1, source_target_pairs={{0,1},{1,2},{2,3},{3,4},{4,5},{5,6},{6,7},{7,8},{8,9},{9,10},{10,1... | collective-permute-start | bytes 1179656 | tf_op jit(solution)/shard_map/ppermute | solution.py:26
  143.4 49.1 %collective-permute-start.9 = (bf16[256,1280]{1,0:T(8,128)(2,1)S(1)}, bf16[256,1280]{1,0:T(8,128)(2,1)S(1)}, u32[]{:S(2)}, u32[]{:S(2)}) collective-permute-start(bf16[256,1280]{1,0:T(8,128)(2,1)S(1)} %get-tuple-element.34), channel_id=1, source_target_pairs={{16,0},{24,8},{32,16},{40,24},{48,32},{56,40},{64,48},{72,56},{80,... | collective-permute-start | bytes 1966088 | tf_op jit(solution)/shard_map/ppermute | solution.py:26
  145.3 57.0 %collective-permute-start.12 = (bf16[512,1280]{1,0:T(8,128)(2,1)S(1)}, bf16[512,1280]{1,0:T(8,128)(2,1)S(1)}, u32[]{:S(2)}, u32[]{:S(2)}) collective-permute-start(bf16[512,1280]{1,0:T(8,128)(2,1)S(1)} %get-tuple-element.39), channel_id=1, source_target_pairs={{0,16},{8,24},{16,32},{24,40},{32,48},{40,56},{48,64},{56,72},{64,... | collective-permute-start | bytes 3932168 | tf_op jit(solution)/shard_map/ppermute | solution.py:26
  150.8 68.2 %collective-permute-start.13 = (bf16[512,1280]{1,0:T(8,128)(2,1)S(1)}, bf16[512,1280]{1,0:T(8,128)(2,1)S(1)}, u32[]{:S(2)}, u32[]{:S(2)}) collective-permute-start(bf16[512,1280]{1,0:T(8,128)(2,1)S(1)} %get-tuple-element.40), channel_id=1, source_target_pairs={{16,0},{24,8},{32,16},{40,24},{48,32},{56,40},{64,48},{72,56},{80,... | collective-permute-start | bytes 3932168 | tf_op jit(solution)/shard_map/ppermute | solution.py:26
  219.0 2.1 copy-start.1
  230.4 22.9 %collective-permute-start.14 = (f32[768]{0:T(1024)S(1)}, f32[768]{0:T(1024)S(1)}, u32[]{:S(2)}, u32[]{:S(2)}) collective-permute-start(f32[768]{0:T(1024)S(1)} %get-tuple-element.48), channel_id=1, source_target_pairs={{0,16},{8,24},{16,32},{24,40},{32,48},{40,56},{48,64},{56,72},{64,... | collective-permute-start | bytes 9224 | tf_op jit(solution)/shard_map/ppermute | solution.py:26
  232.3 21.0 %collective-permute-start.15 = (f32[768]{0:T(1024)S(1)}, f32[768]{0:T(1024)S(1)}, u32[]{:S(2)}, u32[]{:S(2)}) collective-permute-start(f32[768]{0:T(1024)S(1)} %get-tuple-element.49), channel_id=1, source_target_pairs={{16,0},{24,8},{32,16},{40,24},{48,32},{56,40},{64,48},{72,56},{80,... | collective-permute-start | bytes 9224 | tf_op jit(solution)/shard_map/ppermute | solution.py:26
  238.7 14.6 %collective-permute-start.16 = (f32[768]{0:T(1024)S(1)}, f32[768]{0:T(1024)S(1)}, u32[]{:S(2)}, u32[]{:S(2)}) collective-permute-start(f32[768]{0:T(1024)S(1)} %get-tuple-element.45), channel_id=1, source_target_pairs={{0,8},{8,16},{16,24},{24,32},{32,40},{40,48},{48,56},{56,64},{64,7... | collective-permute-start | bytes 9224 | tf_op jit(solution)/shard_map/ppermute | solution.py:26
  240.6 12.7 %collective-permute-start.17 = (f32[768]{0:T(1024)S(1)}, f32[768]{0:T(1024)S(1)}, u32[]{:S(2)}, u32[]{:S(2)}) collective-permute-start(f32[768]{0:T(1024)S(1)} %get-tuple-element.47), channel_id=1, source_target_pairs={{8,0},{16,8},{24,16},{32,24},{40,32},{48,40},{56,48},{64,56},{72,6... | collective-permute-start | bytes 9224 | tf_op jit(solution)/shard_map/ppermute | solution.py:26
  244.6 2.1 copy-start
where the time goes:
time: 255 us; the launch traced here: 254 us
  waiting for transfers between devices  120 us (47%)
  Pallas kernels  62.7 us (25%)
  starting transfers between devices  61.8 us (24%)
  local copies, waits for them, and re-layouts  5.14 us (2%)
  other arithmetic  3.49 us (1%)
    ppermute x18, waiting for transfers between devices, passed_along(): return lax.ppermute(x, axis, pairs)  120 us
    ppermute x18, starting transfers between devices, passed_along(): return lax.ppermute(x, axis, pairs)  61.8 us
    pallas_call x4, Pallas kernels, square_step(): pl.pallas_call(square_kernel, grid=(rows,), in_specs=[pl.BlockSpec(memory...  29.9 us
    pallas_call x2, Pallas kernels, domain_step(): pl.pallas_call(functools.partial(domain_kernel, slots, has_base, factor),...  16.9 us
    pallas_call x1, Pallas kernels, block_step(): pl.pallas_call(functools.partial(block_kernel, slots), in_specs=[smem, vm...  6.59 us
  transfers between devices with their start and end apart: 18, of which 7 were waited for; matrix products, arithmetic and copies ran while one was open for 0% of the time, Pallas kernels for 15%

commit v1 on v0

--- a/solution.py
+++ b/solution.py
@@ -30,72 +30,148 @@
     return lax.dot_general(a, b, dims, preferred_element_type=jnp.float32)
 
 
-def square_kernel(choice_ref, x_ref, narrow_ref, top_ref, bottom_ref, x_out, narrow_out, ext):
+def edge_blocks(rows):
+    return ((0, 0), (0, 1), (1, 0), (rows - 2, 2), (rows - 1, 1), (rows - 1, 2))
+
+
+def local_kernel(
+    choice_ref, x_ref, edge_ref, narrow_ref, down_ref, up_ref, x_out, narrow_out, ext
+):
     rows = narrow_ref.shape[0]
-    row = pl.program_id(0)
-
-    @pl.when(row == 0)
+    edges = edge_blocks(rows)
+    none = jnp.zeros((BS, BS), jnp.bfloat16)
+    for r in (0, 1, rows + 2, rows + 3):
+        for q in range(3):
+            ext[r, q] = none
+    for r in range(rows):
+        for q in range(3):
+            if (r, q) in edges:
+                place = edges.index((r, q))
+                ext[r + 2, q] = down_ref[place] if place < 3 else up_ref[place - 3]
+            else:
+                ext[r + 2, q] = narrow_ref[r, q]
+    twice = choice_ref[0] == 1
+
+    @pl.loop(0, rows)
+    def _(row):
+        i = row + 2
+        here = [ext[i, q] for q in range(3)]
+        up1, up0 = ext[i - 1, 1], ext[i - 1, 2]
+        upup = ext[i - 2, 2]
+        dn1, dn0 = ext[i + 1, 1], ext[i + 1, 0]
+        dd = ext[i + 2, 0]
+        diag = (
+            dot32(here[0], here[0], NT)
+            + dot32(here[1], here[1], NT)
+            + dot32(here[2], here[2], NT)
+            + dot32(dn1, dn1, TN)
+            + dot32(dd, dd, TN)
+        )
+        near = (
+            dot32(here[0], up1, NT)
+            + dot32(here[1], up0, NN)
+            + dot32(here[2], here[1], NN)
+            + dot32(dn1, dn0, TN)
+        )
+        far = dot32(here[0], upup, NN) + dot32(here[1], up1, NN) + dot32(here[2], here[0], NN)
+        for q, squared in ((0, far), (1, near), (2, diag)):
+            new = jnp.where(twice, 2.0 * x_ref[row, q] - squared, squared)
+            x_out[row, q] = new
+            narrow_out[row, q] = new.astype(jnp.bfloat16)
+
+    @pl.when(twice)
     def _():
-        ext[0, 2] = top_ref[0]
-        ext[1, 1] = top_ref[1]
-        ext[1, 2] = top_ref[2]
-        ext[rows + 2, 0] = bottom_ref[0]
-        ext[rows + 2, 1] = bottom_ref[1]
-        ext[rows + 3, 0] = bottom_ref[2]
-        for r in range(rows):
-            ext[r + 2] = narrow_ref[r]
-
-    i = row + 2
-
-    def blk(r, q):
-        return ext[r, q]
-
-    here = [blk(i, q) for q in range(3)]
-    up1, up0 = blk(i - 1, 1), blk(i - 1, 2)
-    upup = blk(i - 2, 2)
-    dn1, dn0 = blk(i + 1, 1), blk(i + 1, 0)
-    dd = blk(i + 2, 0)
-    diag = (
-        dot32(here[0], here[0], NT)
-        + dot32(here[1], here[1], NT)
-        + dot32(here[2], here[2], NT)
-        + dot32(dn1, dn1, TN)
-        + dot32(dd, dd, TN)
+        for place, (r, q) in enumerate(edges):
+            x_out[r, q] += 2.0 * (edge_ref[place] - x_ref[r, q])
+
+
+def local_step(choice, x, edge, narrow, down, up):
+    rows = x.shape[0]
+    vmem = pl.BlockSpec(memory_space=pltpu.VMEM)
+    return pl.pallas_call(
+        local_kernel,
+        in_specs=[pl.BlockSpec(memory_space=pltpu.SMEM)] + [vmem] * 5,
+        out_specs=[vmem, vmem],
+        out_shape=[
+            jax.ShapeDtypeStruct(x.shape, jnp.float32),
+            jax.ShapeDtypeStruct(x.shape, jnp.bfloat16),
+        ],
+        scratch_shapes=[pltpu.VMEM((rows + 4, 3, BS, BS), jnp.bfloat16)],
+        compiler_params=pltpu.CompilerParams(vmem_limit_bytes=22 << 20),
+        cost_estimate=pl.CostEstimate(
+            flops=rows * 12 * 2 * BS**3, bytes_accessed=x.size * 4, transcendentals=0
+        ),
+        name="local_step",
+    )(choice, x, edge, narrow, down, up)
+
+
+def border_kernel(
+    choice_ref, before_ref, top_ref, bottom_ref, x_ref, edge_out, down_out, up_out
+):
+    rows = x_ref.shape[0]
+    sign = jnp.where(choice_ref[0] == 1, -1.0, 1.0)
+    x00, x01, x10 = before_ref[0], before_ref[1], before_ref[2]
+    t_far, t_mid, t_near = top_ref[0], top_ref[1], top_ref[2]
+    b_far, b_near, b_last = bottom_ref[0], bottom_ref[1], bottom_ref[2]
+    added = (
+        lambda: dot32(x00, t_far, NN) + dot32(x01, t_mid, NN),
+        lambda: dot32(x00, t_mid, NT) + dot32(x01, t_near, NN),
+        lambda: dot32(x10, t_near, NN),
+        lambda: dot32(b_far, b_far, TN),
+        lambda: dot32(b_near, b_far, TN),
+        lambda: dot32(b_near, b_near, TN) + dot32(b_last, b_last, TN),
     )
-    near = (
-        dot32(here[0], up1, NT)
-        + dot32(here[1], up0, NN)
-        + dot32(here[2], here[1], NN)
-        + dot32(dn1, dn0, TN)
-    )
-    far = dot32(here[0], upup, NN) + dot32(here[1], up1, NN) + dot32(here[2], here[0], NN)
-    twice = choice_ref[0] == 1
-    for q, squared in ((0, far), (1, near), (2, diag)):
-        new = jnp.where(twice, 2.0 * x_ref[0, q] - squared, squared)
-        x_out[0, q] = new
-        narrow_out[0, q] = new.astype(jnp.bfloat16)
-
-
-def square_step(choice, x, narrow, top, bottom):
-    rows = x.shape[0]
-    per_row = pl.BlockSpec((1, 3, BS, BS), lambda r: (r, 0, 0, 0))
-    whole = pl.BlockSpec(memory_space=pltpu.VMEM)
-    return pl.pallas_call(
-        square_kernel,
-        grid=(rows,),
-        in_specs=[pl.BlockSpec(memory_space=pltpu.SMEM), per_row, whole, whole, whole],
-        out_specs=[per_row, per_row],
-        out_shape=[
-            pltpu.HBM(x.shape, jnp.float32),
-            jax.ShapeDtypeStruct(x.shape, jnp.bfloat16),
-        ],
-        scratch_shapes=[pltpu.VMEM((rows + 4, 3, BS, BS), jnp.bfloat16)],
-        compiler_params=pltpu.CompilerParams(vmem_limit_bytes=24 << 20),
+    for place, (r, q) in enumerate(edge_blocks(rows)):
+        new = x_ref[r, q] + sign * added[place]()
+        edge_out[place] = new
+        if place < 3:
+            down_out[place] = new.astype(jnp.bfloat16)
+        else:
+            up_out[place - 3] = new.astype(jnp.bfloat16)
+
+
+def border_step(choice, before, top, bottom, x):
+    vmem = pl.BlockSpec(memory_space=pltpu.VMEM)
+    edge = jax.ShapeDtypeStruct(top.shape, jnp.bfloat16)
+    return pl.pallas_call(
+        border_kernel,
+        in_specs=[pl.BlockSpec(memory_space=pltpu.SMEM)] + [vmem] * 4,
+        out_specs=[vmem] * 3,
+        out_shape=[jax.ShapeDtypeStruct((6, BS, BS), jnp.float32), edge, edge],
+        compiler_params=pltpu.CompilerParams(vmem_limit_bytes=12 << 20),
         cost_estimate=pl.CostEstimate(
-            flops=rows * 12 * 2 * BS**3, bytes_accessed=x.size * 12, transcendentals=0
+            flops=9 * 2 * BS**3, bytes_accessed=x.size, transcendentals=0
         ),
-        name="square_step",
-    )(choice, pltpu.with_memory_space_constraint(x, pltpu.HBM), narrow, top, bottom)
+        name="border_step",
+    )(choice, before, top, bottom, x)
+
+
+def density_kernel(x_ref, edge_ref, out, sems):
+    rows = x_ref.shape[0]
+    edges = edge_blocks(rows)
+    copies = []
+    for r in range(rows):
+        for q in range(3):
+            source = edge_ref.at[edges.index((r, q))] if (r, q) in edges else x_ref.at[r, q]
+            copies.append(pltpu.make_async_copy(source, out.at[r, q], sems.at[r * 3 + q]))
+    for copy in copies:
+        copy.start()
+    for copy in copies:
+        copy.wait()
+
+
+def density_step(x, edge):
+    vmem = pl.BlockSpec(memory_space=pltpu.VMEM)
+    return pl.pallas_call(
+        density_kernel,
+        in_specs=[vmem, vmem],
+        out_specs=pl.BlockSpec(memory_space=pltpu.HBM),
+        out_shape=pltpu.HBM(x.shape, jnp.float32),
+        scratch_shapes=[pltpu.SemaphoreType.DMA((x.shape[0] * 3,))],
+        compiler_params=pltpu.CompilerParams(vmem_limit_bytes=8 << 20),
+        cost_estimate=pl.CostEstimate(flops=0, bytes_accessed=x.size * 4, transcendentals=0),
+        name="density_step",
+    )(x, edge)
 
 
 def plan_kernel(moves, geometry, blocks_ref, basis_ref, *refs):
@@ -217,14 +293,23 @@
     )(table, basis)
 
 
-def fill_stack(tile_ref, stack):
-    rows = tile_ref.shape[0]
+def fill_stack(tile_refs, stack):
+    main, down, up = tile_refs
+    rows = main.shape[0]
+    edges = edge_blocks(rows)
+
+    def tile(r, q):
+        if (r, q) not in edges:
+            return main[r, q]
+        place = edges.index((r, q))
+        return down[place] if place < 3 else up[place - 3]
+
     for r in range(rows):
-        stack[r, 0:BS] = tile_ref[r, 2]
+        stack[r, 0:BS] = tile(r, 2)
         for gap in (1, 2):
             where = pl.ds(gap * BS, BS)
             if r + gap < rows:
-                stack[r, where] = tile_ref[r + gap, 2 - gap] * 2
+                stack[r, where] = tile(r + gap, 2 - gap) * 2
             else:
                 stack[r, where] = jnp.zeros((BS, BS), jnp.bfloat16)
 
@@ -268,11 +353,11 @@
                 ham[first + k, 2 - (k - j)] += piece[:, (j - low) * BS : (j - low + 1) * BS]
 
 
-def domain_kernel(slots, has_base, factor, table_ref, tile_ref, *refs):
+def domain_kernel(slots, has_base, factor, table_ref, main_ref, down_ref, up_ref, *refs):
     refs = list(refs)
     base_ref = refs.pop(0) if has_base else None
     basis_refs = [refs.pop(0) for _ in slots]
-    ham_out, pot_out, phi, psi, stack, ham, sems, base_sem = refs
+    ham, pot_out, phi, psi, stack, sems = refs
 
     def fetch(n):
         source = basis_refs[n]
@@ -282,17 +367,12 @@
 
     for n in range(len(slots)):
         fetch(n).start()
-    if has_base:
-        base = pltpu.make_async_copy(base_ref, ham, base_sem)
-        base.start()
-    else:
-        ham[...] = jnp.zeros_like(ham)
-    fill_stack(tile_ref, stack)
+    for r in range(ham.shape[0]):
+        ham[r] = base_ref[r] if has_base else jnp.zeros_like(ham[r])
+    fill_stack((main_ref, down_ref, up_ref), stack)
     pot_out[...] = jnp.zeros_like(pot_out)
     for n in range(len(slots)):
         fetch(n).wait()
-    if has_base:
-        base.wait()
 
     @pl.loop(0, len(slots))
     def _(n):
@@ -305,38 +385,31 @@
             potential_of_slot(phi, n, first, stack, pot_out, lambda here: psi.at[here], factor)
             add_blocks(ham, psi, phi, n, first, blocks)
 
-    result = pltpu.make_async_copy(ham, ham_out, base_sem)
-    result.start()
-    result.wait()
-
 
 def domain_step(slots, table, tiles, base, arrays, factor):
-    rows = tiles.shape[0]
+    rows = tiles[0].shape[0]
     points, width = arrays[-1].shape[-2:]
     number = len(arrays)
     has_base = base is not None
     smem = pl.BlockSpec(memory_space=pltpu.SMEM)
     vmem = pl.BlockSpec(memory_space=pltpu.VMEM)
     hbm = pl.BlockSpec(memory_space=pl.ANY)
-    operands = [table, tiles] + ([base] if has_base else []) + list(arrays)
+    operands = [table, *tiles] + ([base] if has_base else []) + list(arrays)
     return pl.pallas_call(
         functools.partial(domain_kernel, slots, has_base, factor),
-        in_specs=[smem, vmem]
-        + [pl.BlockSpec(memory_space=pltpu.HBM) if o.ndim >= 3 else hbm for o in operands[2:]],
-        out_specs=[pl.BlockSpec(memory_space=pltpu.HBM), vmem],
+        in_specs=[smem] + [vmem] * (3 + has_base) + [hbm] * number,
+        out_specs=[vmem, vmem],
         out_shape=[
-            pltpu.HBM((rows, 3, BS, BS), jnp.float32),
+            jax.ShapeDtypeStruct((rows, 3, BS, BS), jnp.float32),
             jax.ShapeDtypeStruct((number, 1, points), jnp.float32),
         ],
         scratch_shapes=[
             pltpu.VMEM((number, points, width), jnp.bfloat16),
             pltpu.VMEM((points, width), jnp.bfloat16),
             pltpu.VMEM((rows, 3 * BS, BS), jnp.bfloat16),
-            pltpu.VMEM((rows, 3, BS, BS), jnp.float32),
             pltpu.SemaphoreType.DMA((number,)),
-            pltpu.SemaphoreType.DMA,
-        ],
-        compiler_params=pltpu.CompilerParams(vmem_limit_bytes=36 << 20),
+        ],
+        compiler_params=pltpu.CompilerParams(vmem_limit_bytes=(17 << 20) + number * points * width * 2),
         cost_estimate=pl.CostEstimate(
             flops=number * 24 * 2 * points * BS * BS,
             bytes_accessed=number * points * width * 2 + rows * 3 * BS * BS * 6,
@@ -346,10 +419,10 @@
     )(*operands)
 
 
-def potential_kernel(slots, factor, table_ref, tile_ref, *refs):
+def potential_kernel(slots, factor, table_ref, main_ref, down_ref, up_ref, *refs):
     basis_refs = refs[: len(slots)]
     psi_out, pot_out, phi, stack = refs[len(slots) :]
-    fill_stack(tile_ref, stack)
+    fill_stack((main_ref, down_ref, up_ref), stack)
     pot_out[...] = jnp.zeros_like(pot_out)
     for n in range(len(slots)):
         phi[n] = basis_refs[n][...]
@@ -366,7 +439,7 @@
 
 
 def potential_step(slots, table, tiles, arrays, factor):
-    rows = tiles.shape[0]
+    rows = tiles[0].shape[0]
     points, width = arrays[-1].shape
     number = len(arrays)
     smem = pl.BlockSpec(memory_space=pltpu.SMEM)
@@ -374,7 +447,7 @@
     hbm = pl.BlockSpec(memory_space=pl.ANY)
     return pl.pallas_call(
         functools.partial(potential_kernel, slots, factor),
-        in_specs=[smem, vmem] + [vmem] * number,
+        in_specs=[smem] + [vmem] * (3 + number),
         out_specs=[vmem, vmem],
         out_shape=[
             jax.ShapeDtypeStruct((number, points, width), jnp.bfloat16),
@@ -391,7 +464,7 @@
             transcendentals=number * points,
         ),
         name="potential_step",
-    )(table, tiles, *arrays)
+    )(table, *tiles, *arrays)
 
 
 def block_kernel(slots, table_ref, psi_ref, base_ref, *refs):
@@ -461,25 +534,32 @@
     basis_values = pltpu.with_memory_space_constraint(basis_values, pltpu.HBM)
     blocks = pltpu.with_memory_space_constraint(domain_blocks.T, pltpu.HBM)
     plus, minus, table = plan_step(
-        (1, -1), blocks, basis_values, row_count, band_count, grid_count
+        (2, -2), blocks, basis_values, row_count, band_count, grid_count
     )
+    halfway = [orbitals(plus, 1), orbitals(minus, -1)]
+    plus, minus = pick_step((1, -1), ((0, points),), table, basis_values)
     near = [orbitals(plus, 1), orbitals(minus, -1)]
-    plus_a, plus_b, minus_a, minus_b = pick_step((2, -2), cuts, table, basis_values)
-    far_a = [orbitals(plus_a, 2), orbitals(minus_a, -2)]
-    far_b = [orbitals(plus_b, 2), orbitals(minus_b, -2)]
+    far_a = [orbitals(halfway[n][: cuts[0][1]], 1 - 2 * n) for n in (0, 1)]
+    far_b = [orbitals(halfway[n][cuts[1][0] :], 1 - 2 * n) for n in (0, 1)]
 
     x = x_initial
     narrow = x.astype(jnp.bfloat16)
+    upward = jnp.stack([narrow[-2, 2], narrow[-1, 1], narrow[-1, 2]])
+    downward = jnp.stack([narrow[0, 0], narrow[0, 1], narrow[1, 0]])
+    edge = jnp.stack([x[r, q] for r, q in edge_blocks(row_count)])
     for iteration in range(ITERS):
-        upward = jnp.stack([narrow[-2, 2], narrow[-1, 1], narrow[-1, 2]])
-        downward = jnp.stack([narrow[0, 0], narrow[0, 1], narrow[1, 0]])
+        choice = sp2_choices[iteration : iteration + 1]
         top = passed_along(upward, ("band", "grid"), 1)
         bottom = passed_along(downward, ("band", "grid"), -1)
-        x, narrow = square_step(sp2_choices[iteration : iteration + 1], x, narrow, top, bottom)
-
-    ham, near_pot = domain_step((0, 1, 2), table, narrow, None, [basis_values] + near, factor)
-    ham, pot_a = domain_step((3, 4), table, narrow, ham, far_a, factor)
-    psi_b, pot_b = potential_step((3, 4), table, narrow, far_b, factor)
+        before = downward
+        x, narrow = local_step(choice, x, edge, narrow, downward, upward)
+        edge, downward, upward = border_step(choice, before, top, bottom, x)
+    tiles = (narrow, downward, upward)
+    density = density_step(x, edge)
+
+    ham, near_pot = domain_step((0, 1, 2), table, tiles, None, [basis_values] + near, factor)
+    ham, pot_a = domain_step((3, 4), table, tiles, ham, far_a, factor)
+    psi_b, pot_b = potential_step((3, 4), table, tiles, far_b, factor)
     far_pot = jnp.concatenate([pot_a[:, 0], pot_b[:, 0]], axis=1)
     ham = block_step((3, 4), table, psi_b, ham, far_b)
     sent_back = [near_pot[0, 0]]
@@ -489,7 +569,7 @@
     own_potential = jnp.zeros((local_domains, points), jnp.float32)
     for move, values in zip(SLOT_MOVES, sent_back):
         own_potential = jnp.where((own_moves == move)[:, None], values[None, :], own_potential)
-    return x, ham, own_potential
+    return density, ham, own_potential
 
 
 def solution(mesh):

time: 255 us -> 191 us (0.75)
  waiting for transfers between devices: 120 us -> 46.8 us
  starting transfers between devices: 61.8 us -> 86.3 us
  Pallas kernels: 62.7 us -> 51.9 us
  local copies, waits for them, and re-layouts: 5.14 us -> 1.15 us
    ppermute x18 -> x20, waiting for transfers between devices: 120 us -> 46.8 us  [passed_along(): return lax.ppermute(x, axis, pairs)]
    ppermute x18 -> x20, starting transfers between devices: 61.8 us -> 86.3 us  [passed_along(): return lax.ppermute(x, axis, pairs)]
    pallas_call x4 -> x9, Pallas kernels: 29.9 us -> 22.7 us  [the longest x4 16.1 us: local_step(): pl.pallas_call(local_kernel, in_specs=[pl.BlockSpec(memory_space=pltpu.SM...]
    unnamed x8 -> x11, local copies, waits for them, and re-layouts: 4.24 us -> 0.12 us
    pallas_call x2, Pallas kernels: 16.9 us -> 13 us  [domain_step(): pl.pallas_call(functools.partial(domain_kernel, slots, has_base, factor),...]
  transfers between devices with their start and end apart: 18 -> 20, of which waited for: 7 -> 5; matrix products, arithmetic and copies ran while one was open for 0% -> 1% of each run, Pallas kernels for 15% -> 27%
where the time goes in v1:
time: 191 us
  starting transfers between devices  86.3 us (45%)
  Pallas kernels  51.9 us (27%)
  waiting for transfers between devices  46.8 us (25%)
  other arithmetic  3.21 us (2%)
    ppermute x20, starting transfers between devices, passed_along(): return lax.ppermute(x, axis, pairs)  86.3 us
    ppermute x20, waiting for transfers between devices, passed_along(): return lax.ppermute(x, axis, pairs)  46.8 us
    pallas_call x4, Pallas kernels, local_step(): pl.pallas_call(local_kernel, in_specs=[pl.BlockSpec(memory_space=pltpu.SM...  16.1 us
    pallas_call x2, Pallas kernels, domain_step(): pl.pallas_call(functools.partial(domain_kernel, slots, has_base, factor),...  13 us
    pallas_call x1, Pallas kernels, block_step(): pl.pallas_call(functools.partial(block_kernel, slots), in_specs=[smem, vm...  6.58 us
    pallas_call x4, Pallas kernels, border_step(): pl.pallas_call(border_kernel, in_specs=[pl.BlockSpec(memory_space=pltpu.S...  4.56 us
    pallas_call x1, Pallas kernels, plan_step(): pl.pallas_call(functools.partial(plan_kernel, moves, (rows, band_count, g...  4.29 us
  transfers between devices with their start and end apart: 20, of which 5 were waited for; matrix products, arithmetic and copies ran while one was open for 1% of the time, Pallas kernels for 27%

profile of v1, /device:TPU:56, one launch (start us, length us, event | category | flops | bytes accessed | tf_op | source)
XLA Modules:
  0.0 190.5 jit_solution(144980461438726399)
XLA Ops:
  0.6 2.3 %convert_element_type.3.narrow_ref = bf16[5,3,256,256]{3,2,1,0:T(8,128)(2,1)S(1)} convert(f32[5,3,256,256]{3,2,1,0:T(8,128)} %x_ref.1) | non-fusion elementwise | flops 983040 | bytes 5898240 | tf_op jit(solution)/shard_map/convert_element_type | solution.py:546
  3.1 3.7 %collective-permute-start.1 = (bf16[3,256,256]{2,1,0:T(8,128)(2,1)S(1)}, bf16[3,256,256]{2,1,0:T(8,128)(2,1)S(1)}, u32[]{:S(2)}, u32[]{:S(2)}) collective-permute-start(bf16[3,256,256]{2,1,0:T(8,128)(2,1)S(1)} %pad_maximum_fusion.down_ref.before_ref), channel_id=1, source_target_pairs={{1,0},{2,1},{3,2},{4,3},{5,4},{6,5},{7,6},{8,7},{9,8},{10,9},{11,1... | collective-permute-start | bytes 1179656 | tf_op jit(solution)/shard_map/ppermute | solution.py:26
  8.8 4.3 %plan_step.1 = (bf16[768,1280]{1,0:T(8,128)(2,1)S(1)}, bf16[768,1280]{1,0:T(8,128)(2,1)S(1)}, s32[16]{0:T(128)S(1)}) custom-call(s32[5,384]{1,0:T(8,128)} %bitcast.32, bf16[3,768,1280]{2,1,0:T(8,128)(2,1)} %refs_0_.1), custom_call_target="tpu_custom_call" | custom-call | tf_op jit(solution)/shard_map/plan_step/pallas_call | solution.py:227
  13.1 3.8 %collective-permute-start.8 = (bf16[768,1280]{1,0:T(8,128)(2,1)S(1)}, bf16[768,1280]{1,0:T(8,128)(2,1)S(1)}, u32[]{:S(2)}, u32[]{:S(2)}) collective-permute-start(bf16[768,1280]{1,0:T(8,128)(2,1)S(1)} %get-tuple-element.55), channel_id=1, source_target_pairs={{0,8},{8,16},{16,24},{24,32},{32,40},{40,48},{48,56},{56,64},{64,7... | collective-permute-start | bytes 5898248 | tf_op jit(solution)/shard_map/ppermute | solution.py:26
  16.9 4.2 %collective-permute-start.10 = (bf16[768,1280]{1,0:T(8,128)(2,1)S(1)}, bf16[768,1280]{1,0:T(8,128)(2,1)S(1)}, u32[]{:S(2)}, u32[]{:S(2)}) collective-permute-start(bf16[768,1280]{1,0:T(8,128)(2,1)S(1)} %get-tuple-element.56), channel_id=1, source_target_pairs={{8,0},{16,8},{24,16},{32,24},{40,32},{48,40},{56,48},{64,56},{72,6... | collective-permute-start | bytes 5898248 | tf_op jit(solution)/shard_map/ppermute | solution.py:26
  22.0 3.8 %local_step.4 = (f32[5,3,256,256]{3,2,1,0:T(8,128)S(1)}, bf16[5,3,256,256]{3,2,1,0:T(8,128)(2,1)S(1)}) custom-call(s32[1]{0:T(128)} %get-tuple-element.81.choice_ref, f32[5,3,256,256]{3,2,1,0:T(8,128)S(1)} %copy-done, f32[6,256,256]{2,1,0:T(8,128)S(1)} %bitcast_dynamic-update-slice_fusion.edge_ref, ...), custom_call_target="tpu_custom_call" | custom-call | flops 2013265920 | bytes 3932160 | tf_op jit(solution)/shard_map/local_step/pallas_call | solution.py:91
  28.9 7.6 %collective-permute-start.3 = (bf16[3,256,256]{2,1,0:T(8,128)(2,1)S(1)}, bf16[3,256,256]{2,1,0:T(8,128)(2,1)S(1)}, u32[]{:S(2)}, u32[]{:S(2)}) collective-permute-start(bf16[3,256,256]{2,1,0:T(8,128)(2,1)S(1)} %get-tuple-element.37.down_ref.before_ref), channel_id=1, source_target_pairs={{1,0},{2,1},{3,2},{4,3},{5,4},{6,5},{7,6},{8,7},{9,8},{10,9},{11,1... | collective-permute-start | bytes 1179656 | tf_op jit(solution)/shard_map/ppermute | solution.py:26
  36.5 3.0 %pick_step.1 = (bf16[768,1280]{1,0:T(8,128)(2,1)S(1)}, bf16[768,1280]{1,0:T(8,128)(2,1)S(1)}) custom-call(s32[16]{0:T(128)S(1)} %get-tuple-element.51.table_ref, bf16[3,768,1280]{2,1,0:T(8,128)(2,1)} %refs_0_.1), custom_call_target="tpu_custom_call" | custom-call | tf_op jit(solution)/shard_map/pick_step/pallas_call | solution.py:281
  41.4 6.3 %collective-permute-start.13 = (bf16[768,1280]{1,0:T(8,128)(2,1)S(1)}, bf16[768,1280]{1,0:T(8,128)(2,1)S(1)}, u32[]{:S(2)}, u32[]{:S(2)}) collective-permute-start(bf16[768,1280]{1,0:T(8,128)(2,1)S(1)} %get-tuple-element.59), channel_id=1, source_target_pairs={{8,0},{16,8},{24,16},{32,24},{40,32},{48,40},{56,48},{64,56},{72,6... | collective-permute-start | bytes 5898248 | tf_op jit(solution)/shard_map/ppermute | solution.py:26
  47.7 3.9 %local_step.5 = (f32[5,3,256,256]{3,2,1,0:T(8,128)S(1)}, bf16[5,3,256,256]{3,2,1,0:T(8,128)(2,1)S(1)}) custom-call(s32[1]{0:T(128)} %get-tuple-element.84.choice_ref, f32[5,3,256,256]{3,2,1,0:T(8,128)S(1)} %get-tuple-element.34.x_ref, f32[6,256,256]{2,1,0:T(8,128)S(1)} %get-tuple-element.35.edge_ref, ...), custom_call_target="tpu_custom_call" | custom-call | flops 2013265920 | bytes 3932160 | tf_op jit(solution)/shard_map/local_step/pallas_call | solution.py:91
  54.7 9.4 %collective-permute-done.4.top_ref = bf16[3,256,256]{2,1,0:T(8,128)(2,1)S(1)} collective-permute-done((bf16[3,256,256]{2,1,0:T(8,128)(2,1)S(1)}, bf16[3,256,256]{2,1,0:T(8,128)(2,1)S(1)}, u32[]{:S(2)}, u32[]{:S(2)}) %collective-permute-start.4) | collective-permute-done | bytes 393248 | tf_op jit(solution)/shard_map/ppermute | solution.py:26
  66.0 4.2 %local_step.6 = (f32[5,3,256,256]{3,2,1,0:T(8,128)S(1)}, bf16[5,3,256,256]{3,2,1,0:T(8,128)(2,1)S(1)}) custom-call(s32[1]{0:T(128)} %get-tuple-element.82.choice_ref, f32[5,3,256,256]{3,2,1,0:T(8,128)S(1)} %get-tuple-element.39.x_ref, f32[6,256,256]{2,1,0:T(8,128)S(1)} %get-tuple-element.40.edge_ref, ...), custom_call_target="tpu_custom_call" | custom-call | flops 2013265920 | bytes 3932160 | tf_op jit(solution)/shard_map/local_step/pallas_call | solution.py:91
  76.6 8.1 %collective-permute-start.15 = (bf16[512,1280]{1,0:T(8,128)(2,1)S(1)}, bf16[512,1280]{1,0:T(8,128)(2,1)S(1)}, u32[]{:S(2)}, u32[]{:S(2)}) collective-permute-start(bf16[512,1280]{1,0:T(8,128)(2,1)S(1)} %slice.113), channel_id=1, source_target_pairs={{8,0},{16,8},{24,16},{32,24},{40,32},{48,40},{56,48},{64,56},{72,6... | collective-permute-start | bytes 3932168 | tf_op jit(solution)/shard_map/ppermute | solution.py:26
  84.7 7.8 %collective-permute-start.7 = (bf16[3,256,256]{2,1,0:T(8,128)(2,1)S(1)}, bf16[3,256,256]{2,1,0:T(8,128)(2,1)S(1)}, u32[]{:S(2)}, u32[]{:S(2)}) collective-permute-start(bf16[3,256,256]{2,1,0:T(8,128)(2,1)S(1)} %get-tuple-element.47.down_ref.before_ref), channel_id=1, source_target_pairs={{1,0},{2,1},{3,2},{4,3},{5,4},{6,5},{7,6},{8,7},{9,8},{10,9},{11,1... | collective-permute-start | bytes 1179656 | tf_op jit(solution)/shard_map/ppermute | solution.py:26
  92.6 4.2 %local_step.7 = (f32[5,3,256,256]{3,2,1,0:T(8,128)S(1)}, bf16[5,3,256,256]{3,2,1,0:T(8,128)(2,1)S(1)}) custom-call(s32[1]{0:T(128)} %get-tuple-element.83.choice_ref, f32[5,3,256,256]{3,2,1,0:T(8,128)S(1)} %get-tuple-element.44.x_ref, f32[6,256,256]{2,1,0:T(8,128)S(1)} %get-tuple-element.45.edge_ref, ...), custom_call_target="tpu_custom_call" | custom-call | flops 2013265920 | bytes 3932160 | tf_op jit(solution)/shard_map/local_step/pallas_call | solution.py:91
  103.1 14.5 %collective-permute-done.12.refs_1_ = bf16[768,1280]{1,0:T(8,128)(2,1)S(1)} collective-permute-done((bf16[768,1280]{1,0:T(8,128)(2,1)S(1)}, bf16[768,1280]{1,0:T(8,128)(2,1)S(1)}, u32[]{:S(2)}, u32[]{:S(2)}) %collective-permute-start.12) | collective-permute-done | bytes 1966112 | tf_op jit(solution)/shard_map/ppermute | solution.py:26
  117.6 6.2 %collective-permute-start.11 = (bf16[256,1280]{1,0:T(8,128)(2,1)S(1)}, bf16[256,1280]{1,0:T(8,128)(2,1)S(1)}, u32[]{:S(2)}, u32[]{:S(2)}) collective-permute-start(bf16[256,1280]{1,0:T(8,128)(2,1)S(1)} %slice.111), channel_id=1, source_target_pairs={{8,0},{16,8},{24,16},{32,24},{40,32},{48,40},{56,48},{64,56},{72,6... | collective-permute-start | bytes 1966088 | tf_op jit(solution)/shard_map/ppermute | solution.py:26
  123.8 5.6 %domain_step.2 = (f32[5,3,256,256]{3,2,1,0:T(8,128)S(1)}, f32[3,1,768]{2,1,0:T(1,128)S(1)}) custom-call(s32[16]{0:T(128)S(1)} %get-tuple-element.51.table_ref, bf16[5,3,256,256]{3,2,1,0:T(8,128)(2,1)S(1)} %get-tuple-element.52.main_ref, bf16[3,256,256]{2,1,0:T(8,128)(2,1)S(1)} %get-tuple-element.53.down_ref, ...), custom_call_target="tpu_custom_call" | custom-call | flops 7247757312 | bytes 11796480 | tf_op jit(solution)/shard_map/domain_step/pallas_call | solution.py:398
  129.5 6.9 %collective-permute-start.18 = (f32[768]{0:T(1024)S(1)}, f32[768]{0:T(1024)S(1)}, u32[]{:S(2)}, u32[]{:S(2)}) collective-permute-start(f32[768]{0:T(1024)S(1)} %get-tuple-element.65), channel_id=1, source_target_pairs={{0,8},{8,16},{16,24},{24,32},{32,40},{40,48},{48,56},{56,64},{64,7... | collective-permute-start | bytes 9224 | tf_op jit(solution)/shard_map/ppermute | solution.py:26
  136.4 20.7 %collective-permute-done.9.refs_0_ = bf16[256,1280]{1,0:T(8,128)(2,1)S(1)} collective-permute-done((bf16[256,1280]{1,0:T(8,128)(2,1)S(1)}, bf16[256,1280]{1,0:T(8,128)(2,1)S(1)}, u32[]{:S(2)}, u32[]{:S(2)}) %collective-permute-start.9) | collective-permute-done | bytes 655392 | tf_op jit(solution)/shard_map/ppermute | solution.py:26
  157.1 8.1 %collective-permute-start.19 = (f32[768]{0:T(1024)S(1)}, f32[768]{0:T(1024)S(1)}, u32[]{:S(2)}, u32[]{:S(2)}) collective-permute-start(f32[768]{0:T(1024)S(1)} %get-tuple-element.67), channel_id=1, source_target_pairs={{8,0},{16,8},{24,16},{32,24},{40,32},{48,40},{56,48},{64,56},{72,6... | collective-permute-start | bytes 9224 | tf_op jit(solution)/shard_map/ppermute | solution.py:26
  167.5 7.4 %domain_step.3 = (f32[5,3,256,256]{3,2,1,0:T(8,128)S(1)}, f32[2,1,512]{2,1,0:T(1,128)S(1)}) custom-call(s32[16]{0:T(128)S(1)} %get-tuple-element.51.table_ref, bf16[5,3,256,256]{3,2,1,0:T(8,128)(2,1)S(1)} %get-tuple-element.52.main_ref, bf16[3,256,256]{2,1,0:T(8,128)(2,1)S(1)} %get-tuple-element.53.down_ref, ...), custom_call_target="tpu_custom_call" | custom-call | flops 3221225472 | bytes 8519680 | tf_op jit(solution)/shard_map/domain_step/pallas_call | solution.py:398
  176.9 6.3 %collective-permute-start.17 = (f32[768]{0:T(1024)S(1)}, f32[768]{0:T(1024)S(1)}, u32[]{:S(2)}, u32[]{:S(2)}) collective-permute-start(f32[768]{0:T(1024)S(1)} %get-tuple-element.69), channel_id=1, source_target_pairs={{16,0},{24,8},{32,16},{40,24},{48,32},{56,40},{64,48},{72,56},{80,... | collective-permute-start | bytes 9224 | tf_op jit(solution)/shard_map/ppermute | solution.py:26
  183.2 6.6 %block_step.1 = f32[5,3,256,256]{3,2,1,0:T(8,128)} custom-call(s32[16]{0:T(128)S(1)} %get-tuple-element.51.table_ref, bf16[2,256,1280]{2,1,0:T(8,128)(2,1)S(1)} %get-tuple-element.57.psi_ref, f32[5,3,256,256]{3,2,1,0:T(8,128)S(1)} %get-tuple-element.61.base_ref, bf16[256,1280]{1,0:T(8,128)(2,1)S(1)} %collective-permute-done.9.refs_0_, ...), custom_call_target="tpu_custom_call" | custom-call | flops 805306368 | bytes 10485760 | tf_op jit(solution)/shard_map/block_step/pallas_call | solution.py:504
  (56 shorter events, 30.4 us)
Async XLA Ops:
  3.1 22.7 %collective-permute-start.1 = (bf16[3,256,256]{2,1,0:T(8,128)(2,1)S(1)}, bf16[3,256,256]{2,1,0:T(8,128)(2,1)S(1)}, u32[]{:S(2)}, u32[]{:S(2)}) collective-permute-start(bf16[3,256,256]{2,1,0:T(8,128)(2,1)S(1)} %pad_maximum_fusion.down_ref.before_ref), channel_id=1, source_target_pairs={{1,0},{2,1},{3,2},{4,3},{5,4},{6,5},{7,6},{8,7},{9,8},{10,9},{11,1... | collective-permute-start | bytes 1179656 | tf_op jit(solution)/shard_map/ppermute | solution.py:26
  6.8 19.0 %collective-permute-start = (bf16[3,256,256]{2,1,0:T(8,128)(2,1)S(1)}, bf16[3,256,256]{2,1,0:T(8,128)(2,1)S(1)}, u32[]{:S(2)}, u32[]{:S(2)}) collective-permute-start(bf16[3,256,256]{2,1,0:T(8,128)(2,1)S(1)} %pad_maximum_fusion.1.up_ref), channel_id=1, source_target_pairs={{0,1},{1,2},{2,3},{3,4},{4,5},{5,6},{6,7},{7,8},{8,9},{9,10},{10,1... | collective-permute-start | bytes 1179656 | tf_op jit(solution)/shard_map/ppermute | solution.py:26
  8.7 12.4 %copy-start = (f32[5,3,256,256]{3,2,1,0:T(8,128)S(1)}, f32[5,3,256,256]{3,2,1,0:T(8,128)}, u32[]{:S(2)}) copy-start(f32[5,3,256,256]{3,2,1,0:T(8,128)} %x_ref.1) | copy-start | bytes 11796484
  8.7 12.4 %copy-start.1 = (s32[4]{0:T(128)S(1)}, s32[4]{0:T(128)}, u32[]{:S(2)}) copy-start(s32[4]{0:T(128)} %param.5) | copy-start | bytes 52
  13.1 61.4 %collective-permute-start.8 = (bf16[768,1280]{1,0:T(8,128)(2,1)S(1)}, bf16[768,1280]{1,0:T(8,128)(2,1)S(1)}, u32[]{:S(2)}, u32[]{:S(2)}) collective-permute-start(bf16[768,1280]{1,0:T(8,128)(2,1)S(1)} %get-tuple-element.55), channel_id=1, source_target_pairs={{0,8},{8,16},{16,24},{24,32},{32,40},{40,48},{48,56},{56,64},{64,7... | collective-permute-start | bytes 5898248 | tf_op jit(solution)/shard_map/ppermute | solution.py:26
  16.9 59.6 %collective-permute-start.10 = (bf16[768,1280]{1,0:T(8,128)(2,1)S(1)}, bf16[768,1280]{1,0:T(8,128)(2,1)S(1)}, u32[]{:S(2)}, u32[]{:S(2)}) collective-permute-start(bf16[768,1280]{1,0:T(8,128)(2,1)S(1)} %get-tuple-element.56), channel_id=1, source_target_pairs={{8,0},{16,8},{24,16},{32,24},{40,32},{48,40},{56,48},{64,56},{72,6... | collective-permute-start | bytes 5898248 | tf_op jit(solution)/shard_map/ppermute | solution.py:26
  27.0 14.5 %collective-permute-start.2 = (bf16[3,256,256]{2,1,0:T(8,128)(2,1)S(1)}, bf16[3,256,256]{2,1,0:T(8,128)(2,1)S(1)}, u32[]{:S(2)}, u32[]{:S(2)}) collective-permute-start(bf16[3,256,256]{2,1,0:T(8,128)(2,1)S(1)} %get-tuple-element.38.up_ref), channel_id=1, source_target_pairs={{0,1},{1,2},{2,3},{3,4},{4,5},{5,6},{6,7},{7,8},{8,9},{9,10},{10,1... | collective-permute-start | bytes 1179656 | tf_op jit(solution)/shard_map/ppermute | solution.py:26
  28.9 22.7 %collective-permute-start.3 = (bf16[3,256,256]{2,1,0:T(8,128)(2,1)S(1)}, bf16[3,256,256]{2,1,0:T(8,128)(2,1)S(1)}, u32[]{:S(2)}, u32[]{:S(2)}) collective-permute-start(bf16[3,256,256]{2,1,0:T(8,128)(2,1)S(1)} %get-tuple-element.37.down_ref.before_ref), channel_id=1, source_target_pairs={{1,0},{2,1},{3,2},{4,3},{5,4},{6,5},{7,6},{8,7},{9,8},{10,9},{11,1... | collective-permute-start | bytes 1179656 | tf_op jit(solution)/shard_map/ppermute | solution.py:26
  39.5 78.1 %collective-permute-start.12 = (bf16[768,1280]{1,0:T(8,128)(2,1)S(1)}, bf16[768,1280]{1,0:T(8,128)(2,1)S(1)}, u32[]{:S(2)}, u32[]{:S(2)}) collective-permute-start(bf16[768,1280]{1,0:T(8,128)(2,1)S(1)} %get-tuple-element.58), channel_id=1, source_target_pairs={{0,8},{8,16},{16,24},{24,32},{32,40},{40,48},{48,56},{56,64},{64,7... | collective-permute-start | bytes 5898248 | tf_op jit(solution)/shard_map/ppermute | solution.py:26
  41.4 82.4 %collective-permute-start.13 = (bf16[768,1280]{1,0:T(8,128)(2,1)S(1)}, bf16[768,1280]{1,0:T(8,128)(2,1)S(1)}, u32[]{:S(2)}, u32[]{:S(2)}) collective-permute-start(bf16[768,1280]{1,0:T(8,128)(2,1)S(1)} %get-tuple-element.59), channel_id=1, source_target_pairs={{8,0},{16,8},{24,16},{32,24},{40,32},{48,40},{56,48},{64,56},{72,6... | collective-permute-start | bytes 5898248 | tf_op jit(solution)/shard_map/ppermute | solution.py:26
  52.8 11.3 %collective-permute-start.4 = (bf16[3,256,256]{2,1,0:T(8,128)(2,1)S(1)}, bf16[3,256,256]{2,1,0:T(8,128)(2,1)S(1)}, u32[]{:S(2)}, u32[]{:S(2)}) collective-permute-start(bf16[3,256,256]{2,1,0:T(8,128)(2,1)S(1)} %get-tuple-element.43.up_ref), channel_id=1, source_target_pairs={{0,1},{1,2},{2,3},{3,4},{4,5},{5,6},{6,7},{7,8},{8,9},{9,10},{10,1... | collective-permute-start | bytes 1179656 | tf_op jit(solution)/shard_map/ppermute | solution.py:26
  64.1 7.2 %collective-permute-start.5 = (bf16[3,256,256]{2,1,0:T(8,128)(2,1)S(1)}, bf16[3,256,256]{2,1,0:T(8,128)(2,1)S(1)}, u32[]{:S(2)}, u32[]{:S(2)}) collective-permute-start(bf16[3,256,256]{2,1,0:T(8,128)(2,1)S(1)} %get-tuple-element.42.down_ref.before_ref), channel_id=1, source_target_pairs={{1,0},{2,1},{3,2},{4,3},{5,4},{6,5},{7,6},{8,7},{9,8},{10,9},{11,1... | collective-permute-start | bytes 1179656 | tf_op jit(solution)/shard_map/ppermute | solution.py:26
  72.5 12.2 %collective-permute-start.6 = (bf16[3,256,256]{2,1,0:T(8,128)(2,1)S(1)}, bf16[3,256,256]{2,1,0:T(8,128)(2,1)S(1)}, u32[]{:S(2)}, u32[]{:S(2)}) collective-permute-start(bf16[3,256,256]{2,1,0:T(8,128)(2,1)S(1)} %get-tuple-element.48.up_ref), channel_id=1, source_target_pairs={{0,1},{1,2},{2,3},{3,4},{4,5},{5,6},{6,7},{7,8},{8,9},{9,10},{10,1... | collective-permute-start | bytes 1179656 | tf_op jit(solution)/shard_map/ppermute | solution.py:26
  74.5 93.0 %collective-permute-start.14 = (bf16[512,1280]{1,0:T(8,128)(2,1)S(1)}, bf16[512,1280]{1,0:T(8,128)(2,1)S(1)}, u32[]{:S(2)}, u32[]{:S(2)}) collective-permute-start(bf16[512,1280]{1,0:T(8,128)(2,1)S(1)} %slice.112), channel_id=1, source_target_pairs={{0,8},{8,16},{16,24},{24,32},{32,40},{40,48},{48,56},{56,64},{64,7... | collective-permute-start | bytes 3932168 | tf_op jit(solution)/shard_map/ppermute | solution.py:26
  76.6 91.0 %collective-permute-start.15 = (bf16[512,1280]{1,0:T(8,128)(2,1)S(1)}, bf16[512,1280]{1,0:T(8,128)(2,1)S(1)}, u32[]{:S(2)}, u32[]{:S(2)}) collective-permute-start(bf16[512,1280]{1,0:T(8,128)(2,1)S(1)} %slice.113), channel_id=1, source_target_pairs={{8,0},{16,8},{24,16},{32,24},{40,32},{48,40},{56,48},{64,56},{72,6... | collective-permute-start | bytes 3932168 | tf_op jit(solution)/shard_map/ppermute | solution.py:26
  84.7 13.1 %collective-permute-start.7 = (bf16[3,256,256]{2,1,0:T(8,128)(2,1)S(1)}, bf16[3,256,256]{2,1,0:T(8,128)(2,1)S(1)}, u32[]{:S(2)}, u32[]{:S(2)}) collective-permute-start(bf16[3,256,256]{2,1,0:T(8,128)(2,1)S(1)} %get-tuple-element.47.down_ref.before_ref), channel_id=1, source_target_pairs={{1,0},{2,1},{3,2},{4,3},{5,4},{6,5},{7,6},{8,7},{9,8},{10,9},{11,1... | collective-permute-start | bytes 1179656 | tf_op jit(solution)/shard_map/ppermute | solution.py:26
  101.1 56.0 %collective-permute-start.9 = (bf16[256,1280]{1,0:T(8,128)(2,1)S(1)}, bf16[256,1280]{1,0:T(8,128)(2,1)S(1)}, u32[]{:S(2)}, u32[]{:S(2)}) collective-permute-start(bf16[256,1280]{1,0:T(8,128)(2,1)S(1)} %slice.110), channel_id=1, source_target_pairs={{0,8},{8,16},{16,24},{24,32},{32,40},{40,48},{48,56},{56,64},{64,7... | collective-permute-start | bytes 1966088 | tf_op jit(solution)/shard_map/ppermute | solution.py:26
  117.6 47.6 %collective-permute-start.11 = (bf16[256,1280]{1,0:T(8,128)(2,1)S(1)}, bf16[256,1280]{1,0:T(8,128)(2,1)S(1)}, u32[]{:S(2)}, u32[]{:S(2)}) collective-permute-start(bf16[256,1280]{1,0:T(8,128)(2,1)S(1)} %slice.111), channel_id=1, source_target_pairs={{8,0},{16,8},{24,16},{32,24},{40,32},{48,40},{56,48},{64,56},{72,6... | collective-permute-start | bytes 1966088 | tf_op jit(solution)/shard_map/ppermute | solution.py:26
  129.5 60.3 %collective-permute-start.18 = (f32[768]{0:T(1024)S(1)}, f32[768]{0:T(1024)S(1)}, u32[]{:S(2)}, u32[]{:S(2)}) collective-permute-start(f32[768]{0:T(1024)S(1)} %get-tuple-element.65), channel_id=1, source_target_pairs={{0,8},{8,16},{16,24},{24,32},{32,40},{40,48},{48,56},{56,64},{64,7... | collective-permute-start | bytes 9224 | tf_op jit(solution)/shard_map/ppermute | solution.py:26
  157.1 32.7 %collective-permute-start.19 = (f32[768]{0:T(1024)S(1)}, f32[768]{0:T(1024)S(1)}, u32[]{:S(2)}, u32[]{:S(2)}) collective-permute-start(f32[768]{0:T(1024)S(1)} %get-tuple-element.67), channel_id=1, source_target_pairs={{8,0},{16,8},{24,16},{32,24},{40,32},{48,40},{56,48},{64,56},{72,6... | collective-permute-start | bytes 9224 | tf_op jit(solution)/shard_map/ppermute | solution.py:26
  174.9 14.9 %collective-permute-start.16 = (f32[768]{0:T(1024)S(1)}, f32[768]{0:T(1024)S(1)}, u32[]{:S(2)}, u32[]{:S(2)}) collective-permute-start(f32[768]{0:T(1024)S(1)} %get-tuple-element.68), channel_id=1, source_target_pairs={{0,16},{8,24},{16,32},{24,40},{32,48},{40,56},{48,64},{56,72},{64,... | collective-permute-start | bytes 9224 | tf_op jit(solution)/shard_map/ppermute | solution.py:26
  176.9 13.0 %collective-permute-start.17 = (f32[768]{0:T(1024)S(1)}, f32[768]{0:T(1024)S(1)}, u32[]{:S(2)}, u32[]{:S(2)}) collective-permute-start(f32[768]{0:T(1024)S(1)} %get-tuple-element.69), channel_id=1, source_target_pairs={{16,0},{24,8},{32,16},{40,24},{48,32},{56,40},{64,48},{72,56},{80,... | collective-permute-start | bytes 9224 | tf_op jit(solution)/shard_map/ppermute | solution.py:26

commit v2 on v1

--- a/solution.py
+++ b/solution.py
@@ -24,6 +24,31 @@
     count = lax.axis_size(axis)
     pairs = [(i, i + by) for i in range(count) if 0 <= i + by < count]
     return lax.ppermute(x, axis, pairs)
+
+
+DETOUR = ((0, 2), (1, 4))
+
+
+def detour_out(band_count, grid_count):
+    last = grid_count - 1
+    pairs = []
+    for b in range(band_count):
+        for g, via in DETOUR:
+            if b + 1 < band_count:
+                pairs.append((b * grid_count + g, (b + 1) * grid_count + via))
+            if b > 0:
+                pairs.append((b * grid_count + last - g, (b - 1) * grid_count + last - via))
+    return pairs
+
+
+def detour_back(band_count, grid_count):
+    last = grid_count - 1
+    pairs = []
+    for b in range(band_count):
+        for g, via in DETOUR:
+            pairs.append((b * grid_count + via, b * grid_count + g))
+            pairs.append((b * grid_count + last - via, b * grid_count + last - g))
+    return pairs
 
 
 def dot32(a, b, dims):
@@ -97,7 +122,7 @@
             jax.ShapeDtypeStruct(x.shape, jnp.bfloat16),
         ],
         scratch_shapes=[pltpu.VMEM((rows + 4, 3, BS, BS), jnp.bfloat16)],
-        compiler_params=pltpu.CompilerParams(vmem_limit_bytes=22 << 20),
+        compiler_params=pltpu.CompilerParams(vmem_limit_bytes=8 << 20),
         cost_estimate=pl.CostEstimate(
             flops=rows * 12 * 2 * BS**3, bytes_accessed=x.size * 4, transcendentals=0
         ),
@@ -138,7 +163,7 @@
         in_specs=[pl.BlockSpec(memory_space=pltpu.SMEM)] + [vmem] * 4,
         out_specs=[vmem] * 3,
         out_shape=[jax.ShapeDtypeStruct((6, BS, BS), jnp.float32), edge, edge],
-        compiler_params=pltpu.CompilerParams(vmem_limit_bytes=12 << 20),
+        compiler_params=pltpu.CompilerParams(vmem_limit_bytes=4 << 20),
         cost_estimate=pl.CostEstimate(
             flops=9 * 2 * BS**3, bytes_accessed=x.size, transcendentals=0
         ),
@@ -409,7 +434,7 @@
             pltpu.VMEM((rows, 3 * BS, BS), jnp.bfloat16),
             pltpu.SemaphoreType.DMA((number,)),
         ],
-        compiler_params=pltpu.CompilerParams(vmem_limit_bytes=(17 << 20) + number * points * width * 2),
+        compiler_params=pltpu.CompilerParams(vmem_limit_bytes=(8 << 20) + number * points * width * 2),
         cost_estimate=pl.CostEstimate(
             flops=number * 24 * 2 * points * BS * BS,
             bytes_accessed=number * points * width * 2 + rows * 3 * BS * BS * 6,
@@ -420,12 +445,26 @@
 
 
 def potential_kernel(slots, factor, table_ref, main_ref, down_ref, up_ref, *refs):
-    basis_refs = refs[: len(slots)]
-    psi_out, pot_out, phi, stack = refs[len(slots) :]
+    *basis_refs, detour_ref = refs[: len(slots) + 1]
+    psi_out, phi_out, pot_out, phi, stack = refs[len(slots) + 1 :]
+    points, width = phi.shape[1:]
+    pad = phi_out.shape[2] - width
+    grid = lax.axis_index("grid")
+    last = lax.axis_size("grid") - 1
+    detoured = (grid <= 1, grid >= last - 1)
     fill_stack((main_ref, down_ref, up_ref), stack)
     pot_out[...] = jnp.zeros_like(pot_out)
     for n in range(len(slots)):
-        phi[n] = basis_refs[n][...]
+
+        @pl.when(detoured[n])
+        def _():
+            phi[n] = detour_ref[...]
+
+        @pl.when(jnp.logical_not(detoured[n]))
+        def _():
+            phi[n] = basis_refs[n][...]
+
+        phi_out[n, :, 0:pad] = jnp.zeros((points, pad), jnp.bfloat16)
 
     @pl.loop(0, len(slots))
     def _(n):
@@ -435,41 +474,40 @@
         @pl.when(blocks > 0)
         def _():
             blank_tail(phi, n, blocks)
+            phi_out[n, :, pad:] = phi[n]
             potential_of_slot(phi, n, first, stack, pot_out, lambda here: psi_out.at[n, here], factor)
 
 
-def potential_step(slots, table, tiles, arrays, factor):
+def potential_step(slots, table, tiles, arrays, detour, factor):
     rows = tiles[0].shape[0]
     points, width = arrays[-1].shape
     number = len(arrays)
     smem = pl.BlockSpec(memory_space=pltpu.SMEM)
     vmem = pl.BlockSpec(memory_space=pltpu.VMEM)
-    hbm = pl.BlockSpec(memory_space=pl.ANY)
     return pl.pallas_call(
         functools.partial(potential_kernel, slots, factor),
-        in_specs=[smem] + [vmem] * (3 + number),
-        out_specs=[vmem, vmem],
+        in_specs=[smem] + [vmem] * (4 + number),
+        out_specs=[vmem] * 3,
         out_shape=[
             jax.ShapeDtypeStruct((number, points, width), jnp.bfloat16),
+            jax.ShapeDtypeStruct((number, points, width + 2 * BS), jnp.bfloat16),
             jax.ShapeDtypeStruct((number, 1, points), jnp.float32),
         ],
         scratch_shapes=[
             pltpu.VMEM((number, points, width), jnp.bfloat16),
             pltpu.VMEM((rows, 3 * BS, BS), jnp.bfloat16),
         ],
-        compiler_params=pltpu.CompilerParams(vmem_limit_bytes=16 << 20),
+        compiler_params=pltpu.CompilerParams(vmem_limit_bytes=10 << 20),
         cost_estimate=pl.CostEstimate(
             flops=number * 12 * 2 * points * BS * BS,
             bytes_accessed=number * points * width * 4,
             transcendentals=number * points,
         ),
         name="potential_step",
-    )(table, *tiles, *arrays)
-
-
-def block_kernel(slots, table_ref, psi_ref, base_ref, *refs):
-    basis_refs = refs[: len(slots)]
-    ham_out, ham, sems = refs[len(slots) :]
+    )(table, *tiles, *arrays, detour)
+
+
+def block_kernel(slots, table_ref, psi_ref, phi_ref, base_ref, ham_out, ham, sems):
     rows = ham.shape[0]
 
     def send(r):
@@ -483,41 +521,39 @@
 
             @pl.when((k >= 0) & (k < blocks))
             def _():
-                left = psi_ref[n, :, pl.ds(pl.multiple_of(k * BS, BS), BS)]
-                for gap in range(3):
-
-                    @pl.when(k >= gap)
-                    def _():
-                        where = pl.ds(pl.multiple_of((k - gap) * BS, BS), BS)
-                        ham[r, 2 - gap] += dot32(left, basis_refs[n][:, where], TN)
+                offset = pl.multiple_of(k * BS, BS)
+                left = psi_ref[n, :, pl.ds(offset, BS)]
+                piece = dot32(left, phi_ref[n, :, pl.ds(offset, 3 * BS)], TN)
+                for q in range(3):
+                    ham[r, q] += piece[:, q * BS : (q + 1) * BS]
 
         send(r).start()
     for r in range(rows):
         send(r).wait()
 
 
-def block_step(slots, table, psi, base, arrays):
+def block_step(slots, table, psi, phi, base):
     number, points, width = psi.shape
     rows = base.shape[0]
     smem = pl.BlockSpec(memory_space=pltpu.SMEM)
     vmem = pl.BlockSpec(memory_space=pltpu.VMEM)
     return pl.pallas_call(
         functools.partial(block_kernel, slots),
-        in_specs=[smem, vmem, vmem] + [vmem] * number,
+        in_specs=[smem, vmem, vmem, vmem],
         out_specs=pl.BlockSpec(memory_space=pltpu.HBM),
         out_shape=pltpu.HBM(base.shape, jnp.float32),
         scratch_shapes=[
             pltpu.VMEM(base.shape, jnp.float32),
             pltpu.SemaphoreType.DMA((rows,)),
         ],
-        compiler_params=pltpu.CompilerParams(vmem_limit_bytes=20 << 20),
+        compiler_params=pltpu.CompilerParams(vmem_limit_bytes=10 << 20),
         cost_estimate=pl.CostEstimate(
             flops=number * 12 * 2 * points * BS * BS,
             bytes_accessed=number * points * width * 4 + base.size * 8,
             transcendentals=0,
         ),
         name="block_step",
-    )(table, psi, base, *arrays)
+    )(table, psi, phi, base)
 
 
 def whole_step(x_initial, sp2_choices, domain_blocks, basis_values):
@@ -540,7 +576,20 @@
     plus, minus = pick_step((1, -1), ((0, points),), table, basis_values)
     near = [orbitals(plus, 1), orbitals(minus, -1)]
     far_a = [orbitals(halfway[n][: cuts[0][1]], 1 - 2 * n) for n in (0, 1)]
-    far_b = [orbitals(halfway[n][cuts[1][0] :], 1 - 2 * n) for n in (0, 1)]
+    rest = [halfway[n][cuts[1][0] :] for n in (0, 1)]
+    turned = jnp.where(lax.axis_index("grid") < grid_count // 2, rest[0], rest[1])
+    detour = lax.ppermute(turned, ("band", "grid"), detour_out(band_count, grid_count))
+    far_b = []
+    for n, skipped in ((0, (0, 1)), (1, (grid_count - 2, grid_count - 1))):
+        move = 1 - 2 * n
+        pairs = [
+            (b * grid_count + g, (b + move) * grid_count + g)
+            for b in range(band_count)
+            for g in range(grid_count)
+            if 0 <= b + move < band_count and g not in skipped
+        ]
+        far_b.append(lax.ppermute(rest[n], ("band", "grid"), pairs))
+    detour = lax.ppermute(detour, ("band", "grid"), detour_back(band_count, grid_count))
 
     x = x_initial
     narrow = x.astype(jnp.bfloat16)
@@ -559,9 +608,9 @@
 
     ham, near_pot = domain_step((0, 1, 2), table, tiles, None, [basis_values] + near, factor)
     ham, pot_a = domain_step((3, 4), table, tiles, ham, far_a, factor)
-    psi_b, pot_b = potential_step((3, 4), table, tiles, far_b, factor)
-    far_pot = jnp.concatenate([pot_a[:, 0], pot_b[:, 0]], axis=1)
-    ham = block_step((3, 4), table, psi_b, ham, far_b)
+    psi_b, phi_b, pot_b = potential_step((3, 4), table, tiles, far_b, detour, factor)
+    far_pot = [jnp.concatenate([pot_a[n, 0], pot_b[n, 0]]) for n in (0, 1)]
+    ham = block_step((3, 4), table, psi_b, phi_b, ham)
     sent_back = [near_pot[0, 0]]
     for move, values in ((1, near_pot[1, 0]), (-1, near_pot[2, 0]), (2, far_pot[0]), (-2, far_pot[1])):
         sent_back.append(passed_along(values, "band", -move))

time: 191 us -> 186 us (0.974)
  the two profiles are of different devices: /device:TPU:56 before, /device:TPU:26 now
where the time goes in v2:
time: 186 us; the launch traced here: 184 us
  starting transfers between devices  85.8 us (46%)
  Pallas kernels  59.9 us (32%)
  waiting for transfers between devices  25.4 us (14%)
  local copies, waits for them, and re-layouts  7.57 us (4%)
  other arithmetic  4.62 us (2%)
    ppermute x18, starting transfers between devices, passed_along(): return lax.ppermute(x, axis, pairs)  68 us
    pallas_call x2, Pallas kernels, domain_step(): pl.pallas_call(functools.partial(domain_kernel, slots, has_base, factor),...  18.8 us
    pallas_call x4, Pallas kernels, local_step(): pl.pallas_call(local_kernel, in_specs=[pl.BlockSpec(memory_space=pltpu.SM...  16.9 us
    ppermute x2, waiting for transfers between devices, whole_step(): far_b.append(lax.ppermute(rest[n], ('band', 'grid'), pairs))  13.6 us
    ppermute x18, waiting for transfers between devices, passed_along(): return lax.ppermute(x, axis, pairs)  11.7 us
    ppermute x1, starting transfers between devices, whole_step(): lax.ppermute(detour, ('band', 'grid'), detour_back(band_count, grid_count))  8.36 us
    ppermute x2, starting transfers between devices, whole_step(): far_b.append(lax.ppermute(rest[n], ('band', 'grid'), pairs))  8.13 us
    pallas_call x4, Pallas kernels, border_step(): pl.pallas_call(border_kernel, in_specs=[pl.BlockSpec(memory_space=pltpu.S...  6.27 us
  transfers between devices with their start and end apart: 22, of which 5 were waited for; matrix products, arithmetic and copies ran while one was open for 3% of the time, Pallas kernels for 32%

profile of v2, /device:TPU:26, one launch (start us, length us, event | category | flops | bytes accessed | tf_op | source)
XLA Modules:
  0.0 184.5 jit_solution(16759287886883805152)
XLA Ops:
  7.5 5.3 %plan_step.1 = (bf16[768,1280]{1,0:T(8,128)(2,1)}, bf16[768,1280]{1,0:T(8,128)(2,1)}, s32[16]{0:T(128)S(1)}) custom-call(s32[5,384]{1,0:T(8,128)} %bitcast.29, bf16[3,768,1280]{2,1,0:T(8,128)(2,1)} %refs_0_.1), custom_call_target="tpu_custom_call" | custom-call | tf_op jit(solution)/shard_map/plan_step/pallas_call | solution.py:252
  12.8 3.8 %collective-permute-start.8 = (bf16[768,1280]{1,0:T(8,128)(2,1)}, bf16[768,1280]{1,0:T(8,128)(2,1)}, u32[]{:S(2)}, u32[]{:S(2)}) collective-permute-start(bf16[768,1280]{1,0:T(8,128)(2,1)} %get-tuple-element.56), channel_id=1, source_target_pairs={{0,8},{8,16},{16,24},{24,32},{32,40},{40,48},{48,56},{56,64},{64,7... | collective-permute-start | bytes 5898248 | tf_op jit(solution)/shard_map/ppermute | solution.py:26
  16.7 4.2 %collective-permute-start.10 = (bf16[768,1280]{1,0:T(8,128)(2,1)}, bf16[768,1280]{1,0:T(8,128)(2,1)}, u32[]{:S(2)}, u32[]{:S(2)}) collective-permute-start(bf16[768,1280]{1,0:T(8,128)(2,1)} %get-tuple-element.57), channel_id=1, source_target_pairs={{8,0},{16,8},{24,16},{32,24},{40,32},{48,40},{56,48},{64,56},{72,6... | collective-permute-start | bytes 5898248 | tf_op jit(solution)/shard_map/ppermute | solution.py:26
  21.7 3.8 %local_step.4 = (f32[5,3,256,256]{3,2,1,0:T(8,128)S(1)}, bf16[5,3,256,256]{3,2,1,0:T(8,128)(2,1)S(1)}) custom-call(s32[1]{0:T(128)} %get-tuple-element.88.choice_ref, f32[5,3,256,256]{3,2,1,0:T(8,128)S(1)} %copy-done, f32[6,256,256]{2,1,0:T(8,128)S(1)} %bitcast_dynamic-update-slice_fusion.edge_ref, ...), custom_call_target="tpu_custom_call" | custom-call | flops 2013265920 | bytes 3932160 | tf_op jit(solution)/shard_map/local_step/pallas_call | solution.py:116
  26.7 2.7 %collective-permute-start.2 = (bf16[3,256,256]{2,1,0:T(8,128)(2,1)S(1)}, bf16[3,256,256]{2,1,0:T(8,128)(2,1)S(1)}, u32[]{:S(2)}, u32[]{:S(2)}) collective-permute-start(bf16[3,256,256]{2,1,0:T(8,128)(2,1)S(1)} %get-tuple-element.39.up_ref), channel_id=1, source_target_pairs={{0,1},{1,2},{2,3},{3,4},{4,5},{5,6},{6,7},{7,8},{8,9},{9,10},{10,1... | collective-permute-start | bytes 1179656 | tf_op jit(solution)/shard_map/ppermute | solution.py:26
  29.5 2.8 %collective-permute-start.3 = (bf16[3,256,256]{2,1,0:T(8,128)(2,1)S(1)}, bf16[3,256,256]{2,1,0:T(8,128)(2,1)S(1)}, u32[]{:S(2)}, u32[]{:S(2)}) collective-permute-start(bf16[3,256,256]{2,1,0:T(8,128)(2,1)S(1)} %get-tuple-element.38.down_ref.before_ref), channel_id=1, source_target_pairs={{1,0},{2,1},{3,2},{4,3},{5,4},{6,5},{7,6},{8,7},{9,8},{10,9},{11,1... | collective-permute-start | bytes 1179656 | tf_op jit(solution)/shard_map/ppermute | solution.py:26
  32.3 3.9 %local_step.5 = (f32[5,3,256,256]{3,2,1,0:T(8,128)S(1)}, bf16[5,3,256,256]{3,2,1,0:T(8,128)(2,1)S(1)}) custom-call(s32[1]{0:T(128)} %get-tuple-element.91.choice_ref, f32[5,3,256,256]{3,2,1,0:T(8,128)S(1)} %get-tuple-element.35.x_ref, f32[6,256,256]{2,1,0:T(8,128)S(1)} %get-tuple-element.36.edge_ref, ...), custom_call_target="tpu_custom_call" | custom-call | flops 2013265920 | bytes 3932160 | tf_op jit(solution)/shard_map/local_step/pallas_call | solution.py:116
  39.4 4.1 %collective-permute-start.4 = (bf16[3,256,256]{2,1,0:T(8,128)(2,1)S(1)}, bf16[3,256,256]{2,1,0:T(8,128)(2,1)S(1)}, u32[]{:S(2)}, u32[]{:S(2)}) collective-permute-start(bf16[3,256,256]{2,1,0:T(8,128)(2,1)S(1)} %get-tuple-element.44.up_ref), channel_id=1, source_target_pairs={{0,1},{1,2},{2,3},{3,4},{4,5},{5,6},{6,7},{7,8},{8,9},{9,10},{10,1... | collective-permute-start | bytes 1179656 | tf_op jit(solution)/shard_map/ppermute | solution.py:26
  43.5 4.1 %pick_step.1 = (bf16[768,1280]{1,0:T(8,128)(2,1)}, bf16[768,1280]{1,0:T(8,128)(2,1)}) custom-call(s32[16]{0:T(128)S(1)} %get-tuple-element.52.table_ref, bf16[3,768,1280]{2,1,0:T(8,128)(2,1)} %refs_0_.1), custom_call_target="tpu_custom_call" | custom-call | tf_op jit(solution)/shard_map/pick_step/pallas_call | solution.py:306
  49.5 6.0 %collective-permute-start.15 = (bf16[768,1280]{1,0:T(8,128)(2,1)}, bf16[768,1280]{1,0:T(8,128)(2,1)}, u32[]{:S(2)}, u32[]{:S(2)}) collective-permute-start(bf16[768,1280]{1,0:T(8,128)(2,1)} %get-tuple-element.61), channel_id=1, source_target_pairs={{8,0},{16,8},{24,16},{32,24},{40,32},{48,40},{56,48},{64,56},{72,6... | collective-permute-start | bytes 5898248 | tf_op jit(solution)/shard_map/ppermute | solution.py:26
  61.6 5.3 %local_step.6 = (f32[5,3,256,256]{3,2,1,0:T(8,128)S(1)}, bf16[5,3,256,256]{3,2,1,0:T(8,128)(2,1)S(1)}) custom-call(s32[1]{0:T(128)} %get-tuple-element.89.choice_ref, f32[5,3,256,256]{3,2,1,0:T(8,128)S(1)} %copy-done.2, f32[6,256,256]{2,1,0:T(8,128)S(1)} %get-tuple-element.41.edge_ref, bf16[5,3,256,256]{3,2,1,0:T(8,128)(2,1)S(1)} %get-tuple-element.42.narrow_ref, ...), custom_call_target="tpu_custom_call" | custom-call | flops 2013265920 | bytes 3932160 | tf_op jit(solution)/shard_map/local_step/pallas_call | solution.py:116
  69.2 3.9 %collective-permute-start.6 = (bf16[3,256,256]{2,1,0:T(8,128)(2,1)S(1)}, bf16[3,256,256]{2,1,0:T(8,128)(2,1)S(1)}, u32[]{:S(2)}, u32[]{:S(2)}) collective-permute-start(bf16[3,256,256]{2,1,0:T(8,128)(2,1)S(1)} %get-tuple-element.49.up_ref), channel_id=1, source_target_pairs={{0,1},{1,2},{2,3},{3,4},{4,5},{5,6},{6,7},{7,8},{8,9},{9,10},{10,1... | collective-permute-start | bytes 1179656 | tf_op jit(solution)/shard_map/ppermute | solution.py:26
  73.1 7.7 %collective-permute-start.7 = (bf16[3,256,256]{2,1,0:T(8,128)(2,1)S(1)}, bf16[3,256,256]{2,1,0:T(8,128)(2,1)S(1)}, u32[]{:S(2)}, u32[]{:S(2)}) collective-permute-start(bf16[3,256,256]{2,1,0:T(8,128)(2,1)S(1)} %get-tuple-element.48.down_ref.before_ref), channel_id=1, source_target_pairs={{1,0},{2,1},{3,2},{4,3},{5,4},{6,5},{7,6},{8,7},{9,8},{10,9},{11,1... | collective-permute-start | bytes 1179656 | tf_op jit(solution)/shard_map/ppermute | solution.py:26
  88.3 6.0 %collective-permute-start.17 = (bf16[512,1280]{1,0:T(8,128)(2,1)S(1)}, bf16[512,1280]{1,0:T(8,128)(2,1)S(1)}, u32[]{:S(2)}, u32[]{:S(2)}) collective-permute-start(bf16[512,1280]{1,0:T(8,128)(2,1)S(1)} %slice.121), channel_id=1, source_target_pairs={{8,0},{16,8},{24,16},{32,24},{40,32},{48,40},{56,48},{64,56},{72,6... | collective-permute-start | bytes 3932168 | tf_op jit(solution)/shard_map/ppermute | solution.py:26
  94.4 3.9 %local_step.7 = (f32[5,3,256,256]{3,2,1,0:T(8,128)S(1)}, bf16[5,3,256,256]{3,2,1,0:T(8,128)(2,1)S(1)}) custom-call(s32[1]{0:T(128)} %get-tuple-element.90.choice_ref, f32[5,3,256,256]{3,2,1,0:T(8,128)S(1)} %get-tuple-element.45.x_ref, f32[6,256,256]{2,1,0:T(8,128)S(1)} %get-tuple-element.46.edge_ref, ...), custom_call_target="tpu_custom_call" | custom-call | flops 2013265920 | bytes 3932160 | tf_op jit(solution)/shard_map/local_step/pallas_call | solution.py:116
  101.4 10.2 %collective-permute-done.14.refs_1_ = bf16[768,1280]{1,0:T(8,128)(2,1)} collective-permute-done((bf16[768,1280]{1,0:T(8,128)(2,1)}, bf16[768,1280]{1,0:T(8,128)(2,1)}, u32[]{:S(2)}, u32[]{:S(2)}) %collective-permute-start.14) | collective-permute-done | bytes 1966112 | tf_op jit(solution)/shard_map/ppermute | solution.py:26
  113.7 6.2 %collective-permute-start.11 = (bf16[256,1280]{1,0:T(8,128)(2,1)S(1)}, bf16[256,1280]{1,0:T(8,128)(2,1)S(1)}, u32[]{:S(2)}, u32[]{:S(2)}) collective-permute-start(bf16[256,1280]{1,0:T(8,128)(2,1)S(1)} %get-tuple-element.72), channel_id=1, source_target_pairs={{8,0},{9,1},{10,2},{11,3},{12,4},{13,5},{16,8},{17,9},{18,10},{19,... | collective-permute-start | bytes 1966088 | tf_op jit(solution)/shard_map/ppermute | solution.py:591
  119.9 8.4 %collective-permute-start.13 = (bf16[256,1280]{1,0:T(8,128)(2,1)S(1)}, bf16[256,1280]{1,0:T(8,128)(2,1)S(1)}, u32[]{:S(2)}, u32[]{:S(2)}) collective-permute-start(bf16[256,1280]{1,0:T(8,128)(2,1)S(1)} %collective-permute-done.12), channel_id=1, source_target_pairs={{2,0},{5,7},{4,1},{3,6},{10,8},{13,15},{12,9},{11,14},{18,16},{21,... | collective-permute-start | bytes 1966088 | tf_op jit(solution)/shard_map/ppermute | solution.py:592
  128.3 11.8 %domain_step.2 = (f32[5,3,256,256]{3,2,1,0:T(8,128)S(1)}, f32[3,1,768]{2,1,0:T(1,128)S(1)}) custom-call(s32[16]{0:T(128)S(1)} %get-tuple-element.52.table_ref, bf16[5,3,256,256]{3,2,1,0:T(8,128)(2,1)S(1)} %get-tuple-element.53.main_ref, bf16[3,256,256]{2,1,0:T(8,128)(2,1)S(1)} %get-tuple-element.54.down_ref, ...), custom_call_target="tpu_custom_call" | custom-call | flops 7247757312 | bytes 11796480 | tf_op jit(solution)/shard_map/domain_step/pallas_call | solution.py:423
  140.2 13.5 %collective-permute-done.9.refs_0_ = bf16[256,1280]{1,0:T(8,128)(2,1)S(1)} collective-permute-done((bf16[256,1280]{1,0:T(8,128)(2,1)S(1)}, bf16[256,1280]{1,0:T(8,128)(2,1)S(1)}, u32[]{:S(2)}, u32[]{:S(2)}) %collective-permute-start.9) | collective-permute-done | bytes 655392 | tf_op jit(solution)/shard_map/ppermute | solution.py:591
  155.7 6.2 %collective-permute-start.21 = (f32[768]{0:T(1024)S(1)}, f32[768]{0:T(1024)S(1)}, u32[]{:S(2)}, u32[]{:S(2)}) collective-permute-start(f32[768]{0:T(1024)S(1)} %get-tuple-element.69), channel_id=1, source_target_pairs={{8,0},{16,8},{24,16},{32,24},{40,32},{48,40},{56,48},{64,56},{72,6... | collective-permute-start | bytes 9224 | tf_op jit(solution)/shard_map/ppermute | solution.py:26
  164.3 7.0 %domain_step.3 = (f32[5,3,256,256]{3,2,1,0:T(8,128)S(1)}, f32[2,1,512]{2,1,0:T(1,128)S(1)}) custom-call(s32[16]{0:T(128)S(1)} %get-tuple-element.52.table_ref, bf16[5,3,256,256]{3,2,1,0:T(8,128)(2,1)S(1)} %get-tuple-element.53.main_ref, bf16[3,256,256]{2,1,0:T(8,128)(2,1)S(1)} %get-tuple-element.54.down_ref, ...), custom_call_target="tpu_custom_call" | custom-call | flops 3221225472 | bytes 8519680 | tf_op jit(solution)/shard_map/domain_step/pallas_call | solution.py:423
  173.3 6.3 %collective-permute-start.19 = (f32[768]{0:T(1024)S(1)}, f32[768]{0:T(1024)S(1)}, u32[]{:S(2)}, u32[]{:S(2)}) collective-permute-start(f32[768]{0:T(1024)S(1)} %pad_maximum_fusion.3), channel_id=1, source_target_pairs={{16,0},{24,8},{32,16},{40,24},{48,32},{56,40},{64,48},{72,56},{80,... | collective-permute-start | bytes 9224 | tf_op jit(solution)/shard_map/ppermute | solution.py:26
  179.6 4.2 %block_step.1 = f32[5,3,256,256]{3,2,1,0:T(8,128)} custom-call(s32[16]{0:T(128)S(1)} %get-tuple-element.52.table_ref, bf16[2,256,1280]{2,1,0:T(8,128)(2,1)S(1)} %get-tuple-element.58.psi_ref, bf16[2,256,1792]{2,1,0:T(8,128)(2,1)S(1)} %get-tuple-element.59.phi_ref, f32[5,3,256,256]{3,2,1,0:T(8,128)S(1)} %get-tuple-element.63.base_ref), custom_call_target="tpu_custom_call" | custom-call | flops 805306368 | bytes 10485760 | tf_op jit(solution)/shard_map/block_step/pallas_call | solution.py:540
  (72 shorter events, 41.8 us)
Async XLA Ops:
  3.1 22.5 %collective-permute-start.1 = (bf16[3,256,256]{2,1,0:T(8,128)(2,1)S(1)}, bf16[3,256,256]{2,1,0:T(8,128)(2,1)S(1)}, u32[]{:S(2)}, u32[]{:S(2)}) collective-permute-start(bf16[3,256,256]{2,1,0:T(8,128)(2,1)S(1)} %pad_maximum_fusion.down_ref.before_ref), channel_id=1, source_target_pairs={{1,0},{2,1},{3,2},{4,3},{5,4},{6,5},{7,6},{8,7},{9,8},{10,9},{11,1... | collective-permute-start | bytes 1179656 | tf_op jit(solution)/shard_map/ppermute | solution.py:26
  5.1 20.5 %collective-permute-start = (bf16[3,256,256]{2,1,0:T(8,128)(2,1)S(1)}, bf16[3,256,256]{2,1,0:T(8,128)(2,1)S(1)}, u32[]{:S(2)}, u32[]{:S(2)}) collective-permute-start(bf16[3,256,256]{2,1,0:T(8,128)(2,1)S(1)} %pad_maximum_fusion.1.up_ref), channel_id=1, source_target_pairs={{0,1},{1,2},{2,3},{3,4},{4,5},{5,6},{6,7},{7,8},{8,9},{9,10},{10,1... | collective-permute-start | bytes 1179656 | tf_op jit(solution)/shard_map/ppermute | solution.py:26
  7.5 13.4 %copy-start = (f32[5,3,256,256]{3,2,1,0:T(8,128)S(1)}, f32[5,3,256,256]{3,2,1,0:T(8,128)}, u32[]{:S(2)}) copy-start(f32[5,3,256,256]{3,2,1,0:T(8,128)} %x_ref.1) | copy-start | bytes 11796484
  12.8 8.2 %copy-start.7 = (s32[4]{0:T(128)S(1)}, s32[4]{0:T(128)}, u32[]{:S(2)}) copy-start(s32[4]{0:T(128)} %param.5) | copy-start | bytes 52
  12.8 60.3 %collective-permute-start.8 = (bf16[768,1280]{1,0:T(8,128)(2,1)}, bf16[768,1280]{1,0:T(8,128)(2,1)}, u32[]{:S(2)}, u32[]{:S(2)}) collective-permute-start(bf16[768,1280]{1,0:T(8,128)(2,1)} %get-tuple-element.56), channel_id=1, source_target_pairs={{0,8},{8,16},{16,24},{24,32},{32,40},{40,48},{48,56},{56,64},{64,7... | collective-permute-start | bytes 5898248 | tf_op jit(solution)/shard_map/ppermute | solution.py:26
  16.7 64.1 %collective-permute-start.10 = (bf16[768,1280]{1,0:T(8,128)(2,1)}, bf16[768,1280]{1,0:T(8,128)(2,1)}, u32[]{:S(2)}, u32[]{:S(2)}) collective-permute-start(bf16[768,1280]{1,0:T(8,128)(2,1)} %get-tuple-element.57), channel_id=1, source_target_pairs={{8,0},{16,8},{24,16},{32,24},{40,32},{48,40},{56,48},{64,56},{72,6... | collective-permute-start | bytes 5898248 | tf_op jit(solution)/shard_map/ppermute | solution.py:26
  26.7 9.5 %collective-permute-start.2 = (bf16[3,256,256]{2,1,0:T(8,128)(2,1)S(1)}, bf16[3,256,256]{2,1,0:T(8,128)(2,1)S(1)}, u32[]{:S(2)}, u32[]{:S(2)}) collective-permute-start(bf16[3,256,256]{2,1,0:T(8,128)(2,1)S(1)} %get-tuple-element.39.up_ref), channel_id=1, source_target_pairs={{0,1},{1,2},{2,3},{3,4},{4,5},{5,6},{6,7},{7,8},{8,9},{9,10},{10,1... | collective-permute-start | bytes 1179656 | tf_op jit(solution)/shard_map/ppermute | solution.py:26
  29.5 8.1 %collective-permute-start.3 = (bf16[3,256,256]{2,1,0:T(8,128)(2,1)S(1)}, bf16[3,256,256]{2,1,0:T(8,128)(2,1)S(1)}, u32[]{:S(2)}, u32[]{:S(2)}) collective-permute-start(bf16[3,256,256]{2,1,0:T(8,128)(2,1)S(1)} %get-tuple-element.38.down_ref.before_ref), channel_id=1, source_target_pairs={{1,0},{2,1},{3,2},{4,3},{5,4},{6,5},{7,6},{8,7},{9,8},{10,9},{11,1... | collective-permute-start | bytes 1179656 | tf_op jit(solution)/shard_map/ppermute | solution.py:26
  39.4 16.1 %collective-permute-start.4 = (bf16[3,256,256]{2,1,0:T(8,128)(2,1)S(1)}, bf16[3,256,256]{2,1,0:T(8,128)(2,1)S(1)}, u32[]{:S(2)}, u32[]{:S(2)}) collective-permute-start(bf16[3,256,256]{2,1,0:T(8,128)(2,1)S(1)} %get-tuple-element.44.up_ref), channel_id=1, source_target_pairs={{0,1},{1,2},{2,3},{3,4},{4,5},{5,6},{6,7},{7,8},{8,9},{9,10},{10,1... | collective-permute-start | bytes 1179656 | tf_op jit(solution)/shard_map/ppermute | solution.py:26
  47.6 64.1 %collective-permute-start.14 = (bf16[768,1280]{1,0:T(8,128)(2,1)}, bf16[768,1280]{1,0:T(8,128)(2,1)}, u32[]{:S(2)}, u32[]{:S(2)}) collective-permute-start(bf16[768,1280]{1,0:T(8,128)(2,1)} %get-tuple-element.60), channel_id=1, source_target_pairs={{0,8},{8,16},{16,24},{24,32},{32,40},{40,48},{48,56},{56,64},{64,7... | collective-permute-start | bytes 5898248 | tf_op jit(solution)/shard_map/ppermute | solution.py:26
  49.5 64.2 %collective-permute-start.15 = (bf16[768,1280]{1,0:T(8,128)(2,1)}, bf16[768,1280]{1,0:T(8,128)(2,1)}, u32[]{:S(2)}, u32[]{:S(2)}) collective-permute-start(bf16[768,1280]{1,0:T(8,128)(2,1)} %get-tuple-element.61), channel_id=1, source_target_pairs={{8,0},{16,8},{24,16},{32,24},{40,32},{48,40},{56,48},{64,56},{72,6... | collective-permute-start | bytes 5898248 | tf_op jit(solution)/shard_map/ppermute | solution.py:26
  56.3 10.5 %collective-permute-start.5 = (bf16[3,256,256]{2,1,0:T(8,128)(2,1)}, bf16[3,256,256]{2,1,0:T(8,128)(2,1)}, u32[]{:S(2)}, u32[]{:S(2)}) collective-permute-start(bf16[3,256,256]{2,1,0:T(8,128)(2,1)} %get-tuple-element.43.down_ref.before_ref), channel_id=1, source_target_pairs={{1,0},{2,1},{3,2},{4,3},{5,4},{6,5},{7,6},{8,7},{9,8},{10,9},{11,1... | collective-permute-start | bytes 1179656 | tf_op jit(solution)/shard_map/ppermute | solution.py:26
  69.2 17.2 %collective-permute-start.6 = (bf16[3,256,256]{2,1,0:T(8,128)(2,1)S(1)}, bf16[3,256,256]{2,1,0:T(8,128)(2,1)S(1)}, u32[]{:S(2)}, u32[]{:S(2)}) collective-permute-start(bf16[3,256,256]{2,1,0:T(8,128)(2,1)S(1)} %get-tuple-element.49.up_ref), channel_id=1, source_target_pairs={{0,1},{1,2},{2,3},{3,4},{4,5},{5,6},{6,7},{7,8},{8,9},{9,10},{10,1... | collective-permute-start | bytes 1179656 | tf_op jit(solution)/shard_map/ppermute | solution.py:26
  73.1 15.2 %collective-permute-start.7 = (bf16[3,256,256]{2,1,0:T(8,128)(2,1)S(1)}, bf16[3,256,256]{2,1,0:T(8,128)(2,1)S(1)}, u32[]{:S(2)}, u32[]{:S(2)}) collective-permute-start(bf16[3,256,256]{2,1,0:T(8,128)(2,1)S(1)} %get-tuple-element.48.down_ref.before_ref), channel_id=1, source_target_pairs={{1,0},{2,1},{3,2},{4,3},{5,4},{6,5},{7,6},{8,7},{9,8},{10,9},{11,1... | collective-permute-start | bytes 1179656 | tf_op jit(solution)/shard_map/ppermute | solution.py:26
  82.2 37.7 %collective-permute-start.12 = (bf16[256,1280]{1,0:T(8,128)(2,1)S(1)}, bf16[256,1280]{1,0:T(8,128)(2,1)S(1)}, u32[]{:S(2)}, u32[]{:S(2)}) collective-permute-start(bf16[256,1280]{1,0:T(8,128)(2,1)S(1)} %get-tuple-element.70), channel_id=1, source_target_pairs={{0,10},{1,12},{8,18},{15,5},{9,20},{14,3},{16,26},{23,13},{17,28},... | collective-permute-start | bytes 1966088 | tf_op jit(solution)/shard_map/ppermute | solution.py:581
  86.3 78.0 %collective-permute-start.16 = (bf16[512,1280]{1,0:T(8,128)(2,1)S(1)}, bf16[512,1280]{1,0:T(8,128)(2,1)S(1)}, u32[]{:S(2)}, u32[]{:S(2)}) collective-permute-start(bf16[512,1280]{1,0:T(8,128)(2,1)S(1)} %slice.120), channel_id=1, source_target_pairs={{0,8},{8,16},{16,24},{24,32},{32,40},{40,48},{48,56},{56,64},{64,7... | collective-permute-start | bytes 3932168 | tf_op jit(solution)/shard_map/ppermute | solution.py:26
  88.3 76.0 %collective-permute-start.17 = (bf16[512,1280]{1,0:T(8,128)(2,1)S(1)}, bf16[512,1280]{1,0:T(8,128)(2,1)S(1)}, u32[]{:S(2)}, u32[]{:S(2)}) collective-permute-start(bf16[512,1280]{1,0:T(8,128)(2,1)S(1)} %slice.121), channel_id=1, source_target_pairs={{8,0},{16,8},{24,16},{32,24},{40,32},{48,40},{56,48},{64,56},{72,6... | collective-permute-start | bytes 3932168 | tf_op jit(solution)/shard_map/ppermute | solution.py:26
  111.7 42.0 %collective-permute-start.9 = (bf16[256,1280]{1,0:T(8,128)(2,1)S(1)}, bf16[256,1280]{1,0:T(8,128)(2,1)S(1)}, u32[]{:S(2)}, u32[]{:S(2)}) collective-permute-start(bf16[256,1280]{1,0:T(8,128)(2,1)S(1)} %get-tuple-element.71), channel_id=1, source_target_pairs={{2,10},{3,11},{4,12},{5,13},{6,14},{7,15},{10,18},{11,19},{12,20},... | collective-permute-start | bytes 1966088 | tf_op jit(solution)/shard_map/ppermute | solution.py:591
  113.7 42.0 %collective-permute-start.11 = (bf16[256,1280]{1,0:T(8,128)(2,1)S(1)}, bf16[256,1280]{1,0:T(8,128)(2,1)S(1)}, u32[]{:S(2)}, u32[]{:S(2)}) collective-permute-start(bf16[256,1280]{1,0:T(8,128)(2,1)S(1)} %get-tuple-element.72), channel_id=1, source_target_pairs={{8,0},{9,1},{10,2},{11,3},{12,4},{13,5},{16,8},{17,9},{18,10},{19,... | collective-permute-start | bytes 1966088 | tf_op jit(solution)/shard_map/ppermute | solution.py:591
  119.9 42.0 %collective-permute-start.13 = (bf16[256,1280]{1,0:T(8,128)(2,1)S(1)}, bf16[256,1280]{1,0:T(8,128)(2,1)S(1)}, u32[]{:S(2)}, u32[]{:S(2)}) collective-permute-start(bf16[256,1280]{1,0:T(8,128)(2,1)S(1)} %collective-permute-done.12), channel_id=1, source_target_pairs={{2,0},{5,7},{4,1},{3,6},{10,8},{13,15},{12,9},{11,14},{18,16},{21,... | collective-permute-start | bytes 1966088 | tf_op jit(solution)/shard_map/ppermute | solution.py:592
  153.7 30.1 %collective-permute-start.20 = (f32[768]{0:T(1024)S(1)}, f32[768]{0:T(1024)S(1)}, u32[]{:S(2)}, u32[]{:S(2)}) collective-permute-start(f32[768]{0:T(1024)S(1)} %get-tuple-element.67), channel_id=1, source_target_pairs={{0,8},{8,16},{16,24},{24,32},{32,40},{40,48},{48,56},{56,64},{64,7... | collective-permute-start | bytes 9224 | tf_op jit(solution)/shard_map/ppermute | solution.py:26
  155.7 28.1 %collective-permute-start.21 = (f32[768]{0:T(1024)S(1)}, f32[768]{0:T(1024)S(1)}, u32[]{:S(2)}, u32[]{:S(2)}) collective-permute-start(f32[768]{0:T(1024)S(1)} %get-tuple-element.69), channel_id=1, source_target_pairs={{8,0},{16,8},{24,16},{32,24},{40,32},{48,40},{56,48},{64,56},{72,6... | collective-permute-start | bytes 9224 | tf_op jit(solution)/shard_map/ppermute | solution.py:26
  171.3 12.5 %collective-permute-start.18 = (f32[768]{0:T(1024)S(1)}, f32[768]{0:T(1024)S(1)}, u32[]{:S(2)}, u32[]{:S(2)}) collective-permute-start(f32[768]{0:T(1024)S(1)} %pad_maximum_fusion.2), channel_id=1, source_target_pairs={{0,16},{8,24},{16,32},{24,40},{32,48},{40,56},{48,64},{56,72},{64,... | collective-permute-start | bytes 9224 | tf_op jit(solution)/shard_map/ppermute | solution.py:26
  173.3 10.5 %collective-permute-start.19 = (f32[768]{0:T(1024)S(1)}, f32[768]{0:T(1024)S(1)}, u32[]{:S(2)}, u32[]{:S(2)}) collective-permute-start(f32[768]{0:T(1024)S(1)} %pad_maximum_fusion.3), channel_id=1, source_target_pairs={{16,0},{24,8},{32,16},{40,24},{48,32},{56,40},{64,48},{72,56},{80,... | collective-permute-start | bytes 9224 | tf_op jit(solution)/shard_map/ppermute | solution.py:26
  (6 other events, 20.6 us)

commit v3 on v2

--- a/solution.py
+++ b/solution.py
@@ -9,6 +9,7 @@
 
 
 DBLK = 5
+RB = 5
 ITERS = 4
 BS = 256
 TILE = 256
@@ -367,22 +368,24 @@
         psi_at(here)[...] = (scale * phi[slot, here, :].astype(jnp.float32)).astype(jnp.bfloat16)
 
 
-def add_blocks(ham, psi, phi, slot, first, blocks):
+def add_blocks(ham, psi, phi, slot, first):
     for k in range(DBLK):
-
-        @pl.when(k < blocks)
-        def _():
-            low = max(0, k - 2)
-            piece = dot32(psi[:, k * BS : (k + 1) * BS], phi[slot, :, low * BS : (k + 1) * BS], TN)
-            for j in range(low, k + 1):
-                ham[first + k, 2 - (k - j)] += piece[:, (j - low) * BS : (j - low + 1) * BS]
-
-
-def domain_kernel(slots, has_base, factor, table_ref, main_ref, down_ref, up_ref, *refs):
+        row = jnp.minimum(first + k, ham.shape[0] - 1)
+        low = max(0, k - 2)
+        piece = dot32(psi[:, k * BS : (k + 1) * BS], phi[slot, :, low * BS : (k + 1) * BS], TN)
+        for j in range(low, k + 1):
+            ham[row, 2 - (k - j)] += piece[:, (j - low) * BS : (j - low + 1) * BS]
+
+
+def domain_kernel(slots, has_base, factor, table_ref, *refs):
     refs = list(refs)
-    base_ref = refs.pop(0) if has_base else None
+    if has_base:
+        base_ref, stack = refs.pop(0), refs.pop(0)
+    else:
+        tile_refs = [refs.pop(0) for _ in range(3)]
+        stack = refs.pop(len(slots) + 2)
     basis_refs = [refs.pop(0) for _ in slots]
-    ham, pot_out, phi, psi, stack, sems = refs
+    ham, pot_out, phi, psi, sems = refs
 
     def fetch(n):
         source = basis_refs[n]
@@ -394,7 +397,8 @@
         fetch(n).start()
     for r in range(ham.shape[0]):
         ham[r] = base_ref[r] if has_base else jnp.zeros_like(ham[r])
-    fill_stack((main_ref, down_ref, up_ref), stack)
+    if not has_base:
+        fill_stack(tile_refs, stack)
     pot_out[...] = jnp.zeros_like(pot_out)
     for n in range(len(slots)):
         fetch(n).wait()
@@ -408,51 +412,54 @@
         def _():
             blank_tail(phi, n, blocks)
             potential_of_slot(phi, n, first, stack, pot_out, lambda here: psi.at[here], factor)
-            add_blocks(ham, psi, phi, n, first, blocks)
+            add_blocks(ham, psi, phi, n, first)
 
 
 def domain_step(slots, table, tiles, base, arrays, factor):
-    rows = tiles[0].shape[0]
+    rows = RB
     points, width = arrays[-1].shape[-2:]
     number = len(arrays)
     has_base = base is not None
     smem = pl.BlockSpec(memory_space=pltpu.SMEM)
     vmem = pl.BlockSpec(memory_space=pltpu.VMEM)
     hbm = pl.BlockSpec(memory_space=pl.ANY)
-    operands = [table, *tiles] + ([base] if has_base else []) + list(arrays)
+    fixed = base if has_base else tiles
+    outs = [
+        jax.ShapeDtypeStruct((rows, 3, BS, BS), jnp.float32),
+        jax.ShapeDtypeStruct((number, 1, points), jnp.float32),
+    ]
+    if not has_base:
+        outs.append(jax.ShapeDtypeStruct((rows, 3 * BS, BS), jnp.bfloat16))
     return pl.pallas_call(
         functools.partial(domain_kernel, slots, has_base, factor),
-        in_specs=[smem] + [vmem] * (3 + has_base) + [hbm] * number,
-        out_specs=[vmem, vmem],
-        out_shape=[
-            jax.ShapeDtypeStruct((rows, 3, BS, BS), jnp.float32),
-            jax.ShapeDtypeStruct((number, 1, points), jnp.float32),
-        ],
+        in_specs=[smem] + [vmem] * len(fixed) + [hbm] * number,
+        out_specs=[vmem] * len(outs),
+        out_shape=outs,
         scratch_shapes=[
             pltpu.VMEM((number, points, width), jnp.bfloat16),
             pltpu.VMEM((points, width), jnp.bfloat16),
-            pltpu.VMEM((rows, 3 * BS, BS), jnp.bfloat16),
             pltpu.SemaphoreType.DMA((number,)),
         ],
-        compiler_params=pltpu.CompilerParams(vmem_limit_bytes=(8 << 20) + number * points * width * 2),
+        compiler_params=pltpu.CompilerParams(
+            vmem_limit_bytes=(8 << 20) + number * points * width * 2
+        ),
         cost_estimate=pl.CostEstimate(
             flops=number * 24 * 2 * points * BS * BS,
             bytes_accessed=number * points * width * 2 + rows * 3 * BS * BS * 6,
             transcendentals=number * points,
         ),
         name="domain_step",
-    )(*operands)
-
-
-def potential_kernel(slots, factor, table_ref, main_ref, down_ref, up_ref, *refs):
+    )(table, *fixed, *arrays)
+
+
+def potential_kernel(slots, factor, table_ref, stack, *refs):
     *basis_refs, detour_ref = refs[: len(slots) + 1]
-    psi_out, phi_out, pot_out, phi, stack = refs[len(slots) + 1 :]
+    psi_out, phi_out, pot_out, phi = refs[len(slots) + 1 :]
     points, width = phi.shape[1:]
     pad = phi_out.shape[2] - width
     grid = lax.axis_index("grid")
     last = lax.axis_size("grid") - 1
     detoured = (grid <= 1, grid >= last - 1)
-    fill_stack((main_ref, down_ref, up_ref), stack)
     pot_out[...] = jnp.zeros_like(pot_out)
     for n in range(len(slots)):
 
@@ -465,6 +472,8 @@
             phi[n] = basis_refs[n][...]
 
         phi_out[n, :, 0:pad] = jnp.zeros((points, pad), jnp.bfloat16)
+        phi_out[n, :, pad:] = phi[n]
+        psi_out[n, :, width:] = jnp.zeros((points, BS), jnp.bfloat16)
 
     @pl.loop(0, len(slots))
     def _(n):
@@ -474,29 +483,28 @@
         @pl.when(blocks > 0)
         def _():
             blank_tail(phi, n, blocks)
-            phi_out[n, :, pad:] = phi[n]
-            potential_of_slot(phi, n, first, stack, pot_out, lambda here: psi_out.at[n, here], factor)
-
-
-def potential_step(slots, table, tiles, arrays, detour, factor):
-    rows = tiles[0].shape[0]
+
+            def psi_at(here):
+                return psi_out.at[n, here, 0:width]
+
+            potential_of_slot(phi, n, first, stack, pot_out, psi_at, factor)
+
+
+def potential_step(slots, table, stack, arrays, detour, factor):
     points, width = arrays[-1].shape
     number = len(arrays)
     smem = pl.BlockSpec(memory_space=pltpu.SMEM)
     vmem = pl.BlockSpec(memory_space=pltpu.VMEM)
     return pl.pallas_call(
         functools.partial(potential_kernel, slots, factor),
-        in_specs=[smem] + [vmem] * (4 + number),
+        in_specs=[smem] + [vmem] * (2 + number),
         out_specs=[vmem] * 3,
         out_shape=[
-            jax.ShapeDtypeStruct((number, points, width), jnp.bfloat16),
+            jax.ShapeDtypeStruct((number, points, width + BS), jnp.bfloat16),
             jax.ShapeDtypeStruct((number, points, width + 2 * BS), jnp.bfloat16),
             jax.ShapeDtypeStruct((number, 1, points), jnp.float32),
         ],
-        scratch_shapes=[
-            pltpu.VMEM((number, points, width), jnp.bfloat16),
-            pltpu.VMEM((rows, 3 * BS, BS), jnp.bfloat16),
-        ],
+        scratch_shapes=[pltpu.VMEM((number, points, width), jnp.bfloat16)],
         compiler_params=pltpu.CompilerParams(vmem_limit_bytes=10 << 20),
         cost_estimate=pl.CostEstimate(
             flops=number * 12 * 2 * points * BS * BS,
@@ -504,7 +512,7 @@
             transcendentals=number * points,
         ),
         name="potential_step",
-    )(table, *tiles, *arrays, detour)
+    )(table, stack, *arrays, detour)
 
 
 def block_kernel(slots, table_ref, psi_ref, phi_ref, base_ref, ham_out, ham, sems):
@@ -514,19 +522,17 @@
         return pltpu.make_async_copy(ham.at[r], ham_out.at[r], sems.at[r])
 
     for r in range(rows):
-        ham[r] = base_ref[r]
+        total = None
         for n, slot in enumerate(slots):
             k = r - table_ref[STARTS + slot]
-            blocks = table_ref[COUNTS + slot]
-
-            @pl.when((k >= 0) & (k < blocks))
-            def _():
-                offset = pl.multiple_of(k * BS, BS)
-                left = psi_ref[n, :, pl.ds(offset, BS)]
-                piece = dot32(left, phi_ref[n, :, pl.ds(offset, 3 * BS)], TN)
-                for q in range(3):
-                    ham[r, q] += piece[:, q * BS : (q + 1) * BS]
-
+            held = (k >= 0) & (k < table_ref[COUNTS + slot])
+            near = jnp.clip(k, 0, DBLK - 1)
+            left = psi_ref[n, :, pl.ds(pl.multiple_of(jnp.where(held, near, DBLK) * BS, BS), BS)]
+            right = phi_ref[n, :, pl.ds(pl.multiple_of(near * BS, BS), 3 * BS)]
+            piece = dot32(left, right, TN)
+            total = piece if total is None else total + piece
+        for q in range(3):
+            ham[r, q] = base_ref[r, q] + total[:, q * BS : (q + 1) * BS]
         send(r).start()
     for r in range(rows):
         send(r).wait()
@@ -606,9 +612,9 @@
     tiles = (narrow, downward, upward)
     density = density_step(x, edge)
 
-    ham, near_pot = domain_step((0, 1, 2), table, tiles, None, [basis_values] + near, factor)
-    ham, pot_a = domain_step((3, 4), table, tiles, ham, far_a, factor)
-    psi_b, phi_b, pot_b = potential_step((3, 4), table, tiles, far_b, detour, factor)
+    ham, near_pot, stack = domain_step((0, 1, 2), table, tiles, None, [basis_values] + near, factor)
+    ham, pot_a = domain_step((3, 4), table, None, (ham, stack), far_a, factor)
+    psi_b, phi_b, pot_b = potential_step((3, 4), table, stack, far_b, detour, factor)
     far_pot = [jnp.concatenate([pot_a[n, 0], pot_b[n, 0]]) for n in (0, 1)]
     ham = block_step((3, 4), table, psi_b, phi_b, ham)
     sent_back = [near_pot[0, 0]]

time: 186 us -> 187 us (level)
  the two profiles are of different devices: /device:TPU:26 before, /device:TPU:60 now
where the time goes in v3:
time: 187 us; the launch traced here: 186 us
  starting transfers between devices  70.1 us (37%)
  Pallas kernels  60.7 us (32%)
  waiting for transfers between devices  41.5 us (22%)
  local copies, waits for them, and re-layouts  7.57 us (4%)
  other arithmetic  4.61 us (2%)
    ppermute x18, starting transfers between devices, passed_along(): return lax.ppermute(x, axis, pairs)  59.3 us
    ppermute x18, waiting for transfers between devices, passed_along(): return lax.ppermute(x, axis, pairs)  25.1 us
    pallas_call x2, Pallas kernels, domain_step(): pl.pallas_call(functools.partial(domain_kernel, slots, has_base, factor),...  20.9 us
    pallas_call x4, Pallas kernels, local_step(): pl.pallas_call(local_kernel, in_specs=[pl.BlockSpec(memory_space=pltpu.SM...  16.9 us
    ppermute x2, waiting for transfers between devices, whole_step(): far_b.append(lax.ppermute(rest[n], ('band', 'grid'), pairs))  16.3 us
    ppermute x2, starting transfers between devices, whole_step(): far_b.append(lax.ppermute(rest[n], ('band', 'grid'), pairs))  7.94 us
    pallas_call x4, Pallas kernels, border_step(): pl.pallas_call(border_kernel, in_specs=[pl.BlockSpec(memory_space=pltpu.S...  6.27 us
    pallas_call x1, Pallas kernels, plan_step(): pl.pallas_call(functools.partial(plan_kernel, moves, (rows, band_count, g...  5.25 us
  transfers between devices with their start and end apart: 22, of which 4 were waited for; matrix products, arithmetic and copies ran while one was open for 3% of the time, Pallas kernels for 33%

profile of v3, /device:TPU:60, one launch (start us, length us, event | category | flops | bytes accessed | tf_op | source)
XLA Modules:
  0.0 185.7 jit_solution(14613431572658571884)
XLA Ops:
  5.1 3.6 %collective-permute-start.1 = (bf16[3,256,256]{2,1,0:T(8,128)(2,1)S(1)}, bf16[3,256,256]{2,1,0:T(8,128)(2,1)S(1)}, u32[]{:S(2)}, u32[]{:S(2)}) collective-permute-start(bf16[3,256,256]{2,1,0:T(8,128)(2,1)S(1)} %pad_maximum_fusion.down_ref.before_ref), channel_id=1, source_target_pairs={{1,0},{2,1},{3,2},{4,3},{5,4},{6,5},{7,6},{8,7},{9,8},{10,9},{11,1... | collective-permute-start | bytes 1179656 | tf_op jit(solution)/shard_map/ppermute | solution.py:27
  8.7 5.3 %plan_step.1 = (bf16[768,1280]{1,0:T(8,128)(2,1)}, bf16[768,1280]{1,0:T(8,128)(2,1)}, s32[16]{0:T(128)S(1)}) custom-call(s32[5,384]{1,0:T(8,128)} %bitcast.29, bf16[3,768,1280]{2,1,0:T(8,128)(2,1)} %refs_3_.1), custom_call_target="tpu_custom_call" | custom-call | tf_op jit(solution)/shard_map/plan_step/pallas_call | solution.py:253
  16.0 3.8 %collective-permute-start.10 = (bf16[768,1280]{1,0:T(8,128)(2,1)}, bf16[768,1280]{1,0:T(8,128)(2,1)}, u32[]{:S(2)}, u32[]{:S(2)}) collective-permute-start(bf16[768,1280]{1,0:T(8,128)(2,1)} %get-tuple-element.60), channel_id=1, source_target_pairs={{0,8},{8,16},{16,24},{24,32},{32,40},{40,48},{48,56},{56,64},{64,7... | collective-permute-start | bytes 5898248 | tf_op jit(solution)/shard_map/ppermute | solution.py:27
  20.7 3.8 %local_step.4 = (f32[5,3,256,256]{3,2,1,0:T(8,128)S(1)}, bf16[5,3,256,256]{3,2,1,0:T(8,128)(2,1)S(1)}) custom-call(s32[1]{0:T(128)} %get-tuple-element.90.choice_ref, f32[5,3,256,256]{3,2,1,0:T(8,128)S(1)} %copy-done, f32[6,256,256]{2,1,0:T(8,128)S(1)} %bitcast_dynamic-update-slice_fusion.edge_ref, ...), custom_call_target="tpu_custom_call" | custom-call | flops 2013265920 | bytes 3932160 | tf_op jit(solution)/shard_map/local_step/pallas_call | solution.py:117
  27.6 3.6 %collective-permute-start.3 = (bf16[3,256,256]{2,1,0:T(8,128)(2,1)S(1)}, bf16[3,256,256]{2,1,0:T(8,128)(2,1)S(1)}, u32[]{:S(2)}, u32[]{:S(2)}) collective-permute-start(bf16[3,256,256]{2,1,0:T(8,128)(2,1)S(1)} %get-tuple-element.39.down_ref.before_ref), channel_id=1, source_target_pairs={{1,0},{2,1},{3,2},{4,3},{5,4},{6,5},{7,6},{8,7},{9,8},{10,9},{11,1... | collective-permute-start | bytes 1179656 | tf_op jit(solution)/shard_map/ppermute | solution.py:27
  31.3 3.9 %local_step.5 = (f32[5,3,256,256]{3,2,1,0:T(8,128)S(1)}, bf16[5,3,256,256]{3,2,1,0:T(8,128)(2,1)S(1)}) custom-call(s32[1]{0:T(128)} %get-tuple-element.93.choice_ref, f32[5,3,256,256]{3,2,1,0:T(8,128)S(1)} %get-tuple-element.36.x_ref, f32[6,256,256]{2,1,0:T(8,128)S(1)} %get-tuple-element.37.edge_ref, ...), custom_call_target="tpu_custom_call" | custom-call | flops 2013265920 | bytes 3932160 | tf_op jit(solution)/shard_map/local_step/pallas_call | solution.py:117
  38.4 3.8 %collective-permute-start.4 = (bf16[3,256,256]{2,1,0:T(8,128)(2,1)S(1)}, bf16[3,256,256]{2,1,0:T(8,128)(2,1)S(1)}, u32[]{:S(2)}, u32[]{:S(2)}) collective-permute-start(bf16[3,256,256]{2,1,0:T(8,128)(2,1)S(1)} %get-tuple-element.45.up_ref), channel_id=1, source_target_pairs={{0,1},{1,2},{2,3},{3,4},{4,5},{5,6},{6,7},{7,8},{8,9},{9,10},{10,1... | collective-permute-start | bytes 1179656 | tf_op jit(solution)/shard_map/ppermute | solution.py:27
  42.2 4.1 %pick_step.1 = (bf16[768,1280]{1,0:T(8,128)(2,1)}, bf16[768,1280]{1,0:T(8,128)(2,1)}) custom-call(s32[16]{0:T(128)S(1)} %get-tuple-element.53.table_ref, bf16[3,768,1280]{2,1,0:T(8,128)(2,1)} %refs_3_.1), custom_call_target="tpu_custom_call" | custom-call | tf_op jit(solution)/shard_map/pick_step/pallas_call | solution.py:307
  46.3 5.1 %collective-permute-start.8 = (bf16[768,1280]{1,0:T(8,128)(2,1)}, bf16[768,1280]{1,0:T(8,128)(2,1)}, u32[]{:S(2)}, u32[]{:S(2)}) collective-permute-start(bf16[768,1280]{1,0:T(8,128)(2,1)} %get-tuple-element.57), channel_id=1, source_target_pairs={{0,8},{8,16},{16,24},{24,32},{32,40},{40,48},{48,56},{56,64},{64,7... | collective-permute-start | bytes 5898248 | tf_op jit(solution)/shard_map/ppermute | solution.py:27
  59.3 5.3 %local_step.6 = (f32[5,3,256,256]{3,2,1,0:T(8,128)S(1)}, bf16[5,3,256,256]{3,2,1,0:T(8,128)(2,1)S(1)}) custom-call(s32[1]{0:T(128)} %get-tuple-element.91.choice_ref, f32[5,3,256,256]{3,2,1,0:T(8,128)S(1)} %copy-done.2, f32[6,256,256]{2,1,0:T(8,128)S(1)} %get-tuple-element.42.edge_ref, bf16[5,3,256,256]{3,2,1,0:T(8,128)(2,1)S(1)} %get-tuple-element.43.narrow_ref, ...), custom_call_target="tpu_custom_call" | custom-call | flops 2013265920 | bytes 3932160 | tf_op jit(solution)/shard_map/local_step/pallas_call | solution.py:117
  66.9 5.4 %collective-permute-start.6 = (bf16[3,256,256]{2,1,0:T(8,128)(2,1)S(1)}, bf16[3,256,256]{2,1,0:T(8,128)(2,1)S(1)}, u32[]{:S(2)}, u32[]{:S(2)}) collective-permute-start(bf16[3,256,256]{2,1,0:T(8,128)(2,1)S(1)} %get-tuple-element.50.up_ref), channel_id=1, source_target_pairs={{0,1},{1,2},{2,3},{3,4},{4,5},{5,6},{6,7},{7,8},{8,9},{9,10},{10,1... | collective-permute-start | bytes 1179656 | tf_op jit(solution)/shard_map/ppermute | solution.py:27
  81.8 5.1 %collective-permute-start.17 = (bf16[512,1280]{1,0:T(8,128)(2,1)S(1)}, bf16[512,1280]{1,0:T(8,128)(2,1)S(1)}, u32[]{:S(2)}, u32[]{:S(2)}) collective-permute-start(bf16[512,1280]{1,0:T(8,128)(2,1)S(1)} %slice.121), channel_id=1, source_target_pairs={{8,0},{16,8},{24,16},{32,24},{40,32},{48,40},{56,48},{64,56},{72,6... | collective-permute-start | bytes 3932168 | tf_op jit(solution)/shard_map/ppermute | solution.py:27
  87.0 3.9 %local_step.7 = (f32[5,3,256,256]{3,2,1,0:T(8,128)S(1)}, bf16[5,3,256,256]{3,2,1,0:T(8,128)(2,1)S(1)}) custom-call(s32[1]{0:T(128)} %get-tuple-element.92.choice_ref, f32[5,3,256,256]{3,2,1,0:T(8,128)S(1)} %get-tuple-element.46.x_ref, f32[6,256,256]{2,1,0:T(8,128)S(1)} %get-tuple-element.47.edge_ref, ...), custom_call_target="tpu_custom_call" | custom-call | flops 2013265920 | bytes 3932160 | tf_op jit(solution)/shard_map/local_step/pallas_call | solution.py:117
  94.0 21.3 %collective-permute-done.8.refs_4_ = bf16[768,1280]{1,0:T(8,128)(2,1)} collective-permute-done((bf16[768,1280]{1,0:T(8,128)(2,1)}, bf16[768,1280]{1,0:T(8,128)(2,1)}, u32[]{:S(2)}, u32[]{:S(2)}) %collective-permute-start.8) | collective-permute-done | bytes 1966112 | tf_op jit(solution)/shard_map/ppermute | solution.py:27
  115.3 2.3 %collective-permute-start.11 = (bf16[256,1280]{1,0:T(8,128)(2,1)S(1)}, bf16[256,1280]{1,0:T(8,128)(2,1)S(1)}, u32[]{:S(2)}, u32[]{:S(2)}) collective-permute-start(bf16[256,1280]{1,0:T(8,128)(2,1)S(1)} %get-tuple-element.73), channel_id=1, source_target_pairs={{2,10},{3,11},{4,12},{5,13},{6,14},{7,15},{10,18},{11,19},{12,20},... | collective-permute-start | bytes 1966088 | tf_op jit(solution)/shard_map/ppermute | solution.py:597
  117.7 5.6 %collective-permute-start.13 = (bf16[256,1280]{1,0:T(8,128)(2,1)S(1)}, bf16[256,1280]{1,0:T(8,128)(2,1)S(1)}, u32[]{:S(2)}, u32[]{:S(2)}) collective-permute-start(bf16[256,1280]{1,0:T(8,128)(2,1)S(1)} %get-tuple-element.74), channel_id=1, source_target_pairs={{8,0},{9,1},{10,2},{11,3},{12,4},{13,5},{16,8},{17,9},{18,10},{19,... | collective-permute-start | bytes 1966088 | tf_op jit(solution)/shard_map/ppermute | solution.py:597
  124.9 14.7 %domain_step.2 = (f32[5,3,256,256]{3,2,1,0:T(8,128)S(1)}, f32[3,1,768]{2,1,0:T(1,128)S(1)}, bf16[5,768,256]{2,1,0:T(8,128)(2,1)S(1)}) custom-call(s32[16]{0:T(128)S(1)} %get-tuple-element.53.table_ref, bf16[5,3,256,256]{3,2,1,0:T(8,128)(2,1)S(1)} %get-tuple-element.54.refs_0_, bf16[3,256,256]{2,1,0:T(8,128)(2,1)S(1)} %get-tuple-element.55.refs_1_, ...), custom_call_target="tpu_custom_call" | custom-call | flops 7247757312 | bytes 11796480 | tf_op jit(solution)/shard_map/domain_step/pallas_call | solution.py:433
  139.6 16.3 %collective-permute-done.11.refs_0_ = bf16[256,1280]{1,0:T(8,128)(2,1)S(1)} collective-permute-done((bf16[256,1280]{1,0:T(8,128)(2,1)S(1)}, bf16[256,1280]{1,0:T(8,128)(2,1)S(1)}, u32[]{:S(2)}, u32[]{:S(2)}) %collective-permute-start.11) | collective-permute-done | bytes 655392 | tf_op jit(solution)/shard_map/ppermute | solution.py:597
  155.9 5.7 %collective-permute-start.21 = (f32[768]{0:T(1024)S(1)}, f32[768]{0:T(1024)S(1)}, u32[]{:S(2)}, u32[]{:S(2)}) collective-permute-start(f32[768]{0:T(1024)S(1)} %get-tuple-element.71), channel_id=1, source_target_pairs={{8,0},{16,8},{24,16},{32,24},{40,32},{48,40},{56,48},{64,56},{72,6... | collective-permute-start | bytes 9224 | tf_op jit(solution)/shard_map/ppermute | solution.py:27
  166.0 6.3 %domain_step.3 = (f32[5,3,256,256]{3,2,1,0:T(8,128)S(1)}, f32[2,1,512]{2,1,0:T(1,128)S(1)}) custom-call(s32[16]{0:T(128)S(1)} %get-tuple-element.53.table_ref, f32[5,3,256,256]{3,2,1,0:T(8,128)S(1)} %get-tuple-element.64.refs_0_, bf16[5,768,256]{2,1,0:T(8,128)(2,1)S(1)} %get-tuple-element.59.stack.refs_1_, ...), custom_call_target="tpu_custom_call" | custom-call | flops 3221225472 | bytes 8519680 | tf_op jit(solution)/shard_map/domain_step/pallas_call | solution.py:433
  172.3 4.9 %collective-permute-start.19 = (f32[768]{0:T(1024)S(1)}, f32[768]{0:T(1024)S(1)}, u32[]{:S(2)}, u32[]{:S(2)}) collective-permute-start(f32[768]{0:T(1024)S(1)} %pad_maximum_fusion.3), channel_id=1, source_target_pairs={{16,0},{24,8},{32,16},{40,24},{48,32},{56,40},{64,48},{72,56},{80,... | collective-permute-start | bytes 9224 | tf_op jit(solution)/shard_map/ppermute | solution.py:27
  177.2 2.5 %collective-permute-start.18 = (f32[768]{0:T(1024)S(1)}, f32[768]{0:T(1024)S(1)}, u32[]{:S(2)}, u32[]{:S(2)}) collective-permute-start(f32[768]{0:T(1024)S(1)} %pad_maximum_fusion.2), channel_id=1, source_target_pairs={{0,16},{8,24},{16,32},{24,40},{32,48},{40,56},{48,64},{56,72},{64,... | collective-permute-start | bytes 9224 | tf_op jit(solution)/shard_map/ppermute | solution.py:27
  179.6 2.9 %block_step.1 = f32[5,3,256,256]{3,2,1,0:T(8,128)} custom-call(s32[16]{0:T(128)S(1)} %get-tuple-element.53.table_ref, bf16[2,256,1536]{2,1,0:T(8,128)(2,1)S(1)} %get-tuple-element.62.psi_ref, bf16[2,256,1792]{2,1,0:T(8,128)(2,1)S(1)} %get-tuple-element.63.phi_ref, f32[5,3,256,256]{3,2,1,0:T(8,128)S(1)} %get-tuple-element.65.base_ref), custom_call_target="tpu_custom_call" | custom-call | flops 805306368 | bytes 11010048 | tf_op jit(solution)/shard_map/block_step/pallas_call | solution.py:546
  182.6 2.4 %collective-permute-done.18 = f32[768]{0:T(1024)S(1)} collective-permute-done((f32[768]{0:T(1024)S(1)}, f32[768]{0:T(1024)S(1)}, u32[]{:S(2)}, u32[]{:S(2)}) %collective-permute-start.18) | collective-permute-done | bytes 3104 | tf_op jit(solution)/shard_map/ppermute | solution.py:27
  (72 shorter events, 42.9 us)
Async XLA Ops:
  3.1 21.5 %collective-permute-start = (bf16[3,256,256]{2,1,0:T(8,128)(2,1)S(1)}, bf16[3,256,256]{2,1,0:T(8,128)(2,1)S(1)}, u32[]{:S(2)}, u32[]{:S(2)}) collective-permute-start(bf16[3,256,256]{2,1,0:T(8,128)(2,1)S(1)} %pad_maximum_fusion.1.up_ref), channel_id=1, source_target_pairs={{0,1},{1,2},{2,3},{3,4},{4,5},{5,6},{6,7},{7,8},{8,9},{9,10},{10,1... | collective-permute-start | bytes 1179656 | tf_op jit(solution)/shard_map/ppermute | solution.py:27
  5.1 19.5 %collective-permute-start.1 = (bf16[3,256,256]{2,1,0:T(8,128)(2,1)S(1)}, bf16[3,256,256]{2,1,0:T(8,128)(2,1)S(1)}, u32[]{:S(2)}, u32[]{:S(2)}) collective-permute-start(bf16[3,256,256]{2,1,0:T(8,128)(2,1)S(1)} %pad_maximum_fusion.down_ref.before_ref), channel_id=1, source_target_pairs={{1,0},{2,1},{3,2},{4,3},{5,4},{6,5},{7,6},{8,7},{9,8},{10,9},{11,1... | collective-permute-start | bytes 1179656 | tf_op jit(solution)/shard_map/ppermute | solution.py:27
  8.7 11.2 %copy-start = (f32[5,3,256,256]{3,2,1,0:T(8,128)S(1)}, f32[5,3,256,256]{3,2,1,0:T(8,128)}, u32[]{:S(2)}) copy-start(f32[5,3,256,256]{3,2,1,0:T(8,128)} %x_ref.1) | copy-start | bytes 11796484
  14.0 58.2 %collective-permute-start.12 = (bf16[768,1280]{1,0:T(8,128)(2,1)}, bf16[768,1280]{1,0:T(8,128)(2,1)}, u32[]{:S(2)}, u32[]{:S(2)}) collective-permute-start(bf16[768,1280]{1,0:T(8,128)(2,1)} %get-tuple-element.61), channel_id=1, source_target_pairs={{8,0},{16,8},{24,16},{32,24},{40,32},{48,40},{56,48},{64,56},{72,6... | collective-permute-start | bytes 5898248 | tf_op jit(solution)/shard_map/ppermute | solution.py:27
  16.0 58.2 %collective-permute-start.10 = (bf16[768,1280]{1,0:T(8,128)(2,1)}, bf16[768,1280]{1,0:T(8,128)(2,1)}, u32[]{:S(2)}, u32[]{:S(2)}) collective-permute-start(bf16[768,1280]{1,0:T(8,128)(2,1)} %get-tuple-element.60), channel_id=1, source_target_pairs={{0,8},{8,16},{16,24},{24,32},{32,40},{40,48},{48,56},{56,64},{64,7... | collective-permute-start | bytes 5898248 | tf_op jit(solution)/shard_map/ppermute | solution.py:27
  25.7 9.5 %collective-permute-start.2 = (bf16[3,256,256]{2,1,0:T(8,128)(2,1)S(1)}, bf16[3,256,256]{2,1,0:T(8,128)(2,1)S(1)}, u32[]{:S(2)}, u32[]{:S(2)}) collective-permute-start(bf16[3,256,256]{2,1,0:T(8,128)(2,1)S(1)} %get-tuple-element.40.up_ref), channel_id=1, source_target_pairs={{0,1},{1,2},{2,3},{3,4},{4,5},{5,6},{6,7},{7,8},{8,9},{9,10},{10,1... | collective-permute-start | bytes 1179656 | tf_op jit(solution)/shard_map/ppermute | solution.py:27
  27.6 8.9 %collective-permute-start.3 = (bf16[3,256,256]{2,1,0:T(8,128)(2,1)S(1)}, bf16[3,256,256]{2,1,0:T(8,128)(2,1)S(1)}, u32[]{:S(2)}, u32[]{:S(2)}) collective-permute-start(bf16[3,256,256]{2,1,0:T(8,128)(2,1)S(1)} %get-tuple-element.39.down_ref.before_ref), channel_id=1, source_target_pairs={{1,0},{2,1},{3,2},{4,3},{5,4},{6,5},{7,6},{8,7},{9,8},{10,9},{11,1... | collective-permute-start | bytes 1179656 | tf_op jit(solution)/shard_map/ppermute | solution.py:27
  38.4 7.9 %copy-start.3 = (bf16[3,256,256]{2,1,0:T(8,128)(2,1)}, bf16[3,256,256]{2,1,0:T(8,128)(2,1)S(1)}, u32[]{:S(2)}) copy-start(bf16[3,256,256]{2,1,0:T(8,128)(2,1)S(1)} %get-tuple-element.45.up_ref) | copy-start | bytes 1179652
  38.4 14.9 %collective-permute-start.4 = (bf16[3,256,256]{2,1,0:T(8,128)(2,1)S(1)}, bf16[3,256,256]{2,1,0:T(8,128)(2,1)S(1)}, u32[]{:S(2)}, u32[]{:S(2)}) collective-permute-start(bf16[3,256,256]{2,1,0:T(8,128)(2,1)S(1)} %get-tuple-element.45.up_ref), channel_id=1, source_target_pairs={{0,1},{1,2},{2,3},{3,4},{4,5},{5,6},{6,7},{7,8},{8,9},{9,10},{10,1... | collective-permute-start | bytes 1179656 | tf_op jit(solution)/shard_map/ppermute | solution.py:27
  46.3 69.0 %collective-permute-start.8 = (bf16[768,1280]{1,0:T(8,128)(2,1)}, bf16[768,1280]{1,0:T(8,128)(2,1)}, u32[]{:S(2)}, u32[]{:S(2)}) collective-permute-start(bf16[768,1280]{1,0:T(8,128)(2,1)} %get-tuple-element.57), channel_id=1, source_target_pairs={{0,8},{8,16},{16,24},{24,32},{32,40},{40,48},{48,56},{56,64},{64,7... | collective-permute-start | bytes 5898248 | tf_op jit(solution)/shard_map/ppermute | solution.py:27
  51.4 66.3 %collective-permute-start.9 = (bf16[768,1280]{1,0:T(8,128)(2,1)}, bf16[768,1280]{1,0:T(8,128)(2,1)}, u32[]{:S(2)}, u32[]{:S(2)}) collective-permute-start(bf16[768,1280]{1,0:T(8,128)(2,1)} %get-tuple-element.58), channel_id=1, source_target_pairs={{8,0},{16,8},{24,16},{32,24},{40,32},{48,40},{56,48},{64,56},{72,6... | collective-permute-start | bytes 5898248 | tf_op jit(solution)/shard_map/ppermute | solution.py:27
  54.1 10.5 %collective-permute-start.5 = (bf16[3,256,256]{2,1,0:T(8,128)(2,1)}, bf16[3,256,256]{2,1,0:T(8,128)(2,1)}, u32[]{:S(2)}, u32[]{:S(2)}) collective-permute-start(bf16[3,256,256]{2,1,0:T(8,128)(2,1)} %get-tuple-element.44.down_ref.before_ref), channel_id=1, source_target_pairs={{1,0},{2,1},{3,2},{4,3},{5,4},{6,5},{7,6},{8,7},{9,8},{10,9},{11,1... | collective-permute-start | bytes 1179656 | tf_op jit(solution)/shard_map/ppermute | solution.py:27
  66.9 12.9 %collective-permute-start.6 = (bf16[3,256,256]{2,1,0:T(8,128)(2,1)S(1)}, bf16[3,256,256]{2,1,0:T(8,128)(2,1)S(1)}, u32[]{:S(2)}, u32[]{:S(2)}) collective-permute-start(bf16[3,256,256]{2,1,0:T(8,128)(2,1)S(1)} %get-tuple-element.50.up_ref), channel_id=1, source_target_pairs={{0,1},{1,2},{2,3},{3,4},{4,5},{5,6},{6,7},{7,8},{8,9},{9,10},{10,1... | collective-permute-start | bytes 1179656 | tf_op jit(solution)/shard_map/ppermute | solution.py:27
  72.3 9.5 %collective-permute-start.7 = (bf16[3,256,256]{2,1,0:T(8,128)(2,1)S(1)}, bf16[3,256,256]{2,1,0:T(8,128)(2,1)S(1)}, u32[]{:S(2)}, u32[]{:S(2)}) collective-permute-start(bf16[3,256,256]{2,1,0:T(8,128)(2,1)S(1)} %get-tuple-element.49.down_ref.before_ref), channel_id=1, source_target_pairs={{1,0},{2,1},{3,2},{4,3},{5,4},{6,5},{7,6},{8,7},{9,8},{10,9},{11,1... | collective-permute-start | bytes 1179656 | tf_op jit(solution)/shard_map/ppermute | solution.py:27
  75.6 47.6 %collective-permute-start.14 = (bf16[256,1280]{1,0:T(8,128)(2,1)S(1)}, bf16[256,1280]{1,0:T(8,128)(2,1)S(1)}, u32[]{:S(2)}, u32[]{:S(2)}) collective-permute-start(bf16[256,1280]{1,0:T(8,128)(2,1)S(1)} %get-tuple-element.72), channel_id=1, source_target_pairs={{0,10},{1,12},{8,18},{15,5},{9,20},{14,3},{16,26},{23,13},{17,28},... | collective-permute-start | bytes 1966088 | tf_op jit(solution)/shard_map/ppermute | solution.py:587
  79.7 86.2 %collective-permute-start.16 = (bf16[512,1280]{1,0:T(8,128)(2,1)S(1)}, bf16[512,1280]{1,0:T(8,128)(2,1)S(1)}, u32[]{:S(2)}, u32[]{:S(2)}) collective-permute-start(bf16[512,1280]{1,0:T(8,128)(2,1)S(1)} %slice.120), channel_id=1, source_target_pairs={{0,8},{8,16},{16,24},{24,32},{32,40},{40,48},{48,56},{56,64},{64,7... | collective-permute-start | bytes 3932168 | tf_op jit(solution)/shard_map/ppermute | solution.py:27
  81.8 84.2 %collective-permute-start.17 = (bf16[512,1280]{1,0:T(8,128)(2,1)S(1)}, bf16[512,1280]{1,0:T(8,128)(2,1)S(1)}, u32[]{:S(2)}, u32[]{:S(2)}) collective-permute-start(bf16[512,1280]{1,0:T(8,128)(2,1)S(1)} %slice.121), channel_id=1, source_target_pairs={{8,0},{16,8},{24,16},{32,24},{40,32},{48,40},{56,48},{64,56},{72,6... | collective-permute-start | bytes 3932168 | tf_op jit(solution)/shard_map/ppermute | solution.py:27
  115.3 40.6 %collective-permute-start.11 = (bf16[256,1280]{1,0:T(8,128)(2,1)S(1)}, bf16[256,1280]{1,0:T(8,128)(2,1)S(1)}, u32[]{:S(2)}, u32[]{:S(2)}) collective-permute-start(bf16[256,1280]{1,0:T(8,128)(2,1)S(1)} %get-tuple-element.73), channel_id=1, source_target_pairs={{2,10},{3,11},{4,12},{5,13},{6,14},{7,15},{10,18},{11,19},{12,20},... | collective-permute-start | bytes 1966088 | tf_op jit(solution)/shard_map/ppermute | solution.py:597
  117.7 44.0 %collective-permute-start.13 = (bf16[256,1280]{1,0:T(8,128)(2,1)S(1)}, bf16[256,1280]{1,0:T(8,128)(2,1)S(1)}, u32[]{:S(2)}, u32[]{:S(2)}) collective-permute-start(bf16[256,1280]{1,0:T(8,128)(2,1)S(1)} %get-tuple-element.74), channel_id=1, source_target_pairs={{8,0},{9,1},{10,2},{11,3},{12,4},{13,5},{16,8},{17,9},{18,10},{19,... | collective-permute-start | bytes 1966088 | tf_op jit(solution)/shard_map/ppermute | solution.py:597
  123.3 40.4 %collective-permute-start.15 = (bf16[256,1280]{1,0:T(8,128)(2,1)S(1)}, bf16[256,1280]{1,0:T(8,128)(2,1)S(1)}, u32[]{:S(2)}, u32[]{:S(2)}) collective-permute-start(bf16[256,1280]{1,0:T(8,128)(2,1)S(1)} %collective-permute-done.14), channel_id=1, source_target_pairs={{2,0},{5,7},{4,1},{3,6},{10,8},{13,15},{12,9},{11,14},{18,16},{21,... | collective-permute-start | bytes 1966088 | tf_op jit(solution)/shard_map/ppermute | solution.py:598
  155.9 26.7 %collective-permute-start.21 = (f32[768]{0:T(1024)S(1)}, f32[768]{0:T(1024)S(1)}, u32[]{:S(2)}, u32[]{:S(2)}) collective-permute-start(f32[768]{0:T(1024)S(1)} %get-tuple-element.71), channel_id=1, source_target_pairs={{8,0},{16,8},{24,16},{32,24},{40,32},{48,40},{56,48},{64,56},{72,6... | collective-permute-start | bytes 9224 | tf_op jit(solution)/shard_map/ppermute | solution.py:27
  161.7 20.9 %collective-permute-start.20 = (f32[768]{0:T(1024)S(1)}, f32[768]{0:T(1024)S(1)}, u32[]{:S(2)}, u32[]{:S(2)}) collective-permute-start(f32[768]{0:T(1024)S(1)} %get-tuple-element.69), channel_id=1, source_target_pairs={{0,8},{8,16},{16,24},{24,32},{32,40},{40,48},{48,56},{56,64},{64,7... | collective-permute-start | bytes 9224 | tf_op jit(solution)/shard_map/ppermute | solution.py:27
  172.3 10.3 %collective-permute-start.19 = (f32[768]{0:T(1024)S(1)}, f32[768]{0:T(1024)S(1)}, u32[]{:S(2)}, u32[]{:S(2)}) collective-permute-start(f32[768]{0:T(1024)S(1)} %pad_maximum_fusion.3), channel_id=1, source_target_pairs={{16,0},{24,8},{32,16},{40,24},{48,32},{56,40},{64,48},{72,56},{80,... | collective-permute-start | bytes 9224 | tf_op jit(solution)/shard_map/ppermute | solution.py:27
  177.2 7.9 %collective-permute-start.18 = (f32[768]{0:T(1024)S(1)}, f32[768]{0:T(1024)S(1)}, u32[]{:S(2)}, u32[]{:S(2)}) collective-permute-start(f32[768]{0:T(1024)S(1)} %pad_maximum_fusion.2), channel_id=1, source_target_pairs={{0,16},{8,24},{16,32},{24,40},{32,48},{40,56},{48,64},{56,72},{64,... | collective-permute-start | bytes 9224 | tf_op jit(solution)/shard_map/ppermute | solution.py:27
  (6 other events, 18.4 us)

commit v4 on v3

--- a/solution.py
+++ b/solution.py
@@ -377,15 +377,11 @@
             ham[row, 2 - (k - j)] += piece[:, (j - low) * BS : (j - low + 1) * BS]
 
 
-def domain_kernel(slots, has_base, factor, table_ref, *refs):
+def domain_kernel(slots, factor, table_ref, *refs):
     refs = list(refs)
-    if has_base:
-        base_ref, stack = refs.pop(0), refs.pop(0)
-    else:
-        tile_refs = [refs.pop(0) for _ in range(3)]
-        stack = refs.pop(len(slots) + 2)
+    tile_refs = [refs.pop(0) for _ in range(3)]
     basis_refs = [refs.pop(0) for _ in slots]
-    ham, pot_out, phi, psi, sems = refs
+    ham, pot_out, stack, phi, psi, sems = refs
 
     def fetch(n):
         source = basis_refs[n]
@@ -396,9 +392,8 @@
     for n in range(len(slots)):
         fetch(n).start()
     for r in range(ham.shape[0]):
-        ham[r] = base_ref[r] if has_base else jnp.zeros_like(ham[r])
-    if not has_base:
-        fill_stack(tile_refs, stack)
+        ham[r] = jnp.zeros_like(ham[r])
+    fill_stack(tile_refs, stack)
     pot_out[...] = jnp.zeros_like(pot_out)
     for n in range(len(slots)):
         fetch(n).wait()
@@ -415,24 +410,21 @@
             add_blocks(ham, psi, phi, n, first)
 
 
-def domain_step(slots, table, tiles, base, arrays, factor):
+def domain_step(slots, table, tiles, arrays, factor):
     rows = RB
     points, width = arrays[-1].shape[-2:]
     number = len(arrays)
-    has_base = base is not None
     smem = pl.BlockSpec(memory_space=pltpu.SMEM)
     vmem = pl.BlockSpec(memory_space=pltpu.VMEM)
     hbm = pl.BlockSpec(memory_space=pl.ANY)
-    fixed = base if has_base else tiles
     outs = [
         jax.ShapeDtypeStruct((rows, 3, BS, BS), jnp.float32),
         jax.ShapeDtypeStruct((number, 1, points), jnp.float32),
+        jax.ShapeDtypeStruct((rows, 3 * BS, BS), jnp.bfloat16),
     ]
-    if not has_base:
-        outs.append(jax.ShapeDtypeStruct((rows, 3 * BS, BS), jnp.bfloat16))
-    return pl.pallas_call(
-        functools.partial(domain_kernel, slots, has_base, factor),
-        in_specs=[smem] + [vmem] * len(fixed) + [hbm] * number,
+    return pl.pallas_call(
+        functools.partial(domain_kernel, slots, factor),
+        in_specs=[smem] + [vmem] * len(tiles) + [hbm] * number,
         out_specs=[vmem] * len(outs),
         out_shape=outs,
         scratch_shapes=[
@@ -449,12 +441,12 @@
             transcendentals=number * points,
         ),
         name="domain_step",
-    )(table, *fixed, *arrays)
+    )(table, *tiles, *arrays)
 
 
 def potential_kernel(slots, factor, table_ref, stack, *refs):
-    *basis_refs, detour_ref = refs[: len(slots) + 1]
-    psi_out, phi_out, pot_out, phi = refs[len(slots) + 1 :]
+    *given, psi_out, phi_out, pot_out, phi = refs
+    basis_refs, detour_refs = given[: len(slots)], given[len(slots) :]
     points, width = phi.shape[1:]
     pad = phi_out.shape[2] - width
     grid = lax.axis_index("grid")
@@ -462,14 +454,12 @@
     detoured = (grid <= 1, grid >= last - 1)
     pot_out[...] = jnp.zeros_like(pot_out)
     for n in range(len(slots)):
-
-        @pl.when(detoured[n])
-        def _():
-            phi[n] = detour_ref[...]
-
-        @pl.when(jnp.logical_not(detoured[n]))
-        def _():
-            phi[n] = basis_refs[n][...]
+        phi[n] = basis_refs[n][...]
+        for detour_ref in detour_refs:
+
+            @pl.when(detoured[n])
+            def _():
+                phi[n] = detour_ref[...]
 
         phi_out[n, :, 0:pad] = jnp.zeros((points, pad), jnp.bfloat16)
         phi_out[n, :, pad:] = phi[n]
@@ -490,14 +480,14 @@
             potential_of_slot(phi, n, first, stack, pot_out, psi_at, factor)
 
 
-def potential_step(slots, table, stack, arrays, detour, factor):
+def potential_step(slots, table, stack, arrays, detours, factor):
     points, width = arrays[-1].shape
     number = len(arrays)
     smem = pl.BlockSpec(memory_space=pltpu.SMEM)
     vmem = pl.BlockSpec(memory_space=pltpu.VMEM)
     return pl.pallas_call(
         functools.partial(potential_kernel, slots, factor),
-        in_specs=[smem] + [vmem] * (2 + number),
+        in_specs=[smem] + [vmem] * (1 + number + len(detours)),
         out_specs=[vmem] * 3,
         out_shape=[
             jax.ShapeDtypeStruct((number, points, width + BS), jnp.bfloat16),
@@ -505,17 +495,18 @@
             jax.ShapeDtypeStruct((number, 1, points), jnp.float32),
         ],
         scratch_shapes=[pltpu.VMEM((number, points, width), jnp.bfloat16)],
-        compiler_params=pltpu.CompilerParams(vmem_limit_bytes=10 << 20),
+        compiler_params=pltpu.CompilerParams(vmem_limit_bytes=12 << 20),
         cost_estimate=pl.CostEstimate(
             flops=number * 12 * 2 * points * BS * BS,
             bytes_accessed=number * points * width * 4,
             transcendentals=number * points,
         ),
         name="potential_step",
-    )(table, stack, *arrays, detour)
-
-
-def block_kernel(slots, table_ref, psi_ref, phi_ref, base_ref, ham_out, ham, sems):
+    )(table, stack, *arrays, *detours)
+
+
+def block_kernel(slots, table_ref, base_ref, *refs):
+    *parts, ham_out, ham, sems = refs
     rows = ham.shape[0]
 
     def send(r):
@@ -527,10 +518,11 @@
             k = r - table_ref[STARTS + slot]
             held = (k >= 0) & (k < table_ref[COUNTS + slot])
             near = jnp.clip(k, 0, DBLK - 1)
-            left = psi_ref[n, :, pl.ds(pl.multiple_of(jnp.where(held, near, DBLK) * BS, BS), BS)]
-            right = phi_ref[n, :, pl.ds(pl.multiple_of(near * BS, BS), 3 * BS)]
-            piece = dot32(left, right, TN)
-            total = piece if total is None else total + piece
+            left = pl.ds(pl.multiple_of(jnp.where(held, near, DBLK) * BS, BS), BS)
+            right = pl.ds(pl.multiple_of(near * BS, BS), 3 * BS)
+            for psi_ref, phi_ref in zip(parts[::2], parts[1::2]):
+                piece = dot32(psi_ref[n, :, left], phi_ref[n, :, right], TN)
+                total = piece if total is None else total + piece
         for q in range(3):
             ham[r, q] = base_ref[r, q] + total[:, q * BS : (q + 1) * BS]
         send(r).start()
@@ -538,14 +530,14 @@
         send(r).wait()
 
 
-def block_step(slots, table, psi, phi, base):
-    number, points, width = psi.shape
+def block_step(slots, table, base, parts):
     rows = base.shape[0]
+    size = sum(part.size for part in parts)
     smem = pl.BlockSpec(memory_space=pltpu.SMEM)
     vmem = pl.BlockSpec(memory_space=pltpu.VMEM)
     return pl.pallas_call(
         functools.partial(block_kernel, slots),
-        in_specs=[smem, vmem, vmem, vmem],
+        in_specs=[smem, vmem] + [vmem] * len(parts),
         out_specs=pl.BlockSpec(memory_space=pltpu.HBM),
         out_shape=pltpu.HBM(base.shape, jnp.float32),
         scratch_shapes=[
@@ -554,12 +546,12 @@
         ],
         compiler_params=pltpu.CompilerParams(vmem_limit_bytes=10 << 20),
         cost_estimate=pl.CostEstimate(
-            flops=number * 12 * 2 * points * BS * BS,
-            bytes_accessed=number * points * width * 4 + base.size * 8,
+            flops=size * 3 * BS,
+            bytes_accessed=size * 2 + base.size * 8,
             transcendentals=0,
         ),
         name="block_step",
-    )(table, psi, phi, base)
+    )(table, base, *parts)
 
 
 def whole_step(x_initial, sp2_choices, domain_blocks, basis_values):
@@ -612,11 +604,13 @@
     tiles = (narrow, downward, upward)
     density = density_step(x, edge)
 
-    ham, near_pot, stack = domain_step((0, 1, 2), table, tiles, None, [basis_values] + near, factor)
-    ham, pot_a = domain_step((3, 4), table, None, (ham, stack), far_a, factor)
-    psi_b, phi_b, pot_b = potential_step((3, 4), table, stack, far_b, detour, factor)
+    ham, near_pot, stack = domain_step(
+        (0, 1, 2), table, tiles, [basis_values] + near, factor
+    )
+    psi_a, phi_a, pot_a = potential_step((3, 4), table, stack, far_a, [], factor)
+    psi_b, phi_b, pot_b = potential_step((3, 4), table, stack, far_b, [detour], factor)
     far_pot = [jnp.concatenate([pot_a[n, 0], pot_b[n, 0]]) for n in (0, 1)]
-    ham = block_step((3, 4), table, psi_b, phi_b, ham)
+    ham = block_step((3, 4), table, ham, [psi_a, phi_a, psi_b, phi_b])
     sent_back = [near_pot[0, 0]]
     for move, values in ((1, near_pot[1, 0]), (-1, near_pot[2, 0]), (2, far_pot[0]), (-2, far_pot[1])):
         sent_back.append(passed_along(values, "band", -move))

time: 187 us -> 184 us (0.984)
  the two profiles are of different devices: /device:TPU:60 before, /device:TPU:26 now
where the time goes in v4:
time: 184 us; the launch traced here: 183 us
  starting transfers between devices  85.8 us (47%)
  Pallas kernels  56.9 us (31%)
  waiting for transfers between devices  26.5 us (14%)
  local copies, waits for them, and re-layouts  7.58 us (4%)
  other arithmetic  4.62 us (3%)
    ppermute x18, starting transfers between devices, passed_along(): return lax.ppermute(x, axis, pairs)  68 us
    pallas_call x4, Pallas kernels, local_step(): pl.pallas_call(local_kernel, in_specs=[pl.BlockSpec(memory_space=pltpu.SM...  16.9 us
    ppermute x2, waiting for transfers between devices, whole_step(): far_b.append(lax.ppermute(rest[n], ('band', 'grid'), pairs))  14.7 us
    ppermute x18, waiting for transfers between devices, passed_along(): return lax.ppermute(x, axis, pairs)  11.7 us
    pallas_call x1, Pallas kernels, domain_step(): pl.pallas_call(functools.partial(domain_kernel, slots, factor), in_specs=...  10.7 us
    ppermute x1, starting transfers between devices, whole_step(): lax.ppermute(detour, ('band', 'grid'), detour_back(band_count, grid_count))  8.36 us
    ppermute x2, starting transfers between devices, whole_step(): far_b.append(lax.ppermute(rest[n], ('band', 'grid'), pairs))  8.13 us
    pallas_call x2, Pallas kernels, potential_step(): pl.pallas_call(functools.partial(potential_kernel, slots, factor), in_spe...  6.38 us
  transfers between devices with their start and end apart: 22, of which 5 were waited for; matrix products, arithmetic and copies ran while one was open for 3% of the time, Pallas kernels for 31%

profile of v4, /device:TPU:26, one launch (start us, length us, event | category | flops | bytes accessed | tf_op | source)
XLA Modules:
  0.0 182.6 jit_solution(105650592110120467)
XLA Ops:
  7.5 5.3 %plan_step.1 = (bf16[768,1280]{1,0:T(8,128)(2,1)}, bf16[768,1280]{1,0:T(8,128)(2,1)}, s32[16]{0:T(128)S(1)}) custom-call(s32[5,384]{1,0:T(8,128)} %bitcast.29, bf16[3,768,1280]{2,1,0:T(8,128)(2,1)} %refs_3_.1), custom_call_target="tpu_custom_call" | custom-call | tf_op jit(solution)/shard_map/plan_step/pallas_call | solution.py:253
  12.8 3.8 %collective-permute-start.10 = (bf16[768,1280]{1,0:T(8,128)(2,1)}, bf16[768,1280]{1,0:T(8,128)(2,1)}, u32[]{:S(2)}, u32[]{:S(2)}) collective-permute-start(bf16[768,1280]{1,0:T(8,128)(2,1)} %get-tuple-element.62), channel_id=1, source_target_pairs={{0,8},{8,16},{16,24},{24,32},{32,40},{40,48},{48,56},{56,64},{64,7... | collective-permute-start | bytes 5898248 | tf_op jit(solution)/shard_map/ppermute | solution.py:27
  16.7 4.2 %collective-permute-start.12 = (bf16[768,1280]{1,0:T(8,128)(2,1)}, bf16[768,1280]{1,0:T(8,128)(2,1)}, u32[]{:S(2)}, u32[]{:S(2)}) collective-permute-start(bf16[768,1280]{1,0:T(8,128)(2,1)} %get-tuple-element.63), channel_id=1, source_target_pairs={{8,0},{16,8},{24,16},{32,24},{40,32},{48,40},{56,48},{64,56},{72,6... | collective-permute-start | bytes 5898248 | tf_op jit(solution)/shard_map/ppermute | solution.py:27
  21.7 3.8 %local_step.4 = (f32[5,3,256,256]{3,2,1,0:T(8,128)S(1)}, bf16[5,3,256,256]{3,2,1,0:T(8,128)(2,1)S(1)}) custom-call(s32[1]{0:T(128)} %get-tuple-element.92.choice_ref, f32[5,3,256,256]{3,2,1,0:T(8,128)S(1)} %copy-done, f32[6,256,256]{2,1,0:T(8,128)S(1)} %bitcast_dynamic-update-slice_fusion.edge_ref, ...), custom_call_target="tpu_custom_call" | custom-call | flops 2013265920 | bytes 3932160 | tf_op jit(solution)/shard_map/local_step/pallas_call | solution.py:117
  26.7 2.7 %collective-permute-start.2 = (bf16[3,256,256]{2,1,0:T(8,128)(2,1)S(1)}, bf16[3,256,256]{2,1,0:T(8,128)(2,1)S(1)}, u32[]{:S(2)}, u32[]{:S(2)}) collective-permute-start(bf16[3,256,256]{2,1,0:T(8,128)(2,1)S(1)} %get-tuple-element.41.up_ref), channel_id=1, source_target_pairs={{0,1},{1,2},{2,3},{3,4},{4,5},{5,6},{6,7},{7,8},{8,9},{9,10},{10,1... | collective-permute-start | bytes 1179656 | tf_op jit(solution)/shard_map/ppermute | solution.py:27
  29.5 2.8 %collective-permute-start.3 = (bf16[3,256,256]{2,1,0:T(8,128)(2,1)S(1)}, bf16[3,256,256]{2,1,0:T(8,128)(2,1)S(1)}, u32[]{:S(2)}, u32[]{:S(2)}) collective-permute-start(bf16[3,256,256]{2,1,0:T(8,128)(2,1)S(1)} %get-tuple-element.40.down_ref.before_ref), channel_id=1, source_target_pairs={{1,0},{2,1},{3,2},{4,3},{5,4},{6,5},{7,6},{8,7},{9,8},{10,9},{11,1... | collective-permute-start | bytes 1179656 | tf_op jit(solution)/shard_map/ppermute | solution.py:27
  32.3 3.9 %local_step.5 = (f32[5,3,256,256]{3,2,1,0:T(8,128)S(1)}, bf16[5,3,256,256]{3,2,1,0:T(8,128)(2,1)S(1)}) custom-call(s32[1]{0:T(128)} %get-tuple-element.95.choice_ref, f32[5,3,256,256]{3,2,1,0:T(8,128)S(1)} %get-tuple-element.37.x_ref, f32[6,256,256]{2,1,0:T(8,128)S(1)} %get-tuple-element.38.edge_ref, ...), custom_call_target="tpu_custom_call" | custom-call | flops 2013265920 | bytes 3932160 | tf_op jit(solution)/shard_map/local_step/pallas_call | solution.py:117
  39.4 4.1 %collective-permute-start.4 = (bf16[3,256,256]{2,1,0:T(8,128)(2,1)S(1)}, bf16[3,256,256]{2,1,0:T(8,128)(2,1)S(1)}, u32[]{:S(2)}, u32[]{:S(2)}) collective-permute-start(bf16[3,256,256]{2,1,0:T(8,128)(2,1)S(1)} %get-tuple-element.46.up_ref), channel_id=1, source_target_pairs={{0,1},{1,2},{2,3},{3,4},{4,5},{5,6},{6,7},{7,8},{8,9},{9,10},{10,1... | collective-permute-start | bytes 1179656 | tf_op jit(solution)/shard_map/ppermute | solution.py:27
  43.5 4.1 %pick_step.1 = (bf16[768,1280]{1,0:T(8,128)(2,1)}, bf16[768,1280]{1,0:T(8,128)(2,1)}) custom-call(s32[16]{0:T(128)S(1)} %get-tuple-element.54.table_ref, bf16[3,768,1280]{2,1,0:T(8,128)(2,1)} %refs_3_.1), custom_call_target="tpu_custom_call" | custom-call | tf_op jit(solution)/shard_map/pick_step/pallas_call | solution.py:307
  49.5 6.0 %collective-permute-start.9 = (bf16[768,1280]{1,0:T(8,128)(2,1)}, bf16[768,1280]{1,0:T(8,128)(2,1)}, u32[]{:S(2)}, u32[]{:S(2)}) collective-permute-start(bf16[768,1280]{1,0:T(8,128)(2,1)} %get-tuple-element.59), channel_id=1, source_target_pairs={{8,0},{16,8},{24,16},{32,24},{40,32},{48,40},{56,48},{64,56},{72,6... | collective-permute-start | bytes 5898248 | tf_op jit(solution)/shard_map/ppermute | solution.py:27
  61.6 5.3 %local_step.6 = (f32[5,3,256,256]{3,2,1,0:T(8,128)S(1)}, bf16[5,3,256,256]{3,2,1,0:T(8,128)(2,1)S(1)}) custom-call(s32[1]{0:T(128)} %get-tuple-element.93.choice_ref, f32[5,3,256,256]{3,2,1,0:T(8,128)S(1)} %copy-done.2, f32[6,256,256]{2,1,0:T(8,128)S(1)} %get-tuple-element.43.edge_ref, bf16[5,3,256,256]{3,2,1,0:T(8,128)(2,1)S(1)} %get-tuple-element.44.narrow_ref, ...), custom_call_target="tpu_custom_call" | custom-call | flops 2013265920 | bytes 3932160 | tf_op jit(solution)/shard_map/local_step/pallas_call | solution.py:117
  69.2 3.9 %collective-permute-start.6 = (bf16[3,256,256]{2,1,0:T(8,128)(2,1)S(1)}, bf16[3,256,256]{2,1,0:T(8,128)(2,1)S(1)}, u32[]{:S(2)}, u32[]{:S(2)}) collective-permute-start(bf16[3,256,256]{2,1,0:T(8,128)(2,1)S(1)} %get-tuple-element.51.up_ref), channel_id=1, source_target_pairs={{0,1},{1,2},{2,3},{3,4},{4,5},{5,6},{6,7},{7,8},{8,9},{9,10},{10,1... | collective-permute-start | bytes 1179656 | tf_op jit(solution)/shard_map/ppermute | solution.py:27
  73.1 7.7 %collective-permute-start.7 = (bf16[3,256,256]{2,1,0:T(8,128)(2,1)S(1)}, bf16[3,256,256]{2,1,0:T(8,128)(2,1)S(1)}, u32[]{:S(2)}, u32[]{:S(2)}) collective-permute-start(bf16[3,256,256]{2,1,0:T(8,128)(2,1)S(1)} %get-tuple-element.50.down_ref.before_ref), channel_id=1, source_target_pairs={{1,0},{2,1},{3,2},{4,3},{5,4},{6,5},{7,6},{8,7},{9,8},{10,9},{11,1... | collective-permute-start | bytes 1179656 | tf_op jit(solution)/shard_map/ppermute | solution.py:27
  88.3 6.0 %collective-permute-start.13 = (bf16[512,1280]{1,0:T(8,128)(2,1)S(1)}, bf16[512,1280]{1,0:T(8,128)(2,1)S(1)}, u32[]{:S(2)}, u32[]{:S(2)}) collective-permute-start(bf16[512,1280]{1,0:T(8,128)(2,1)S(1)} %slice.119), channel_id=1, source_target_pairs={{8,0},{16,8},{24,16},{32,24},{40,32},{48,40},{56,48},{64,56},{72,6... | collective-permute-start | bytes 3932168 | tf_op jit(solution)/shard_map/ppermute | solution.py:27
  94.4 3.9 %local_step.7 = (f32[5,3,256,256]{3,2,1,0:T(8,128)S(1)}, bf16[5,3,256,256]{3,2,1,0:T(8,128)(2,1)S(1)}) custom-call(s32[1]{0:T(128)} %get-tuple-element.94.choice_ref, f32[5,3,256,256]{3,2,1,0:T(8,128)S(1)} %get-tuple-element.47.x_ref, f32[6,256,256]{2,1,0:T(8,128)S(1)} %get-tuple-element.48.edge_ref, ...), custom_call_target="tpu_custom_call" | custom-call | flops 2013265920 | bytes 3932160 | tf_op jit(solution)/shard_map/local_step/pallas_call | solution.py:117
  101.4 10.2 %collective-permute-done.8.refs_4_ = bf16[768,1280]{1,0:T(8,128)(2,1)} collective-permute-done((bf16[768,1280]{1,0:T(8,128)(2,1)}, bf16[768,1280]{1,0:T(8,128)(2,1)}, u32[]{:S(2)}, u32[]{:S(2)}) %collective-permute-start.8) | collective-permute-done | bytes 1966112 | tf_op jit(solution)/shard_map/ppermute | solution.py:27
  113.7 6.2 %collective-permute-start.15 = (bf16[256,1280]{1,0:T(8,128)(2,1)S(1)}, bf16[256,1280]{1,0:T(8,128)(2,1)S(1)}, u32[]{:S(2)}, u32[]{:S(2)}) collective-permute-start(bf16[256,1280]{1,0:T(8,128)(2,1)S(1)} %get-tuple-element.76), channel_id=1, source_target_pairs={{8,0},{9,1},{10,2},{11,3},{12,4},{13,5},{16,8},{17,9},{18,10},{19,... | collective-permute-start | bytes 1966088 | tf_op jit(solution)/shard_map/ppermute | solution.py:589
  119.9 8.4 %collective-permute-start.17 = (bf16[256,1280]{1,0:T(8,128)(2,1)S(1)}, bf16[256,1280]{1,0:T(8,128)(2,1)S(1)}, u32[]{:S(2)}, u32[]{:S(2)}) collective-permute-start(bf16[256,1280]{1,0:T(8,128)(2,1)S(1)} %collective-permute-done.16), channel_id=1, source_target_pairs={{2,0},{5,7},{4,1},{3,6},{10,8},{13,15},{12,9},{11,14},{18,16},{21,... | collective-permute-start | bytes 1966088 | tf_op jit(solution)/shard_map/ppermute | solution.py:590
  128.3 10.7 %domain_step.1 = (f32[5,3,256,256]{3,2,1,0:T(8,128)S(1)}, f32[3,1,768]{2,1,0:T(1,128)S(1)}, bf16[5,768,256]{2,1,0:T(8,128)(2,1)S(1)}) custom-call(s32[16]{0:T(128)S(1)} %get-tuple-element.54.table_ref, bf16[5,3,256,256]{3,2,1,0:T(8,128)(2,1)S(1)} %get-tuple-element.55.refs_0_, bf16[3,256,256]{2,1,0:T(8,128)(2,1)S(1)} %get-tuple-element.56.refs_1_, ...), custom_call_target="tpu_custom_call" | custom-call | flops 7247757312 | bytes 11796480 | tf_op jit(solution)/shard_map/domain_step/pallas_call | solution.py:425
  139.1 14.6 %collective-permute-done.14.refs_0_ = bf16[256,1280]{1,0:T(8,128)(2,1)S(1)} collective-permute-done((bf16[256,1280]{1,0:T(8,128)(2,1)S(1)}, bf16[256,1280]{1,0:T(8,128)(2,1)S(1)}, u32[]{:S(2)}, u32[]{:S(2)}) %collective-permute-start.14) | collective-permute-done | bytes 655392 | tf_op jit(solution)/shard_map/ppermute | solution.py:589
  155.7 6.2 %collective-permute-start.21 = (f32[768]{0:T(1024)S(1)}, f32[768]{0:T(1024)S(1)}, u32[]{:S(2)}, u32[]{:S(2)}) collective-permute-start(f32[768]{0:T(1024)S(1)} %get-tuple-element.73), channel_id=1, source_target_pairs={{8,0},{16,8},{24,16},{32,24},{40,32},{48,40},{56,48},{64,56},{72,6... | collective-permute-start | bytes 9224 | tf_op jit(solution)/shard_map/ppermute | solution.py:27
  164.3 4.1 %potential_step.2 = (bf16[2,512,1536]{2,1,0:T(8,128)(2,1)S(1)}, bf16[2,512,1792]{2,1,0:T(8,128)(2,1)S(1)}, f32[2,1,512]{2,1,0:T(1,128)S(1)}) custom-call(s32[16]{0:T(128)S(1)} %get-tuple-element.54.table_ref, bf16[5,768,256]{2,1,0:T(8,128)(2,1)S(1)} %get-tuple-element.61.stack, bf16[512,1280]{1,0:T(8,128)(2,1)S(1)} %collective-permute-done.11.refs_0_, ...), custom_call_target="tpu_custom_call" | custom-call | flops 1610612736 | bytes 5242880 | tf_op jit(solution)/shard_map/potential_step/pallas_call | solution.py:488
  170.3 6.3 %collective-permute-start.19 = (f32[768]{0:T(1024)S(1)}, f32[768]{0:T(1024)S(1)}, u32[]{:S(2)}, u32[]{:S(2)}) collective-permute-start(f32[768]{0:T(1024)S(1)} %pad_maximum_fusion.3), channel_id=1, source_target_pairs={{16,0},{24,8},{32,16},{40,24},{48,32},{56,40},{64,48},{72,56},{80,... | collective-permute-start | bytes 9224 | tf_op jit(solution)/shard_map/ppermute | solution.py:27
  176.6 5.2 %block_step.1 = f32[5,3,256,256]{3,2,1,0:T(8,128)} custom-call(s32[16]{0:T(128)S(1)} %get-tuple-element.54.table_ref, f32[5,3,256,256]{3,2,1,0:T(8,128)S(1)} %get-tuple-element.60.base_ref, bf16[2,512,1536]{2,1,0:T(8,128)(2,1)S(1)} %get-tuple-element.64.refs_0_, bf16[2,512,1792]{2,1,0:T(8,128)(2,1)S(1)} %get-tuple-element.65.refs_1_, ...), custom_call_target="tpu_custom_call" | custom-call | flops 3925868544 | bytes 18087936 | tf_op jit(solution)/shard_map/block_step/pallas_call | solution.py:538
  (72 shorter events, 41.8 us)
Async XLA Ops:
  3.1 22.5 %collective-permute-start.1 = (bf16[3,256,256]{2,1,0:T(8,128)(2,1)S(1)}, bf16[3,256,256]{2,1,0:T(8,128)(2,1)S(1)}, u32[]{:S(2)}, u32[]{:S(2)}) collective-permute-start(bf16[3,256,256]{2,1,0:T(8,128)(2,1)S(1)} %pad_maximum_fusion.down_ref.before_ref), channel_id=1, source_target_pairs={{1,0},{2,1},{3,2},{4,3},{5,4},{6,5},{7,6},{8,7},{9,8},{10,9},{11,1... | collective-permute-start | bytes 1179656 | tf_op jit(solution)/shard_map/ppermute | solution.py:27
  5.1 20.5 %collective-permute-start = (bf16[3,256,256]{2,1,0:T(8,128)(2,1)S(1)}, bf16[3,256,256]{2,1,0:T(8,128)(2,1)S(1)}, u32[]{:S(2)}, u32[]{:S(2)}) collective-permute-start(bf16[3,256,256]{2,1,0:T(8,128)(2,1)S(1)} %pad_maximum_fusion.1.up_ref), channel_id=1, source_target_pairs={{0,1},{1,2},{2,3},{3,4},{4,5},{5,6},{6,7},{7,8},{8,9},{9,10},{10,1... | collective-permute-start | bytes 1179656 | tf_op jit(solution)/shard_map/ppermute | solution.py:27
  7.5 13.4 %copy-start = (f32[5,3,256,256]{3,2,1,0:T(8,128)S(1)}, f32[5,3,256,256]{3,2,1,0:T(8,128)}, u32[]{:S(2)}) copy-start(f32[5,3,256,256]{3,2,1,0:T(8,128)} %x_ref.1) | copy-start | bytes 11796484
  12.8 8.2 %copy-start.7 = (s32[4]{0:T(128)S(1)}, s32[4]{0:T(128)}, u32[]{:S(2)}) copy-start(s32[4]{0:T(128)} %param.5) | copy-start | bytes 52
  12.8 60.3 %collective-permute-start.10 = (bf16[768,1280]{1,0:T(8,128)(2,1)}, bf16[768,1280]{1,0:T(8,128)(2,1)}, u32[]{:S(2)}, u32[]{:S(2)}) collective-permute-start(bf16[768,1280]{1,0:T(8,128)(2,1)} %get-tuple-element.62), channel_id=1, source_target_pairs={{0,8},{8,16},{16,24},{24,32},{32,40},{40,48},{48,56},{56,64},{64,7... | collective-permute-start | bytes 5898248 | tf_op jit(solution)/shard_map/ppermute | solution.py:27
  16.7 64.1 %collective-permute-start.12 = (bf16[768,1280]{1,0:T(8,128)(2,1)}, bf16[768,1280]{1,0:T(8,128)(2,1)}, u32[]{:S(2)}, u32[]{:S(2)}) collective-permute-start(bf16[768,1280]{1,0:T(8,128)(2,1)} %get-tuple-element.63), channel_id=1, source_target_pairs={{8,0},{16,8},{24,16},{32,24},{40,32},{48,40},{56,48},{64,56},{72,6... | collective-permute-start | bytes 5898248 | tf_op jit(solution)/shard_map/ppermute | solution.py:27
  26.7 9.5 %collective-permute-start.2 = (bf16[3,256,256]{2,1,0:T(8,128)(2,1)S(1)}, bf16[3,256,256]{2,1,0:T(8,128)(2,1)S(1)}, u32[]{:S(2)}, u32[]{:S(2)}) collective-permute-start(bf16[3,256,256]{2,1,0:T(8,128)(2,1)S(1)} %get-tuple-element.41.up_ref), channel_id=1, source_target_pairs={{0,1},{1,2},{2,3},{3,4},{4,5},{5,6},{6,7},{7,8},{8,9},{9,10},{10,1... | collective-permute-start | bytes 1179656 | tf_op jit(solution)/shard_map/ppermute | solution.py:27
  29.5 8.1 %collective-permute-start.3 = (bf16[3,256,256]{2,1,0:T(8,128)(2,1)S(1)}, bf16[3,256,256]{2,1,0:T(8,128)(2,1)S(1)}, u32[]{:S(2)}, u32[]{:S(2)}) collective-permute-start(bf16[3,256,256]{2,1,0:T(8,128)(2,1)S(1)} %get-tuple-element.40.down_ref.before_ref), channel_id=1, source_target_pairs={{1,0},{2,1},{3,2},{4,3},{5,4},{6,5},{7,6},{8,7},{9,8},{10,9},{11,1... | collective-permute-start | bytes 1179656 | tf_op jit(solution)/shard_map/ppermute | solution.py:27
  39.4 16.1 %collective-permute-start.4 = (bf16[3,256,256]{2,1,0:T(8,128)(2,1)S(1)}, bf16[3,256,256]{2,1,0:T(8,128)(2,1)S(1)}, u32[]{:S(2)}, u32[]{:S(2)}) collective-permute-start(bf16[3,256,256]{2,1,0:T(8,128)(2,1)S(1)} %get-tuple-element.46.up_ref), channel_id=1, source_target_pairs={{0,1},{1,2},{2,3},{3,4},{4,5},{5,6},{6,7},{7,8},{8,9},{9,10},{10,1... | collective-permute-start | bytes 1179656 | tf_op jit(solution)/shard_map/ppermute | solution.py:27
  47.6 64.1 %collective-permute-start.8 = (bf16[768,1280]{1,0:T(8,128)(2,1)}, bf16[768,1280]{1,0:T(8,128)(2,1)}, u32[]{:S(2)}, u32[]{:S(2)}) collective-permute-start(bf16[768,1280]{1,0:T(8,128)(2,1)} %get-tuple-element.58), channel_id=1, source_target_pairs={{0,8},{8,16},{16,24},{24,32},{32,40},{40,48},{48,56},{56,64},{64,7... | collective-permute-start | bytes 5898248 | tf_op jit(solution)/shard_map/ppermute | solution.py:27
  49.5 64.2 %collective-permute-start.9 = (bf16[768,1280]{1,0:T(8,128)(2,1)}, bf16[768,1280]{1,0:T(8,128)(2,1)}, u32[]{:S(2)}, u32[]{:S(2)}) collective-permute-start(bf16[768,1280]{1,0:T(8,128)(2,1)} %get-tuple-element.59), channel_id=1, source_target_pairs={{8,0},{16,8},{24,16},{32,24},{40,32},{48,40},{56,48},{64,56},{72,6... | collective-permute-start | bytes 5898248 | tf_op jit(solution)/shard_map/ppermute | solution.py:27
  56.3 10.5 %collective-permute-start.5 = (bf16[3,256,256]{2,1,0:T(8,128)(2,1)}, bf16[3,256,256]{2,1,0:T(8,128)(2,1)}, u32[]{:S(2)}, u32[]{:S(2)}) collective-permute-start(bf16[3,256,256]{2,1,0:T(8,128)(2,1)} %get-tuple-element.45.down_ref.before_ref), channel_id=1, source_target_pairs={{1,0},{2,1},{3,2},{4,3},{5,4},{6,5},{7,6},{8,7},{9,8},{10,9},{11,1... | collective-permute-start | bytes 1179656 | tf_op jit(solution)/shard_map/ppermute | solution.py:27
  69.2 17.2 %collective-permute-start.6 = (bf16[3,256,256]{2,1,0:T(8,128)(2,1)S(1)}, bf16[3,256,256]{2,1,0:T(8,128)(2,1)S(1)}, u32[]{:S(2)}, u32[]{:S(2)}) collective-permute-start(bf16[3,256,256]{2,1,0:T(8,128)(2,1)S(1)} %get-tuple-element.51.up_ref), channel_id=1, source_target_pairs={{0,1},{1,2},{2,3},{3,4},{4,5},{5,6},{6,7},{7,8},{8,9},{9,10},{10,1... | collective-permute-start | bytes 1179656 | tf_op jit(solution)/shard_map/ppermute | solution.py:27
  73.1 15.2 %collective-permute-start.7 = (bf16[3,256,256]{2,1,0:T(8,128)(2,1)S(1)}, bf16[3,256,256]{2,1,0:T(8,128)(2,1)S(1)}, u32[]{:S(2)}, u32[]{:S(2)}) collective-permute-start(bf16[3,256,256]{2,1,0:T(8,128)(2,1)S(1)} %get-tuple-element.50.down_ref.before_ref), channel_id=1, source_target_pairs={{1,0},{2,1},{3,2},{4,3},{5,4},{6,5},{7,6},{8,7},{9,8},{10,9},{11,1... | collective-permute-start | bytes 1179656 | tf_op jit(solution)/shard_map/ppermute | solution.py:27
  82.2 37.7 %collective-permute-start.16 = (bf16[256,1280]{1,0:T(8,128)(2,1)S(1)}, bf16[256,1280]{1,0:T(8,128)(2,1)S(1)}, u32[]{:S(2)}, u32[]{:S(2)}) collective-permute-start(bf16[256,1280]{1,0:T(8,128)(2,1)S(1)} %get-tuple-element.74), channel_id=1, source_target_pairs={{0,10},{1,12},{8,18},{15,5},{9,20},{14,3},{16,26},{23,13},{17,28},... | collective-permute-start | bytes 1966088 | tf_op jit(solution)/shard_map/ppermute | solution.py:579
  86.3 77.9 %collective-permute-start.11 = (bf16[512,1280]{1,0:T(8,128)(2,1)S(1)}, bf16[512,1280]{1,0:T(8,128)(2,1)S(1)}, u32[]{:S(2)}, u32[]{:S(2)}) collective-permute-start(bf16[512,1280]{1,0:T(8,128)(2,1)S(1)} %slice.118), channel_id=1, source_target_pairs={{0,8},{8,16},{16,24},{24,32},{32,40},{40,48},{48,56},{56,64},{64,7... | collective-permute-start | bytes 3932168 | tf_op jit(solution)/shard_map/ppermute | solution.py:27
  88.3 76.0 %collective-permute-start.13 = (bf16[512,1280]{1,0:T(8,128)(2,1)S(1)}, bf16[512,1280]{1,0:T(8,128)(2,1)S(1)}, u32[]{:S(2)}, u32[]{:S(2)}) collective-permute-start(bf16[512,1280]{1,0:T(8,128)(2,1)S(1)} %slice.119), channel_id=1, source_target_pairs={{8,0},{16,8},{24,16},{32,24},{40,32},{48,40},{56,48},{64,56},{72,6... | collective-permute-start | bytes 3932168 | tf_op jit(solution)/shard_map/ppermute | solution.py:27
  111.7 42.0 %collective-permute-start.14 = (bf16[256,1280]{1,0:T(8,128)(2,1)S(1)}, bf16[256,1280]{1,0:T(8,128)(2,1)S(1)}, u32[]{:S(2)}, u32[]{:S(2)}) collective-permute-start(bf16[256,1280]{1,0:T(8,128)(2,1)S(1)} %get-tuple-element.75), channel_id=1, source_target_pairs={{2,10},{3,11},{4,12},{5,13},{6,14},{7,15},{10,18},{11,19},{12,20},... | collective-permute-start | bytes 1966088 | tf_op jit(solution)/shard_map/ppermute | solution.py:589
  113.7 42.0 %collective-permute-start.15 = (bf16[256,1280]{1,0:T(8,128)(2,1)S(1)}, bf16[256,1280]{1,0:T(8,128)(2,1)S(1)}, u32[]{:S(2)}, u32[]{:S(2)}) collective-permute-start(bf16[256,1280]{1,0:T(8,128)(2,1)S(1)} %get-tuple-element.76), channel_id=1, source_target_pairs={{8,0},{9,1},{10,2},{11,3},{12,4},{13,5},{16,8},{17,9},{18,10},{19,... | collective-permute-start | bytes 1966088 | tf_op jit(solution)/shard_map/ppermute | solution.py:589
  119.9 42.0 %collective-permute-start.17 = (bf16[256,1280]{1,0:T(8,128)(2,1)S(1)}, bf16[256,1280]{1,0:T(8,128)(2,1)S(1)}, u32[]{:S(2)}, u32[]{:S(2)}) collective-permute-start(bf16[256,1280]{1,0:T(8,128)(2,1)S(1)} %collective-permute-done.16), channel_id=1, source_target_pairs={{2,0},{5,7},{4,1},{3,6},{10,8},{13,15},{12,9},{11,14},{18,16},{21,... | collective-permute-start | bytes 1966088 | tf_op jit(solution)/shard_map/ppermute | solution.py:590
  153.7 28.2 %collective-permute-start.20 = (f32[768]{0:T(1024)S(1)}, f32[768]{0:T(1024)S(1)}, u32[]{:S(2)}, u32[]{:S(2)}) collective-permute-start(f32[768]{0:T(1024)S(1)} %get-tuple-element.71), channel_id=1, source_target_pairs={{0,8},{8,16},{16,24},{24,32},{32,40},{40,48},{48,56},{56,64},{64,7... | collective-permute-start | bytes 9224 | tf_op jit(solution)/shard_map/ppermute | solution.py:27
  155.7 26.2 %collective-permute-start.21 = (f32[768]{0:T(1024)S(1)}, f32[768]{0:T(1024)S(1)}, u32[]{:S(2)}, u32[]{:S(2)}) collective-permute-start(f32[768]{0:T(1024)S(1)} %get-tuple-element.73), channel_id=1, source_target_pairs={{8,0},{16,8},{24,16},{32,24},{40,32},{48,40},{56,48},{64,56},{72,6... | collective-permute-start | bytes 9224 | tf_op jit(solution)/shard_map/ppermute | solution.py:27
  168.4 13.6 %collective-permute-start.18 = (f32[768]{0:T(1024)S(1)}, f32[768]{0:T(1024)S(1)}, u32[]{:S(2)}, u32[]{:S(2)}) collective-permute-start(f32[768]{0:T(1024)S(1)} %pad_maximum_fusion.2), channel_id=1, source_target_pairs={{0,16},{8,24},{16,32},{24,40},{32,48},{40,56},{48,64},{56,72},{64,... | collective-permute-start | bytes 9224 | tf_op jit(solution)/shard_map/ppermute | solution.py:27
  170.3 11.6 %collective-permute-start.19 = (f32[768]{0:T(1024)S(1)}, f32[768]{0:T(1024)S(1)}, u32[]{:S(2)}, u32[]{:S(2)}) collective-permute-start(f32[768]{0:T(1024)S(1)} %pad_maximum_fusion.3), channel_id=1, source_target_pairs={{16,0},{24,8},{32,16},{40,24},{48,32},{56,40},{64,48},{72,56},{80,... | collective-permute-start | bytes 9224 | tf_op jit(solution)/shard_map/ppermute | solution.py:27
  (6 other events, 20.6 us)
